TPU v7x, 128 devices: a whole 4x4x4 slice. The times are simulated.
128 devices in a mesh: outer: 8 (over z, core), inner: 16 (over y, x).
Axes of the slice: x: 4, y: 4, z: 4, core: 2. Of those that a mesh axis runs over, the one named last changes fastest.
Arguments:
- tokens_in: bfloat16 [16384, 2048], P(('outer', 'inner')), may hold values from -6 to 6
- expert_ids: int32 [16384, 10], P(('outer', 'inner')), may hold values from 0 to 255, all different within a row; in each aligned block of 128 rows (0 to 127, 128 to 255, ...) at most 6 rows name the same one
- route_weight: float32 [16384, 10], P(('outer', 'inner')), may hold values from 0.05 to 1
- first_gain: float32 [2048], replicated, may hold values from 0.5 to 1.5
- gate_weight: bfloat16 [256, 2048, 512], P(('outer', 'inner')), may hold values from -0.125 to 0.125
- up_weight: bfloat16 [256, 2048, 512], P(('outer', 'inner')), may hold values from -0.125 to 0.125
- down_weight: bfloat16 [256, 512, 2048], P(('outer', 'inner')), may hold values from -0.25 to 0.25
- second_gain: float32 [2048], replicated, may hold values from 0.5 to 1.5
- mixer_weight: bfloat16 [2048, 4096], P(None, 'inner'), may hold values from -0.125 to 0.125
- gating_weight: bfloat16 [2048, 32], replicated, may hold values from -0.125 to 0.125
- filter_taps: bfloat16 [4, 4096], replicated, may hold values from -3 to 3
- decay_log: float32 [16], replicated, may hold values from -9 to -3
- decay_bias: float32 [16], replicated, may hold values from -1 to 1
- output_gain: float32 [128], replicated, may hold values from 0.5 to 1.5
Outputs:
- hidden_out: bfloat16 [16384, 2048], P(('outer', 'inner'))
- core_out: bfloat16 [16384, 2048], P(('outer', 'inner'))
Inputs may be any that keep to these rules, and one draw needn't show every extreme that they name: `expert_ids`: each token names 10 different experts; the 128 rows of one device name any one expert at most 6 times, a bound that some block reaches.
All inputs are finite; a program needn't handle non-finite values.
Results may differ from a plain program's by a relative error of at most 0.015.
Values may be sent and summed in bfloat16 or wider, within the bound.
A program may use at most 576 MiB of HBM per device.

v0:
```python
import jax
import jax.numpy as jnp
from jax import lax
from jax.sharding import PartitionSpec as P


def shifted(value, axis, steps):
    count = lax.axis_size(axis)
    leading, last = (max(0, -steps), min(count, count - steps))
    return lax.ppermute(value, axis, [(source, source + steps) for source in range(leading, last)])


def prefix_2(x, axis, join, neutral):
    place = lax.axis_index(axis)
    gathered = jax.tree.map(
        lambda a, kind: lax.all_gather(a.astype(kind), axis), x, (jnp.bfloat16, jnp.bfloat16)
    )
    state = jax.tree.map(lambda a, e: jnp.zeros_like(a) + jnp.asarray(e, a.dtype), x, neutral)

    def one(lap, state):
        return join(
            state,
            jax.tree.map(
                lambda a, own: lax.dynamic_index_in_dim(a, lap, 0, False).astype(own.dtype),
                gathered,
                x,
            ),
        )

    return lax.fori_loop(0, place, one, state)


def shortened(x):

    def short(part):
        return part.astype(jnp.bfloat16) if part.dtype == jnp.float32 else part

    return jax.tree.map(short, x)


def spread_2(value, axis, source):
    kept = jnp.where(lax.axis_index(axis) == source, value, 0).astype(value.dtype)
    return lax.psum(kept, axis)


def entering(x, axis, combine, identity):
    length, place = (lax.axis_size(axis), lax.axis_index(axis))
    everything = jax.tree.map(
        lambda part, kind: lax.all_gather(part.astype(kind), axis),
        x,
        jax.tree.map(lambda a: jnp.bfloat16 if a.dtype == jnp.float32 else a.dtype, x),
    )
    start = jax.tree.map(
        lambda part, zero: jnp.broadcast_to(jnp.asarray(zero, part.dtype), part.shape), x, identity
    )

    def lap(k, before):
        reached = k < place
        new = combine(
            before, jax.tree.map(lambda part, own: part[k].astype(own.dtype), everything, x)
        )
        return jax.tree.map(lambda a, b: jnp.where(reached, a, b), new, before)

    return lax.fori_loop(0, length, lap, start)


def rms_scale(values, gain):
    wide = values.astype(jnp.float32)
    return wide * lax.rsqrt(jnp.mean(wide * wide, axis=-1, keepdims=True) + 1e-06) * gain


def unit_heads(values):
    return values * lax.rsqrt(jnp.sum(values * values, axis=-1, keepdims=True) + 1e-06)


def run_experts(piece, gate_weight, up_weight, down_weight):
    gate = jnp.einsum("secd,edf->secf", piece, gate_weight, preferred_element_type=jnp.float32)
    upper = jnp.einsum("secd,edf->secf", piece, up_weight, preferred_element_type=jnp.float32)
    hidden = (jax.nn.silu(gate) * upper).astype(jnp.bfloat16)
    return jnp.einsum(
        "secf,efd->secd", hidden, down_weight, preferred_element_type=jnp.float32
    ).astype(jnp.bfloat16)


def join_maps(earlier, later):
    first_map, first_state = earlier
    next_map, next_state = later
    joined_map = jnp.einsum("hij,hjk->hik", next_map, first_map, precision=lax.Precision.HIGHEST)
    joined_state = (
        jnp.einsum("hij,hjv->hiv", next_map, first_state, precision=lax.Precision.HIGHEST)
        + next_state
    )
    return (joined_map, joined_state)


def per_device(
    tokens_in,
    expert_ids,
    route_weight,
    first_gain,
    gate_weight,
    up_weight,
    down_weight,
    second_gain,
    mixer_weight,
    gating_weight,
    filter_taps,
    decay_log,
    decay_bias,
    output_gain,
):
    n_outer = lax.axis_size("outer")
    n_inner = lax.axis_size("inner")
    n_dev = n_outer * n_inner
    tok_count, width = tokens_in.shape
    top_count = expert_ids.shape[1]
    local_experts = gate_weight.shape[0]
    experts_all = local_experts * n_dev
    capacity = max(2, 6 * tok_count * top_count // (5 * experts_all))
    normed_first = rms_scale(tokens_in, first_gain).astype(jnp.bfloat16)
    mix_weight = route_weight / jnp.sum(route_weight, axis=1, keepdims=True)
    pairs = tok_count * top_count
    flat = expert_ids.reshape(-1)
    onehot = (flat[:, None] == jnp.arange(experts_all, dtype=jnp.int32)[None, :]).astype(jnp.int32)
    before = jnp.cumsum(onehot, axis=0) - onehot
    slot_index = jnp.sum(before * onehot, axis=1)
    target = (
        flat // local_experts * (local_experts * capacity)
        + flat % local_experts * capacity
        + slot_index
    )
    owner = jnp.arange(pairs, dtype=jnp.int32) // top_count
    outgoing = (
        jnp.zeros((n_dev * local_experts * capacity, width), jnp.bfloat16)
        .at[target]
        .set(normed_first[owner])
    )
    outgoing = outgoing.reshape(n_dev, local_experts, capacity, width)
    served = run_experts(
        lax.all_to_all(outgoing, ("outer", "inner"), split_axis=0, concat_axis=0, tiled=True),
        gate_weight,
        up_weight,
        down_weight,
    )
    returned = lax.all_to_all(served, ("outer", "inner"), split_axis=0, concat_axis=0, tiled=True)
    rows_back = (
        returned.reshape(-1, width)[target].astype(jnp.float32) * mix_weight.reshape(-1)[:, None]
    )
    mixture = jnp.sum(rows_back.reshape(tok_count, top_count, width), axis=1)
    hidden_out = (tokens_in.astype(jnp.float32) + mixture).astype(jnp.bfloat16)
    normed_second = rms_scale(hidden_out, second_gain).astype(jnp.bfloat16)
    mixed = jnp.dot(
        normed_second,
        lax.all_gather(mixer_weight, "inner", axis=1, tiled=True),
        preferred_element_type=jnp.float32,
    )
    projected = mixed.astype(jnp.bfloat16)
    gating = jnp.dot(normed_second, gating_weight, preferred_element_type=jnp.float32)
    taps = filter_taps.shape[0]
    rim = shifted(projected[tok_count - (taps - 1) :], ("outer", "inner"), 1)
    padded = jnp.concatenate([rim, projected], axis=0).astype(jnp.float32)
    filtered = jnp.zeros(projected.shape, jnp.float32)
    for tap_index in range(taps):
        filtered = (
            filtered
            + filter_taps[tap_index].astype(jnp.float32) * padded[tap_index : tap_index + tok_count]
        )
    filtered = jax.nn.silu(filtered)
    head_dim = output_gain.shape[0]
    value_heads = decay_log.shape[0]
    key_heads = (projected.shape[1] - value_heads * head_dim) // (2 * head_dim)
    ratio = value_heads // key_heads
    queries = unit_heads(
        filtered[:, : key_heads * head_dim].reshape(tok_count, key_heads, head_dim)
    ) * head_dim ** (-0.5)
    keys = unit_heads(
        filtered[:, key_heads * head_dim : 2 * key_heads * head_dim].reshape(
            tok_count, key_heads, head_dim
        )
    )
    values = filtered[:, 2 * key_heads * head_dim :].reshape(tok_count, value_heads, head_dim)
    queries = jnp.repeat(queries, ratio, axis=1)
    keys = jnp.repeat(keys, ratio, axis=1)
    strength = jax.nn.sigmoid(gating[:, :value_heads]).T
    log_decay = (-jnp.exp(decay_log) * jax.nn.softplus(gating[:, value_heads:] + decay_bias)).T
    cumulative = jnp.cumsum(log_decay, axis=1)
    positions = jnp.arange(tok_count)
    lower_incl = positions[:, None] >= positions[None, :]
    lower_strict = positions[:, None] > positions[None, :]
    spread = cumulative[:, :, None] - cumulative[:, None, :]
    decay_mat = jnp.where(lower_incl, jnp.exp(jnp.where(lower_incl, spread, 0.0)), 0.0)
    key_major = keys.transpose(1, 0, 2)
    query_leading = queries.transpose(1, 0, 2)
    value_major = values.transpose(1, 0, 2)
    key_inner = jnp.einsum("htd,hid->hti", key_major, key_major, precision=lax.Precision.HIGHEST)
    lower_part = jnp.where(lower_strict, decay_mat * key_inner, 0.0) * strength[:, :, None]
    system = lower_part + jnp.eye(tok_count, dtype=jnp.float32)
    growth = jnp.exp(cumulative)
    scaled_keys = key_major * (strength * growth)[:, :, None]
    scaled_values = value_major * strength[:, :, None]
    key_resolved = lax.linalg.triangular_solve(
        system, scaled_keys, left_side=True, lower=True, unit_diagonal=True
    )
    value_resolved = lax.linalg.triangular_solve(
        system, scaled_values, left_side=True, lower=True, unit_diagonal=True
    )
    tail = jnp.exp(cumulative[:, -1:] - cumulative)
    trailing_keys = key_major * tail[:, :, None]
    eye_heads = jnp.broadcast_to(
        jnp.eye(head_dim, dtype=jnp.float32), (value_heads, head_dim, head_dim)
    )
    state_map = growth[:, -1][:, None, None] * eye_heads - jnp.einsum(
        "htk,htj->hkj", trailing_keys, key_resolved, precision=lax.Precision.HIGHEST
    )
    state_increment = jnp.einsum(
        "xbe,xbz->xez", trailing_keys, value_resolved, precision=lax.Precision.HIGHEST
    )
    identity = (eye_heads, jnp.zeros_like(state_increment))
    inner_pre = prefix_2((state_map, state_increment), "inner", join_maps, identity)
    inclusive = join_maps(inner_pre, (state_map, state_increment))
    group = spread_2(shortened(jnp.stack(inclusive)), "inner", n_inner - 1)
    outer_pre = entering((group[0], group[1]), "outer", join_maps, identity)
    prefix = join_maps(outer_pre, inner_pre)
    initial_state = prefix[1]
    updates = value_resolved - jnp.einsum(
        "mwx,mxd->mwd", key_resolved, initial_state, precision=lax.Precision.HIGHEST
    )
    query_key = (
        jnp.einsum("htd,hid->hti", query_leading, key_major, precision=lax.Precision.HIGHEST)
        * decay_mat
    )
    carried = (
        jnp.einsum("mwx,mxd->mwd", query_leading, initial_state, precision=lax.Precision.HIGHEST)
        * growth[:, :, None]
    )
    attended = carried + jnp.einsum(
        "hti,hiv->htv", query_key, updates, precision=lax.Precision.HIGHEST
    )
    attended = attended.transpose(1, 0, 2)
    core_out = (
        rms_scale(attended, output_gain)
        .astype(jnp.bfloat16)
        .reshape(tok_count, value_heads * head_dim)
    )
    return (hidden_out, core_out)


def solution(mesh):
    return jax.shard_map(
        per_device,
        mesh=mesh,
        in_specs=(
            P(("outer", "inner"), None),
            P(("outer", "inner"), None),
            P(("outer", "inner"), None),
            P(),
            P(("outer", "inner"), None, None),
            P(("outer", "inner"), None, None),
            P(("outer", "inner"), None, None),
            P(),
            P(None, "inner"),
            P(),
            P(),
            P(),
            P(),
            P(),
        ),
        out_specs=(P(("outer", "inner"), None), P(("outer", "inner"), None)),
        check_vma=False,
    )
```

profile of v0, /device:TPU:83, one launch (start us, length us, event | category | flops | bytes accessed | tf_op | source)
XLA Modules:
  0.0 932.9 jit_solution(5289336182392275664)
XLA Ops:
  11.7 34.4 %scatter_custom_fusion = bf16[1536,2048]{1,0:T(8,128)(2,1)} fusion(s32[1280]{0:T(1024)S(1)} %fusion.80, bf16[128,2048]{1,0:T(8,128)(2,1)S(1)} %fusion.61, s32[2048]{0:T(1024)S(1)} %pad_clamp_fusion.1, bf16[]{:T(256)} %constant.104.clone.1), kind=kCustom, calls=%fused_computation.26 | custom fusion | bytes 6291458 | tf_op jit(solution)/shard_map/scatter | solution.py:136
  46.1 11.0 %reshape.311 = bf16[128,2,6,2048]{3,2,1,0:T(8,128)(2,1)} reshape(bf16[1536,2048]{1,0:T(8,128)(2,1)} %scatter_custom_fusion) | data formatting | bytes 12582912 | tf_op jit(solution)/shard_map/reshape | solution.py:138
  57.1 9.7 %copy.75 = bf16[128,2,6,2048]{3,1,2,0:T(2,128)(2,1)S(1)} copy(bf16[128,2,6,2048]{3,2,1,0:T(8,128)(2,1)} %reshape.311) | data formatting | bytes 12582912 | tf_op jit(solution)/shard_map/reshape | solution.py:138
  66.8 105.8 %all_to_all.10 = bf16[128,2,6,2048]{3,1,2,0:T(2,128)(2,1)S(1)} all-to-all(bf16[128,2,6,2048]{3,1,2,0:T(2,128)(2,1)S(1)} %copy.75), channel_id=1, replica_groups=mesh['outer'=8,'inner'=16] {'outer','inner'}, dimensions={0} | all-to-all | bytes 12582912 | tf_op jit(solution)/shard_map/all_to_all | solution.py:140
  172.6 2.6 copy-done.8
  175.2 8.6 fusion.15
  183.8 19.6 %convert_bitcast_fusion = bf16[128,2,6,2048]{3,0,2,1:T(8,128)(2,1)} fusion(bf16[2,512,2048]{2,1,0:T(8,128)(2,1)} %param.26, f32[2,128,6,512]{3,1,2,0:T(8,128)} %fusion.15, bf16[2,2048,512]{2,1,0:T(8,128)(2,1)} %param.24, bf16[128,2,6,2048]{3,1,2,0:T(2,128)(2,1)} %copy-done.8), kind=kOutput, calls=%fused_computation.21 | convolution fusion | flops 6450315264 | bytes 24117248 | tf_op jit(solution)/shard_map/secf,efd->secd/dot_general | solution.py:80
  203.4 12.8 %copy.78 = bf16[128,2,6,2048]{3,1,2,0:T(2,128)(2,1)} copy(bf16[128,2,6,2048]{3,0,2,1:T(8,128)(2,1)} %convert_bitcast_fusion) | data formatting | bytes 12582912 | tf_op jit(solution)/shard_map/convert_element_type | solution.py:82
  216.2 11.6 %all-to-all-start.1 = ((bf16[128,2,6,2048]{3,1,2,0:T(2,128)(2,1)}), bf16[128,2,6,2048]{3,1,2,0:T(2,128)(2,1)}, u32[]{:S(2)}, u32[]{:S(2)}) async-start(bf16[128,2,6,2048]{3,1,2,0:T(2,128)(2,1)} %copy.78), calls=%async_computation.1 | async-start | bytes 12582912 | tf_op jit(solution)/shard_map/all_to_all | solution.py:145
  228.3 70.9 %all-to-all-done.1 = bf16[128,2,6,2048]{3,1,2,0:T(2,128)(2,1)} async-done(((bf16[128,2,6,2048]{3,1,2,0:T(2,128)(2,1)}), bf16[128,2,6,2048]{3,1,2,0:T(2,128)(2,1)}, u32[]{:S(2)}, u32[]{:S(2)}) %all-to-all-start.1) | async-done | bytes 6291488 | tf_op jit(solution)/shard_map/all_to_all | solution.py:145
  299.2 10.4 %copy.79 = bf16[128,2,6,2048]{3,2,1,0:T(8,128)(2,1)} copy(bf16[128,2,6,2048]{3,1,2,0:T(2,128)(2,1)} %all-to-all-done.1) | data formatting | bytes 12582912 | tf_op jit(solution)/shard_map/all_to_all | solution.py:145
  309.6 11.4 %reshape.312 = bf16[1536,2048]{1,0:T(8,128)(2,1)} reshape(bf16[128,2,6,2048]{3,2,1,0:T(8,128)(2,1)} %copy.79) | data formatting | bytes 12582912 | tf_op jit(solution)/shard_map/reshape | solution.py:147
  321.0 14.4 %gather_fusion = bf16[1280,2048]{1,0:T(8,128)(2,1)} fusion(bf16[1536,2048]{1,0:T(8,128)(2,1)} %reshape.312, s32[2048]{0:T(1024)S(1)} %pad_clamp_fusion), kind=kCustom, calls=%fused_computation.1 | custom fusion | bytes 10490880 | tf_op jit(solution)/shard_map/gather | solution.py:147
  335.5 10.3 %reshape.322 = f32[128,10,2048]{2,1,0:T(8,128)} reshape(bf16[1280,2048]{1,0:T(8,128)(2,1)} %gather_fusion) | data formatting | bytes 15728640 | tf_op jit(solution)/shard_map/convert_element_type | solution.py:147
  345.8 9.5 %multiply_reduce_fusion = f32[128,2048]{1,0:T(8,128)S(1)} fusion(f32[128,10,2048]{2,1,0:T(8,128)} %reshape.322, f32[128,10]{1,0:T(8,128)S(1)} %copy.80), kind=kLoop, calls=%fused_computation.20 | loop fusion | flops 4980736 | bytes 11539456 | tf_op jit(solution)/shard_map/reduce_sum | solution.py:149
  356.6 8.2 convolution_convert_fusion
  364.8 2.5 collective-permute-start
  367.4 2.7 collective-permute-done
  374.3 3.4 fusion.50
  377.8 157.9 %custom-call.5 = f32[16,1,128,128]{2,3,1,0:T(8,128)S(1)} custom-call(f32[16,1,128,128]{3,2,1,0:T(8,128)} %fusion.50), custom_call_target="InvertDiagBlocksLowerTriangular" | custom-call | tf_op jit(solution)/shard_map/triangular_solve/custom-call.1 | solution.py:201
  538.6 2.1 fusion.63
  542.4 3.0 fusion.89
  545.9 3.1 fusion.65
  549.0 2.8 fusion.88
  551.8 64.8 %all-gather.16.cloned.1.call-done = bf16[256,128,128]{2,1,0:T(8,128)(2,1)} async-done(((bf16[16,128,128]{2,1,0:T(8,128)(2,1)}), bf16[256,128,128]{2,1,0:T(8,128)(2,1)}) %all-gather.16.cloned.1.call-update) | async-done | bytes 8388624 | tf_op jit(solution)/shard_map/all_gather | solution.py:16
  616.6 72.5 %all-gather.14.cloned.1.call-done = bf16[256,128,128]{2,1,0:T(8,128)(2,1)} async-done(((bf16[16,128,128]{2,1,0:T(8,128)(2,1)}), bf16[256,128,128]{2,1,0:T(8,128)(2,1)}) %all-gather.14.cloned.1.call-update) | async-done | bytes 8388624 | tf_op jit(solution)/shard_map/all_gather | solution.py:16
  689.3 34.4 %while.26 = (s32[]{:T(128)}, f32[16,128,128]{2,1,0:T(8,128)S(1)}, f32[16,128,128]{2,1,0:T(8,128)S(1)}, s32[]{:T(128)}, bf16[16,16,128,128]{3,2,1,0:T(8,128)(2,1)...) while((s32[]{:T(128)}, f32[16,128,128]{2,1,0:T(8,128)S(1)}, ...), condition=%wide.region_12.14_spmd, body=%wide.region_11.13_spmd.sunk | while | flops 805830656 | bytes 9962627 | solution.py:30
  689.5 1.9 convolution_add_fusion.5
  691.5 1.7 fusion.127
  693.3 1.9 convolution_add_fusion.5
  695.3 1.7 fusion.127
  697.1 1.9 convolution_add_fusion.5
  700.9 1.9 convolution_add_fusion.5
  704.8 1.9 convolution_add_fusion.5
  708.6 1.9 convolution_add_fusion.5
  710.6 1.7 fusion.127
  712.4 1.9 convolution_add_fusion.5
  716.2 1.9 convolution_add_fusion.5
  720.1 1.9 convolution_add_fusion.5
  724.9 2.4 fusion.55
  728.6 106.4 %all-reduce.2.cloned.1.call-done = bf16[2,16,128,128]{3,2,1,0:T(8,128)(2,1)} async-done(((bf16[2,16,128,128]{3,2,1,0:T(8,128)(2,1)}), bf16[2,16,128,128]{3,2,1,0:T(8,128)(2,1)}) %all-reduce.2.cloned.1.call-update) | async-done | bytes 1048592 | tf_op jit(solution)/shard_map/psum | solution.py:43
  835.0 2.3 fusion.87
  839.8 3.3 convolution_multiply_fusion
  843.1 28.5 %all-gather.10.cloned.1.call-done = bf16[8,16,128,128]{3,2,1,0:T(8,128)(2,1)} async-done(((bf16[1,16,128,128]{3,2,1,0:T(8,128)(2,1)}), bf16[8,16,128,128]{3,2,1,0:T(8,128)(2,1)}) %all-gather.10.cloned.1.call-update) | async-done | bytes 4194320 | tf_op jit(solution)/shard_map/all_gather | solution.py:49
  871.6 33.7 %all-gather.12.cloned.1.call-done = bf16[8,16,128,128]{3,2,1,0:T(8,128)(2,1)} async-done(((bf16[1,16,128,128]{3,2,1,0:T(8,128)(2,1)}), bf16[8,16,128,128]{3,2,1,0:T(8,128)(2,1)}) %all-gather.12.cloned.1.call-update) | async-done | bytes 4194320 | tf_op jit(solution)/shard_map/all_gather | solution.py:49
  905.3 12.7 %while.27 = (s32[]{:T(128)}, bf16[16,128,128]{2,1,0:T(8,128)(2,1)S(1)}, s32[]{:T(128)}, bf16[8,16,128,128]{3,2,1,0:T(8,128)(2,1)}, bf16[8,16,128,128]{3,2,1,0:T(8,128)(2,1)}, /*index=5*/s32[]{:T(128)}, s32[]{:T(128)}) while((s32[]{:T(128)}, bf16[16,128,128]{2,1,0:T(8,128)(2,1)S(1)}, s32[]{:T(128)}, ...), condition=%wide.region_15.17_spmd.clone, body=%wide.region_14.16_spmd.clone.sunk | while | flops 68157440 | bytes 3672671 | solution.py:64
  920.7 1.9 fusion.44
  922.7 1.9 multiply_reduce_fusion.1
  (168 shorter events, 48.3 us)
Async XLA Ops:
  7.2 348.4 %copy-start = (bf16[2048,32]{0,1:T(8,128)(2,1)S(1)}, bf16[2048,32]{0,1:T(8,128)(2,1)}, u32[]{:S(2)}) copy-start(bf16[2048,32]{0,1:T(8,128)(2,1)} %param.29) | copy-start | bytes 393220
  7.2 349.4 %all-gather.8.cloned.1.call-start = ((), (), s32[]{:S(2)}) async-start(), calls=%async_computation.2 | async-start | bytes 17825792 | tf_op jit(solution)/shard_map/all_gather | solution.py:154
  9.6 1.6 copy-start.9
  9.6 1.8 copy-start.20
  66.8 108.5 %copy-start.23 = (bf16[2,2048,512]{2,1,0:T(8,128)(2,1)S(1)}, bf16[2,2048,512]{2,1,0:T(8,128)(2,1)}, u32[]{:S(2)}) copy-start(bf16[2,2048,512]{2,1,0:T(8,128)(2,1)} %param.25) | copy-start | bytes 12582916
  172.6 2.6 copy-start.8
  216.2 11.7 %copy-start.19 = (f32[128,10]{0,1:T(8,128)S(1)}, f32[128,10]{0,1:T(8,128)}, u32[]{:S(2)}) copy-start(f32[128,10]{0,1:T(8,128)} %param.22) | copy-start | bytes 15364
  216.2 11.9 %copy-start.24 = (f32[16]{0:T(128)S(1)}, f32[16]{0:T(128)}, u32[]{:S(2)}) copy-start(f32[16]{0:T(128)} %param.31) | copy-start | bytes 196
  216.2 12.0 %copy-start.17 = (bf16[4,4096]{1,0:T(4,128)(2,1)S(1)}, bf16[4,4096]{1,0:T(4,128)(2,1)}, u32[]{:S(2)}) copy-start(bf16[4,4096]{1,0:T(4,128)(2,1)} %param.30) | copy-start | bytes 98308
  216.2 83.0 %all-to-all-start.1 = ((bf16[128,2,6,2048]{3,1,2,0:T(2,128)(2,1)}), bf16[128,2,6,2048]{3,1,2,0:T(2,128)(2,1)}, u32[]{:S(2)}, u32[]{:S(2)}) async-start(bf16[128,2,6,2048]{3,1,2,0:T(2,128)(2,1)} %copy.78), calls=%async_computation.1 | async-start | bytes 12582912 | tf_op jit(solution)/shard_map/all_to_all | solution.py:145
  227.8 388.8 %all-gather.16.cloned.1.call-start = ((), (), s32[]{:S(2)}) async-start(), calls=%async_computation.7 | async-start | bytes 8912896 | tf_op jit(solution)/shard_map/all_gather | solution.py:16
  345.8 9.8 %copy-start.18 = (f32[2048]{0:T(1024)S(1)}, f32[2048]{0:T(1024)}, u32[]{:S(2)}) copy-start(f32[2048]{0:T(1024)} %param.27) | copy-start | bytes 24580
  345.8 10.2 %copy-start.21 = (f32[16]{0:T(128)S(1)}, f32[16]{0:T(128)}, u32[]{:S(2)}) copy-start(f32[16]{0:T(128)} %param.32) | copy-start | bytes 196
  355.6 9.2 copy-start.15
  364.8 5.2 collective-permute-start
  371.6 1.7 copy-start.7
  373.4 1.0 copy-start.12
  373.4 162.4 %slice-start = ((f32[128,4096]{1,0:T(8,128)}), f32[128,2048]{1,0:T(8,128)S(1)}, s32[]{:S(2)}) async-start(f32[128,4096]{1,0:T(8,128)} %copy-done.7), calls=%async_computation.8 | async-start | bytes 2097152 | tf_op jit(solution)/shard_map/slice | solution.py:181
  535.7 6.7 copy-start.10
  540.8 1.7 copy-start.3
  542.4 3.5 copy-start.11
  545.5 143.7 %all-gather.14.cloned.1.call-start = ((), (), s32[]{:S(2)}) async-start(), calls=%async_computation.6 | async-start | bytes 8912896 | tf_op jit(solution)/shard_map/all_gather | solution.py:16
  549.0 140.2 %copy-start.5 = (f32[16,128,128]{2,1,0:T(8,128)}, f32[16,128,128]{2,1,0:T(8,128)S(1)}, u32[]{:S(2)}) copy-start(f32[16,128,128]{2,1,0:T(8,128)S(1)} %fusion.65) | copy-start | bytes 3145732
  551.8 283.2 %all-reduce.2.cloned.1.call-start = ((), (), s32[]{:S(2)}) async-start(), calls=%async_computation.3 | async-start | bytes 2097152 | tf_op jit(solution)/shard_map/psum | solution.py:43
  727.3 110.6 %copy-start.16 = (f32[16,8,8,128]{3,1,2,0:T(8,128)S(1)}, f32[16,8,8,128]{3,1,2,0:T(8,128)}, u32[]{:S(2)}) copy-start(f32[16,8,8,128]{3,1,2,0:T(8,128)} %get-tuple-element.185) | copy-start | bytes 1572868
  728.5 143.1 %all-gather.10.cloned.1.call-start = ((), (), s32[]{:S(2)}) async-start(), calls=%async_computation.4 | async-start | bytes 4718592 | tf_op jit(solution)/shard_map/all_gather | solution.py:49
  837.3 68.0 %all-gather.12.cloned.1.call-start = ((), (), s32[]{:S(2)}) async-start(), calls=%async_computation.5 | async-start | bytes 4718592 | tf_op jit(solution)/shard_map/all_gather | solution.py:49
  837.9 1.8 copy-start.13
  838.7 1.1 copy-start.1
  918.0 1.2 copy-start.4
  918.0 1.5 copy-start.6
  918.0 2.7 copy-start.2
  919.5 3.1 copy-start.14
  920.7 3.9 copy-start.22
Sparse Core Ops, SparseCore 0:
  10.1 183.8 all-gather.7
  545.6 70.9 all-gather.15
  618.8 70.3 all-gather.13
  728.6 106.3 all-reduce.1
  837.5 34.0 all-gather.9
  873.2 32.1 all-gather.11
where the time goes:
time: 942 us; the launch traced here: 933 us
  waiting for transfers between devices  381 us (40%)
  other arithmetic  175 us (19%)
  local copies, waits for them, and re-layouts  132 us (14%)
  matrix products  108 us (11%)
  blocking collectives  106 us (11%)
  between operations  15.1 us (2%)
  starting transfers between devices  14.8 us (2%)
    another operation x4, other arithmetic, per_device(): lax.linalg.triangular_solve(system, scaled_keys, left_side=True, lower=Tr...  158 us
    all_gather x2, waiting for transfers between devices, prefix_2(): lax.all_gather(a.astype(kind), axis)  137 us
    psum x1, waiting for transfers between devices, spread_2(): return lax.psum(kept, axis)  106 us
    all_to_all x1, blocking collectives, per_device(): lax.all_to_all(outgoing, ('outer', 'inner'), split_axis=0, concat_axis=0,...  106 us
    all_to_all x1, waiting for transfers between devices, per_device(): lax.all_to_all(served, ('outer', 'inner'), split_axis=0, concat_axis=0, t...  70.9 us
    all_gather x2, waiting for transfers between devices, entering(): lax.all_gather(part.astype(kind), axis)  62.3 us
    scatter x1, local copies, waits for them, and re-layouts, per_device(): outgoing = jnp.zeros((n_dev * local_experts * capacity, width), jnp.bfloa...  34.4 us
    dot_general x19, matrix products, join_maps(): jnp.einsum('hij,hjv->hiv', next_map, first_state, precision=lax.Precision...  32.1 us
  transfers between devices with their start and end apart: 8, of which 7 were waited for; matrix products, arithmetic and copies ran while one was open for 18% of the time, Pallas kernels for 0%

commit v1 on v0

--- a/solution.py
+++ b/solution.py
@@ -74,12 +74,30 @@
 
 
 def run_experts(piece, gate_weight, up_weight, down_weight):
-    gate = jnp.einsum("secd,edf->secf", piece, gate_weight, preferred_element_type=jnp.float32)
-    upper = jnp.einsum("secd,edf->secf", piece, up_weight, preferred_element_type=jnp.float32)
+    gate = jnp.einsum("esd,edf->esf", piece, gate_weight, preferred_element_type=jnp.float32)
+    upper = jnp.einsum("esd,edf->esf", piece, up_weight, preferred_element_type=jnp.float32)
     hidden = (jax.nn.silu(gate) * upper).astype(jnp.bfloat16)
     return jnp.einsum(
-        "secf,efd->secd", hidden, down_weight, preferred_element_type=jnp.float32
+        "esf,efd->esd", hidden, down_weight, preferred_element_type=jnp.float32
     ).astype(jnp.bfloat16)
+
+
+def unit_lower_inverse(system):
+    size = system.shape[-1]
+    if size == 1:
+        return jnp.ones_like(system)
+    half = size // 2
+    both = unit_lower_inverse(jnp.stack([system[..., :half, :half], system[..., half:, half:]]))
+    first, second = both[0], both[1]
+    corner = -jnp.einsum(
+        "...ij,...jk->...ik",
+        second,
+        jnp.einsum("...ij,...jk->...ik", system[..., half:, :half], first, precision=lax.Precision.HIGHEST),
+        precision=lax.Precision.HIGHEST,
+    )
+    top = jnp.concatenate([first, jnp.zeros_like(first)], axis=-1)
+    bottom = jnp.concatenate([corner, second], axis=-1)
+    return jnp.concatenate([top, bottom], axis=-2)
 
 
 def join_maps(earlier, later):
@@ -119,34 +137,39 @@
     capacity = max(2, 6 * tok_count * top_count // (5 * experts_all))
     normed_first = rms_scale(tokens_in, first_gain).astype(jnp.bfloat16)
     mix_weight = route_weight / jnp.sum(route_weight, axis=1, keepdims=True)
-    pairs = tok_count * top_count
-    flat = expert_ids.reshape(-1)
-    onehot = (flat[:, None] == jnp.arange(experts_all, dtype=jnp.int32)[None, :]).astype(jnp.int32)
-    before = jnp.cumsum(onehot, axis=0) - onehot
-    slot_index = jnp.sum(before * onehot, axis=1)
+    flat_ids = expert_ids
     target = (
-        flat // local_experts * (local_experts * capacity)
-        + flat % local_experts * capacity
-        + slot_index
-    )
-    owner = jnp.arange(pairs, dtype=jnp.int32) // top_count
-    outgoing = (
-        jnp.zeros((n_dev * local_experts * capacity, width), jnp.bfloat16)
-        .at[target]
-        .set(normed_first[owner])
-    )
-    outgoing = outgoing.reshape(n_dev, local_experts, capacity, width)
+        flat_ids % local_experts * (n_dev * capacity)
+        + flat_ids // local_experts * capacity
+    )
+    onehot = (flat_ids[:, :, None] == jnp.arange(experts_all, dtype=jnp.int32)[None, None, :]).astype(
+        jnp.int32
+    )
+    counted = jnp.sum(onehot, axis=1)
+    before = jnp.cumsum(counted, axis=0) - counted
+    slot_index = jnp.sum(before[:, None, :] * onehot, axis=2)
+    target = target + slot_index
+    slots = jnp.arange(n_dev * local_experts * capacity, dtype=jnp.int32)
+    hits = target[:, :, None] == slots[None, None, :]
+    dispatch = jnp.any(hits, axis=1).astype(jnp.bfloat16)
+    outgoing = jnp.einsum(
+        "ts,td->sd", dispatch, normed_first, preferred_element_type=jnp.float32
+    ).astype(jnp.bfloat16)
+    outgoing = outgoing.reshape(local_experts, n_dev * capacity, width)
     served = run_experts(
-        lax.all_to_all(outgoing, ("outer", "inner"), split_axis=0, concat_axis=0, tiled=True),
+        lax.all_to_all(outgoing, ("outer", "inner"), split_axis=1, concat_axis=1, tiled=True),
         gate_weight,
         up_weight,
         down_weight,
     )
-    returned = lax.all_to_all(served, ("outer", "inner"), split_axis=0, concat_axis=0, tiled=True)
-    rows_back = (
-        returned.reshape(-1, width)[target].astype(jnp.float32) * mix_weight.reshape(-1)[:, None]
-    )
-    mixture = jnp.sum(rows_back.reshape(tok_count, top_count, width), axis=1)
+    returned = lax.all_to_all(served, ("outer", "inner"), split_axis=1, concat_axis=1, tiled=True)
+    returned = returned.reshape(-1, width)
+    combine = jnp.sum(jnp.where(hits, mix_weight[:, :, None], 0.0), axis=1)
+    combine_hi = combine.astype(jnp.bfloat16)
+    combine_lo = (combine - combine_hi.astype(jnp.float32)).astype(jnp.bfloat16)
+    mixture = jnp.dot(combine_hi, returned, preferred_element_type=jnp.float32) + jnp.dot(
+        combine_lo, returned, preferred_element_type=jnp.float32
+    )
     hidden_out = (tokens_in.astype(jnp.float32) + mixture).astype(jnp.bfloat16)
     normed_second = rms_scale(hidden_out, second_gain).astype(jnp.bfloat16)
     mixed = jnp.dot(
@@ -198,11 +221,12 @@
     growth = jnp.exp(cumulative)
     scaled_keys = key_major * (strength * growth)[:, :, None]
     scaled_values = value_major * strength[:, :, None]
-    key_resolved = lax.linalg.triangular_solve(
-        system, scaled_keys, left_side=True, lower=True, unit_diagonal=True
-    )
-    value_resolved = lax.linalg.triangular_solve(
-        system, scaled_values, left_side=True, lower=True, unit_diagonal=True
+    inverse = unit_lower_inverse(system)
+    key_resolved = jnp.einsum(
+        "hts,hsd->htd", inverse, scaled_keys, precision=lax.Precision.HIGHEST
+    )
+    value_resolved = jnp.einsum(
+        "hts,hsd->htd", inverse, scaled_values, precision=lax.Precision.HIGHEST
     )
     tail = jnp.exp(cumulative[:, -1:] - cumulative)
     trailing_keys = key_major * tail[:, :, None]

time: 942 us -> 731 us (0.78)
  other arithmetic: 175 us -> 18.3 us
  local copies, waits for them, and re-layouts: 132 us -> 51.3 us
  matrix products: 108 us -> 125 us
  waiting for transfers between devices: 381 us -> 396 us
  blocking collectives: 106 us -> 96 us
    another operation x7 -> x6, other arithmetic: 159 us -> 2.31 us  [the longest x5 2.12 us: unit_lower_inverse(): jnp.stack([system[..., :half, :half], system[..., half:, half:]])]
    scatter x1 -> x0, local copies, waits for them, and re-layouts: 34.4 us -> none  [per_device(): outgoing = jnp.zeros((n_dev * local_experts * capacity, width), jnp.bfloa...]
    dot_general x2 -> x19, matrix products: 28.2 us -> 51.7 us  [the longest x1 16.5 us: run_experts(): jnp.einsum('esf,efd->esd', hidden, down_weight, preferred_element_type=jn...]
    reshape x5 -> x1, local copies, waits for them, and re-layouts: 33.8 us -> 13 us  [per_device(): outgoing = outgoing.reshape(local_experts, n_dev * capacity, width)]
    gather x1 -> x0, local copies, waits for them, and re-layouts: 14.4 us -> none  [per_device(): returned.reshape(-1, width)[target].astype(jnp.float32)]
    all_to_all x1, waiting for transfers between devices: 70.9 us -> 84.8 us  [per_device(): lax.all_to_all(served, ('outer', 'inner'), split_axis=1, concat_axis=1, t...]
    convert_element_type x2 -> x1, local copies, waits for them, and re-layouts: 23.1 us -> 12.7 us  [run_experts(): return jnp.einsum('esf,efd->esd', hidden, down_weight, preferred_element_...]
    all_to_all x1, blocking collectives: 106 us -> 96 us  [per_device(): lax.all_to_all(outgoing, ('outer', 'inner'), split_axis=1, concat_axis=1,...]
  transfers between devices with their start and end apart: 8 -> 8, of which waited for: 7 -> 7; matrix products, arithmetic and copies ran while one was open for 18% -> 11% of each run, Pallas kernels for 0% -> 0%
where the time goes in v1:
time: 731 us; the launch traced here: 722 us
  waiting for transfers between devices  396 us (54%)
  matrix products  125 us (17%)
  blocking collectives  96 us (13%)
  local copies, waits for them, and re-layouts  51.3 us (7%)
  other arithmetic  18.3 us (3%)
  starting transfers between devices  17.9 us (2%)
  between operations  15.7 us (2%)
    all_gather x2, waiting for transfers between devices, prefix_2(): lax.all_gather(a.astype(kind), axis)  141 us
    psum x1, waiting for transfers between devices, spread_2(): return lax.psum(kept, axis)  106 us
    all_to_all x1, blocking collectives, per_device(): lax.all_to_all(outgoing, ('outer', 'inner'), split_axis=1, concat_axis=1,...  96 us
    all_to_all x1, waiting for transfers between devices, per_device(): lax.all_to_all(served, ('outer', 'inner'), split_axis=1, concat_axis=1, t...  84.8 us
    all_gather x2, waiting for transfers between devices, entering(): lax.all_gather(part.astype(kind), axis)  62.3 us
    dot_general x19, matrix products, join_maps(): jnp.einsum('hij,hjv->hiv', next_map, first_state, precision=lax.Precision...  32.1 us
    dot_general x1, matrix products, run_experts(): jnp.einsum('esf,efd->esd', hidden, down_weight, preferred_element_type=jn...  16.5 us
    dot_general x10, matrix products, join_maps(): jnp.einsum('hij,hjk->hik', next_map, first_map, precision=lax.Precision.H...  16.5 us
  transfers between devices with their start and end apart: 8, of which 7 were waited for; matrix products, arithmetic and copies ran while one was open for 11% of the time, Pallas kernels for 0%

profile of v1, /device:TPU:83, one launch (start us, length us, event | category | flops | bytes accessed | tf_op | source)
XLA Modules:
  0.0 721.6 jit_solution(11721711058515278131)
XLA Ops:
  13.5 2.9 convolution_convert_fusion
  16.4 13.0 %copy.112 = bf16[2,768,2048]{2,0,1:T(2,128)(2,1)S(1)} copy(bf16[2,768,2048]{2,1,0:T(8,128)(2,1)S(1)} %bitcast.186) | data formatting | bytes 12582912 | tf_op jit(solution)/shard_map/reshape | solution.py:158
  29.5 96.0 %all_to_all.10 = bf16[2,768,2048]{2,0,1:T(2,128)(2,1)S(1)} all-to-all(bf16[2,768,2048]{2,0,1:T(2,128)(2,1)S(1)} %copy.112), channel_id=1, replica_groups=mesh['outer'=8,'inner'=16] {'outer','inner'}, dimensions={1} | all-to-all | bytes 12582912 | tf_op jit(solution)/shard_map/all_to_all | solution.py:160
  125.5 2.7 copy-done.12
  128.1 5.3 fusion.18
  133.5 16.5 %convolution_convert_fusion.2 = bf16[2,768,2048]{2,1,0:T(8,128)(2,1)} fusion(bf16[2,512,2048]{2,1,0:T(8,128)(2,1)} %param.24, f32[2,768,512]{2,1,0:T(8,128)} %fusion.18, bf16[2,2048,512]{2,1,0:T(8,128)(2,1)} %param.23, bf16[2,768,2048]{2,0,1:T(2,128)(2,1)} %copy-done.12), kind=kOutput, calls=%fused_computation.26 | convolution fusion | flops 6450315264 | bytes 24117248 | tf_op jit(solution)/shard_map/esf,efd->esd/dot_general | solution.py:80
  150.0 12.7 %copy.115 = bf16[2,768,2048]{2,0,1:T(2,128)(2,1)} copy(bf16[2,768,2048]{2,1,0:T(8,128)(2,1)} %convolution_convert_fusion.2) | data formatting | bytes 12582912 | tf_op jit(solution)/shard_map/convert_element_type | solution.py:82
  162.7 13.7 %all-to-all-start.1 = ((bf16[2,768,2048]{2,0,1:T(2,128)(2,1)}), bf16[2,768,2048]{2,0,1:T(2,128)(2,1)}, u32[]{:S(2)}, u32[]{:S(2)}) async-start(bf16[2,768,2048]{2,0,1:T(2,128)(2,1)} %copy.115), calls=%async_computation.1 | async-start | bytes 12582912 | tf_op jit(solution)/shard_map/all_to_all | solution.py:165
  178.0 84.8 %all-to-all-done.1 = bf16[2,768,2048]{2,0,1:T(2,128)(2,1)} async-done(((bf16[2,768,2048]{2,0,1:T(2,128)(2,1)}), bf16[2,768,2048]{2,0,1:T(2,128)(2,1)}, u32[]{:S(2)}, u32[]{:S(2)}) %all-to-all-start.1) | async-done | bytes 6291488 | tf_op jit(solution)/shard_map/all_to_all | solution.py:165
  262.9 5.7 copy.116
  272.0 8.2 %convolution_convert_fusion.1 = bf16[128,4096]{1,0:T(8,128)(2,1)S(1)} fusion(bf16[2048,4096]{1,0:T(8,128)(2,1)} %all-gather.8.cloned.1.call-done, bf16[128,2048]{1,0:T(8,128)(2,1)S(1)} %get-tuple-element.227, f32[2048]{0:T(1024)S(1)} %copy-done.36, f32[128]{0:T(128)S(1)} %add_rsqrt_fusion.3), kind=kOutput, calls=%fused_computation.25 | convolution fusion | flops 2149056512 | bytes 18358784 | tf_op jit(solution)/shard_map/dot_general | solution.py:175
  280.3 3.7 collective-permute-start
  288.3 2.4 fusion.34
  301.7 4.7 fusion.111
  306.5 4.8 convolution_negate_fusion.5
  312.3 3.1 fusion.73
  315.5 1.8 convolution_negate_fusion.4
  327.9 3.0 fusion.119
  331.1 2.8 fusion.78
  333.9 2.8 fusion.118
  336.8 68.7 %all-gather.16.cloned.1.call-done = bf16[256,128,128]{2,1,0:T(8,128)(2,1)} async-done(((bf16[16,128,128]{2,1,0:T(8,128)(2,1)}), bf16[256,128,128]{2,1,0:T(8,128)(2,1)}) %all-gather.16.cloned.1.call-update) | async-done | bytes 8388624 | tf_op jit(solution)/shard_map/all_gather | solution.py:16
  405.6 72.5 %all-gather.14.cloned.1.call-done = bf16[256,128,128]{2,1,0:T(8,128)(2,1)} async-done(((bf16[16,128,128]{2,1,0:T(8,128)(2,1)}), bf16[256,128,128]{2,1,0:T(8,128)(2,1)}) %all-gather.14.cloned.1.call-update) | async-done | bytes 8388624 | tf_op jit(solution)/shard_map/all_gather | solution.py:16
  478.3 34.3 %while.26 = (s32[]{:T(128)}, f32[16,128,128]{2,1,0:T(8,128)S(1)}, f32[16,128,128]{2,1,0:T(8,128)S(1)}, s32[]{:T(128)}, bf16[16,16,128,128]{3,2,1,0:T(8,128)(2,1)...) while((s32[]{:T(128)}, f32[16,128,128]{2,1,0:T(8,128)S(1)}, ...), condition=%wide.region_12.13_spmd, body=%wide.region_11.12_spmd.sunk | while | flops 805830656 | bytes 9962627 | solution.py:30
  478.4 1.9 convolution_add_fusion.6
  480.4 1.7 fusion.170
  482.2 1.9 convolution_add_fusion.6
  484.1 1.7 fusion.170
  486.0 1.9 convolution_add_fusion.6
  487.9 1.7 fusion.170
  489.7 1.9 convolution_add_fusion.6
  491.7 1.7 fusion.170
  493.5 1.9 convolution_add_fusion.6
  495.5 1.7 fusion.170
  497.3 1.9 convolution_add_fusion.6
  499.3 1.7 fusion.170
  501.1 1.9 convolution_add_fusion.6
  503.1 1.7 fusion.170
  504.9 1.9 convolution_add_fusion.6
  508.7 1.9 convolution_add_fusion.6
  513.8 2.4 fusion.37
  517.4 106.1 %all-reduce.9.cloned.1.call-done = bf16[2,16,128,128]{3,2,1,0:T(8,128)(2,1)} async-done(((bf16[2,16,128,128]{3,2,1,0:T(8,128)(2,1)}), bf16[2,16,128,128]{3,2,1,0:T(8,128)(2,1)}) %all-reduce.9.cloned.1.call-update) | async-done | bytes 1048592 | tf_op jit(solution)/shard_map/psum | solution.py:43
  623.5 2.3 fusion.116
  628.2 3.3 convolution_multiply_fusion
  631.5 28.6 %all-gather.10.cloned.1.call-done = bf16[8,16,128,128]{3,2,1,0:T(8,128)(2,1)} async-done(((bf16[1,16,128,128]{3,2,1,0:T(8,128)(2,1)}), bf16[8,16,128,128]{3,2,1,0:T(8,128)(2,1)}) %all-gather.10.cloned.1.call-update) | async-done | bytes 4194320 | tf_op jit(solution)/shard_map/all_gather | solution.py:49
  660.1 33.7 %all-gather.12.cloned.1.call-done = bf16[8,16,128,128]{3,2,1,0:T(8,128)(2,1)} async-done(((bf16[1,16,128,128]{3,2,1,0:T(8,128)(2,1)}), bf16[8,16,128,128]{3,2,1,0:T(8,128)(2,1)}) %all-gather.12.cloned.1.call-update) | async-done | bytes 4194320 | tf_op jit(solution)/shard_map/all_gather | solution.py:49
  693.8 12.6 %while.27 = (s32[]{:T(128)}, bf16[16,128,128]{2,1,0:T(8,128)(2,1)S(1)}, s32[]{:T(128)}, bf16[8,16,128,128]{3,2,1,0:T(8,128)(2,1)}, bf16[8,16,128,128]{3,2,1,0:T(8,128)(2,1)}, /*index=5*/s32[]{:T(128)}, s32[]{:T(128)}) while((s32[]{:T(128)}, bf16[16,128,128]{2,1,0:T(8,128)(2,1)S(1)}, s32[]{:T(128)}, ...), condition=%wide.region_15.16_spmd.clone, body=%wide.region_14.15_spmd.clone.sunk | while | flops 68157440 | bytes 3672671 | solution.py:64
  709.2 1.9 fusion.31
  711.2 1.9 multiply_reduce_fusion
  (225 shorter events, 63.7 us)
Async XLA Ops:
  7.2 263.9 %copy-start = (bf16[2048,32]{0,1:T(8,128)(2,1)S(1)}, bf16[2048,32]{0,1:T(8,128)(2,1)}, u32[]{:S(2)}) copy-start(bf16[2048,32]{0,1:T(8,128)(2,1)} %param.27) | copy-start | bytes 393220
  7.2 264.8 %all-gather.8.cloned.1.call-start = ((), (), s32[]{:S(2)}) async-start(), calls=%async_computation.2 | async-start | bytes 17825792 | tf_op jit(solution)/shard_map/all_gather | solution.py:177
  29.4 98.7 %copy-start.44 = (bf16[2,2048,512]{2,1,0:T(8,128)(2,1)S(1)}, bf16[2,2048,512]{2,1,0:T(8,128)(2,1)}, u32[]{:S(2)}) copy-start(bf16[2,2048,512]{2,1,0:T(8,128)(2,1)} %param.22) | copy-start | bytes 12582916
  125.5 2.7 copy-start.12
  162.7 14.0 %copy-start.41 = (f32[128,10]{0,1:T(8,128)S(1)}, f32[128,10]{0,1:T(8,128)}, u32[]{:S(2)}) copy-start(f32[128,10]{0,1:T(8,128)} %param.20) | copy-start | bytes 15364
  162.7 14.1 %copy-start.45 = (f32[16]{0:T(128)S(1)}, f32[16]{0:T(128)}, u32[]{:S(2)}) copy-start(f32[16]{0:T(128)} %param.29) | copy-start | bytes 196
  162.7 15.3 %copy-start.35 = (bf16[4,4096]{1,0:T(4,128)(2,1)S(1)}, bf16[4,4096]{1,0:T(4,128)(2,1)}, u32[]{:S(2)}) copy-start(bf16[4,4096]{1,0:T(4,128)(2,1)} %param.28) | copy-start | bytes 98308
  162.7 100.2 %all-to-all-start.1 = ((bf16[2,768,2048]{2,0,1:T(2,128)(2,1)}), bf16[2,768,2048]{2,0,1:T(2,128)(2,1)}, u32[]{:S(2)}, u32[]{:S(2)}) async-start(bf16[2,768,2048]{2,0,1:T(2,128)(2,1)} %copy.115), calls=%async_computation.1 | async-start | bytes 12582912 | tf_op jit(solution)/shard_map/all_to_all | solution.py:165
  176.4 229.2 %all-gather.16.cloned.1.call-start = ((), (), s32[]{:S(2)}) async-start(), calls=%async_computation.7 | async-start | bytes 8912896 | tf_op jit(solution)/shard_map/all_gather | solution.py:16
  176.7 111.6 %copy-start.33 = (pred[128,128]{1,0:T(8,128)(4,1)}, pred[128,128]{1,0:T(8,128)(4,1)S(1)}, u32[]{:S(2)}) copy-start(pred[128,128]{1,0:T(8,128)(4,1)S(1)} %get-tuple-element.234) | copy-start | bytes 49156
  269.6 1.4 copy-start.36
  269.6 1.8 copy-start.42
  271.0 9.2 %copy-start.29 = (bf16[128,2048]{1,0:T(8,128)(2,1)}, bf16[128,2048]{1,0:T(8,128)(2,1)S(1)}, u32[]{:S(2)}) copy-start(bf16[128,2048]{1,0:T(8,128)(2,1)S(1)} %get-tuple-element.227) | copy-start | bytes 1572868
  280.3 4.7 collective-permute-start
  286.5 1.6 copy-start.10
  288.3 3.1 copy-start.2
  291.4 1.1 copy-start.24
  292.2 19.1 %copy-start.26 = (f32[1,2,2,2,16,8,8]{6,5,4,3,2,1,0:T(8,128)}, f32[1,2,2,2,16,8,8]{6,5,4,3,2,1,0:T(8,128)S(1)}, u32[]{:S(2)}) copy-start(f32[1,2,2,2,16,8,8]{6,5,4,3,2,1,0:T(8,128)S(1)} %get-tuple-element.201) | copy-start | bytes 98308
  292.2 19.1 %copy-start.27 = (f32[1,2,2,2,16,8,8]{6,5,4,3,2,1,0:T(8,128)}, f32[1,2,2,2,16,8,8]{6,5,4,3,2,1,0:T(8,128)S(1)}, u32[]{:S(2)}) copy-start(f32[1,2,2,2,16,8,8]{6,5,4,3,2,1,0:T(8,128)S(1)} %get-tuple-element.202) | copy-start | bytes 98308
  301.7 9.5 %copy-start.30 = (f32[1,2,2,2,2,2,16,2,2]{8,7,6,5,4,3,2,1,0:T(2,128)S(1)}, f32[1,2,2,2,2,2,16,2,2]{8,7,6,5,4,3,2,1,0:T(2,128)}, u32[]{:S(2)}) copy-start(f32[1,2,2,2,2,2,16,2,2]{8,7,6,5,4,3,2,1,0:T(2,128)} %copy.134) | copy-start | bytes 24580
  301.7 9.5 %copy-start.31 = (f32[1,2,2,2,2,2,16,2,2]{8,7,6,5,4,3,2,1,0:T(2,128)S(1)}, f32[1,2,2,2,2,2,16,2,2]{8,7,6,5,4,3,2,1,0:T(2,128)}, u32[]{:S(2)}) copy-start(f32[1,2,2,2,2,2,16,2,2]{8,7,6,5,4,3,2,1,0:T(2,128)} %copy.135) | copy-start | bytes 24580
  312.2 5.5 copy-start.23
  312.2 5.5 copy-start.25
  317.7 2.3 copy-start.19
  317.7 2.3 copy-start.21
  320.0 1.6 copy-start.17
  323.3 1.7 copy-start.38
  323.3 1.7 copy-start.39
  323.6 3.0 copy-start.11
  324.3 6.6 copy-start.14
  324.3 6.6 copy-start.15
  326.5 4.4 copy-start.40
  327.9 8.9 %copy-start.6 = (f32[16,128,128]{2,1,0:T(8,128)}, f32[16,128,128]{2,1,0:T(8,128)S(1)}, u32[]{:S(2)}) copy-start(f32[16,128,128]{2,1,0:T(8,128)S(1)} %fusion.45) | copy-start | bytes 3145732
  330.9 147.2 %all-gather.14.cloned.1.call-start = ((), (), s32[]{:S(2)}) async-start(), calls=%async_computation.6 | async-start | bytes 8912896 | tf_op jit(solution)/shard_map/all_gather | solution.py:16
  333.9 2.8 copy-start.8
  336.8 286.7 %all-reduce.9.cloned.1.call-start = ((), (), s32[]{:S(2)}) async-start(), calls=%async_computation.3 | async-start | bytes 2097152 | tf_op jit(solution)/shard_map/psum | solution.py:43
  516.2 110.2 %copy-start.32 = (f32[16,8,8,128]{3,1,2,0:T(8,128)S(1)}, f32[16,8,8,128]{3,1,2,0:T(8,128)}, u32[]{:S(2)}) copy-start(f32[16,8,8,128]{3,1,2,0:T(8,128)} %get-tuple-element.186) | copy-start | bytes 1572868
  517.3 110.8 %copy-start.34 = (pred[128,128]{1,0:T(8,128)(4,1)S(1)}, pred[128,128]{1,0:T(8,128)(4,1)}, u32[]{:S(2)}) copy-start(pred[128,128]{1,0:T(8,128)(4,1)} %copy-done.33) | copy-start | bytes 49156
  517.3 142.7 %all-gather.10.cloned.1.call-start = ((), (), s32[]{:S(2)}) async-start(), calls=%async_computation.4 | async-start | bytes 4718592 | tf_op jit(solution)/shard_map/all_gather | solution.py:49
  625.8 68.0 %all-gather.12.cloned.1.call-start = ((), (), s32[]{:S(2)}) async-start(), calls=%async_computation.5 | async-start | bytes 4718592 | tf_op jit(solution)/shard_map/all_gather | solution.py:49
  626.4 1.8 copy-start.3
  706.5 1.2 copy-start.7
  706.5 1.5 copy-start.9
  706.5 2.7 copy-start.5
  706.5 2.7 copy-start.37
  708.0 3.1 copy-start.28
  709.2 3.9 copy-start.43
  709.2 5.1 copy-start.1
  (6 other events, 5.6 us)
Sparse Core Ops, SparseCore 0:
  10.1 217.4 all-gather.7
  331.0 74.5 all-gather.15
  407.7 70.3 all-gather.13
  517.4 106.0 all-reduce.8
  625.9 34.0 all-gather.9
  661.6 32.1 all-gather.11

commit v2 on v1

--- a/solution.py
+++ b/solution.py
@@ -109,6 +109,34 @@
         + next_state
     )
     return (joined_map, joined_state)
+
+
+def shifted_linear(value, axes, count, steps):
+    return lax.ppermute(value, axes, [(source, source + steps) for source in range(count - steps)])
+
+
+def chained_state(state_map, state_increment, axes, count):
+    place = lax.axis_index(axes)
+    steps = 1
+    while steps < count:
+        last = steps * 2 >= count
+        far_state = shifted_linear(state_increment.astype(jnp.bfloat16), axes, count, steps)
+        reached = place >= steps
+        joined_state = (
+            jnp.einsum(
+                "hij,hjv->hiv", state_map, far_state.astype(jnp.float32), precision=lax.Precision.HIGHEST
+            )
+            + state_increment
+        )
+        if not last:
+            far_map = shifted_linear(state_map.astype(jnp.bfloat16), axes, count, steps)
+            joined_map = jnp.einsum(
+                "hij,hjk->hik", state_map, far_map.astype(jnp.float32), precision=lax.Precision.HIGHEST
+            )
+            state_map = jnp.where(reached, joined_map, state_map)
+        state_increment = jnp.where(reached, joined_state, state_increment)
+        steps *= 2
+    return shifted_linear(state_increment.astype(jnp.bfloat16), axes, count, 1).astype(jnp.float32)
 
 
 def per_device(
@@ -239,13 +267,7 @@
     state_increment = jnp.einsum(
         "xbe,xbz->xez", trailing_keys, value_resolved, precision=lax.Precision.HIGHEST
     )
-    identity = (eye_heads, jnp.zeros_like(state_increment))
-    inner_pre = prefix_2((state_map, state_increment), "inner", join_maps, identity)
-    inclusive = join_maps(inner_pre, (state_map, state_increment))
-    group = spread_2(shortened(jnp.stack(inclusive)), "inner", n_inner - 1)
-    outer_pre = entering((group[0], group[1]), "outer", join_maps, identity)
-    prefix = join_maps(outer_pre, inner_pre)
-    initial_state = prefix[1]
+    initial_state = chained_state(state_map, state_increment, ("outer", "inner"), n_dev)
     updates = value_resolved - jnp.einsum(
         "mwx,mxd->mwd", key_resolved, initial_state, precision=lax.Precision.HIGHEST
     )

time: 731 us -> 530 us (0.73)
  the two profiles are of different devices: /device:TPU:83 before, /device:TPU:1 now
where the time goes in v2:
time: 530 us; the launch traced here: 525 us
  waiting for transfers between devices  152 us (29%)
  matrix products  103 us (19%)
  blocking collectives  98.5 us (19%)
  starting transfers between devices  92.3 us (17%)
  local copies, waits for them, and re-layouts  47.6 us (9%)
  other arithmetic  16.2 us (3%)
  between operations  15.4 us (3%)
    all_to_all x1, blocking collectives, per_device(): lax.all_to_all(outgoing, ('outer', 'inner'), split_axis=1, concat_axis=1,...  98.5 us
    all_to_all x1, waiting for transfers between devices, per_device(): lax.all_to_all(served, ('outer', 'inner'), split_axis=1, concat_axis=1, t...  82.6 us
    ppermute x14, starting transfers between devices, shifted_linear(): lax.ppermute(value, axes, [(source, source + steps) for source in range(c...  71 us
    ppermute x14, waiting for transfers between devices, shifted_linear(): lax.ppermute(value, axes, [(source, source + steps) for source in range(c...  68 us
    dot_general x1, matrix products, run_experts(): jnp.einsum('esf,efd->esd', hidden, down_weight, preferred_element_type=jn...  16.5 us
    dot_general x7, matrix products, chained_state(): jnp.einsum('hij,hjv->hiv', state_map, far_state.astype(jnp.float32), prec...  16.2 us
    dot_general x6, matrix products, chained_state(): jnp.einsum('hij,hjk->hik', state_map, far_map.astype(jnp.float32), precis...  15.8 us
    all_to_all x1, starting transfers between devices, per_device(): lax.all_to_all(served, ('outer', 'inner'), split_axis=1, concat_axis=1, t...  13.8 us
  transfers between devices with their start and end apart: 17, of which 13 were waited for; matrix products, arithmetic and copies ran while one was open for 20% of the time, Pallas kernels for 0%

profile of v2, /device:TPU:1, one launch (start us, length us, event | category | flops | bytes accessed | tf_op | source)
XLA Modules:
  0.0 524.6 jit_solution(8350318702020959367)
XLA Ops:
  13.5 2.9 convolution_convert_fusion
  16.4 13.0 %copy.112 = bf16[2,768,2048]{2,0,1:T(2,128)(2,1)S(1)} copy(bf16[2,768,2048]{2,1,0:T(8,128)(2,1)S(1)} %bitcast.171) | data formatting | bytes 12582912 | tf_op jit(solution)/shard_map/reshape | solution.py:186
  29.5 98.5 %all_to_all.10 = bf16[2,768,2048]{2,0,1:T(2,128)(2,1)S(1)} all-to-all(bf16[2,768,2048]{2,0,1:T(2,128)(2,1)S(1)} %copy.112), channel_id=1, replica_groups=mesh['outer'=8,'inner'=16] {'outer','inner'}, dimensions={1} | all-to-all | bytes 12582912 | tf_op jit(solution)/shard_map/all_to_all | solution.py:188
  127.9 2.7 copy-done.9
  130.6 5.3 %fusion.3 = f32[2,768,512]{2,1,0:T(8,128)} fusion(bf16[2,2048,512]{2,1,0:T(8,128)(2,1)S(1)} %copy-done.44, bf16[2,768,2048]{2,0,1:T(2,128)(2,1)S(1)} %all_to_all.10), kind=kOutput, calls=%fused_computation.6 | convolution fusion | flops 3221225472 | bytes 13631488 | tf_op jit(solution)/shard_map/esd,edf->esf/dot_general | solution.py:77
  136.0 16.5 %convolution_convert_fusion.2 = bf16[2,768,2048]{2,1,0:T(8,128)(2,1)} fusion(bf16[2,512,2048]{2,1,0:T(8,128)(2,1)} %param.20, f32[2,768,512]{2,1,0:T(8,128)} %fusion.3, bf16[2,2048,512]{2,1,0:T(8,128)(2,1)} %param.19, bf16[2,768,2048]{2,0,1:T(2,128)(2,1)} %copy-done.9), kind=kOutput, calls=%fused_computation.9 | convolution fusion | flops 6450315264 | bytes 24117248 | tf_op jit(solution)/shard_map/esf,efd->esd/dot_general | solution.py:80
  152.4 12.7 %copy.115 = bf16[2,768,2048]{2,0,1:T(2,128)(2,1)} copy(bf16[2,768,2048]{2,1,0:T(8,128)(2,1)} %convolution_convert_fusion.2) | data formatting | bytes 12582912 | tf_op jit(solution)/shard_map/convert_element_type | solution.py:82
  165.1 13.8 %all-to-all-start.1 = ((bf16[2,768,2048]{2,0,1:T(2,128)(2,1)}), bf16[2,768,2048]{2,0,1:T(2,128)(2,1)}, u32[]{:S(2)}, u32[]{:S(2)}) async-start(bf16[2,768,2048]{2,0,1:T(2,128)(2,1)} %copy.115), calls=%async_computation.1 | async-start | bytes 12582912 | tf_op jit(solution)/shard_map/all_to_all | solution.py:193
  180.4 82.6 %all-to-all-done.1 = bf16[2,768,2048]{2,0,1:T(2,128)(2,1)} async-done(((bf16[2,768,2048]{2,0,1:T(2,128)(2,1)}), bf16[2,768,2048]{2,0,1:T(2,128)(2,1)}, u32[]{:S(2)}, u32[]{:S(2)}) %all-to-all-start.1) | async-done | bytes 6291488 | tf_op jit(solution)/shard_map/all_to_all | solution.py:193
  262.9 5.7 %copy.116 = bf16[2,768,2048]{2,1,0:T(8,128)(2,1)S(1)} copy(bf16[2,768,2048]{2,0,1:T(2,128)(2,1)} %all-to-all-done.1) | data formatting | bytes 12582912 | tf_op jit(solution)/shard_map/all_to_all | solution.py:193
  272.7 8.2 %convolution_convert_fusion.1 = bf16[128,4096]{1,0:T(8,128)(2,1)S(1)} fusion(bf16[2048,4096]{1,0:T(8,128)(2,1)} %all-gather.2.cloned.1.call-done, bf16[128,2048]{1,0:T(8,128)(2,1)S(1)} %get-tuple-element.54, f32[2048]{0:T(1024)S(1)} %copy-done.36, f32[128]{0:T(128)S(1)} %add_rsqrt_fusion.3), kind=kOutput, calls=%fused_computation.8 | convolution fusion | flops 2149056512 | bytes 18358784 | tf_op jit(solution)/shard_map/dot_general | solution.py:203
  281.0 7.5 %collective-permute-start = (bf16[3,4096]{1,0:T(4,128)(2,1)S(1)}, bf16[3,4096]{1,0:T(4,128)(2,1)S(1)}, u32[]{:S(2)}, u32[]{:S(2)}) collective-permute-start(bf16[3,4096]{1,0:T(4,128)(2,1)S(1)} %slice.191), channel_id=1, source_target_pairs={{0,1},{1,2},{2,3},{3,4},{4,5},{5,6},{6,7},{7,8},{8,9},{9,10},{10,1... | collective-permute-start | bytes 73736 | tf_op jit(solution)/shard_map/ppermute | solution.py:10
  292.8 2.4 fusion.17
  306.3 4.8 fusion.94
  311.1 4.8 convolution_negate_fusion.5
  332.8 7.6 %collective-permute-start.7 = (bf16[16,128,128]{2,1,0:T(8,128)(2,1)S(1)}, bf16[16,128,128]{2,1,0:T(8,128)(2,1)S(1)}, u32[]{:S(2)}, u32[]{:S(2)}) collective-permute-start(bf16[16,128,128]{2,1,0:T(8,128)(2,1)S(1)} %get-tuple-element.55), channel_id=1, source_target_pairs={{0,1},{1,2},{2,3},{3,4},{4,5},{5,6},{6,7},{7,8},{8,9},{9,10},{10,1... | collective-permute-start | bytes 1572872 | tf_op jit(solution)/shard_map/ppermute | solution.py:115
  341.8 2.8 fusion.101
  344.6 3.6 collective-permute-start.1
  348.2 4.0 collective-permute-done.7
  354.2 6.3 %collective-permute-start.8 = (bf16[16,128,128]{2,1,0:T(8,128)(2,1)}, bf16[16,128,128]{2,1,0:T(8,128)(2,1)}, u32[]{:S(2)}, u32[]{:S(2)}) collective-permute-start(bf16[16,128,128]{2,1,0:T(8,128)(2,1)} %get-tuple-element.59), channel_id=1, source_target_pairs={{0,2},{1,3},{2,4},{3,5},{4,6},{5,7},{6,8},{7,9},{8,10},{9,11},{10,... | collective-permute-start | bytes 1572872 | tf_op jit(solution)/shard_map/ppermute | solution.py:115
  360.5 3.1 collective-permute-done.1
  363.6 3.2 fusion.103
  366.8 5.3 %collective-permute-start.2 = (bf16[16,128,128]{2,1,0:T(8,128)(2,1)}, bf16[16,128,128]{2,1,0:T(8,128)(2,1)}, u32[]{:S(2)}, u32[]{:S(2)}) collective-permute-start(bf16[16,128,128]{2,1,0:T(8,128)(2,1)} %get-tuple-element.61), channel_id=1, source_target_pairs={{0,2},{1,3},{2,4},{3,5},{4,6},{5,7},{6,8},{7,9},{8,10},{9,11},{10,... | collective-permute-start | bytes 1572872 | tf_op jit(solution)/shard_map/ppermute | solution.py:115
  372.0 2.8 collective-permute-done.8
  374.8 2.9 fusion.104
  377.8 9.6 %collective-permute-start.9 = (bf16[16,128,128]{2,1,0:T(8,128)(2,1)}, bf16[16,128,128]{2,1,0:T(8,128)(2,1)}, u32[]{:S(2)}, u32[]{:S(2)}) collective-permute-start(bf16[16,128,128]{2,1,0:T(8,128)(2,1)} %get-tuple-element.63), channel_id=1, source_target_pairs={{0,4},{1,5},{2,6},{3,7},{4,8},{5,9},{6,10},{7,11},{8,12},{9,13},{1... | collective-permute-start | bytes 1572872 | tf_op jit(solution)/shard_map/ppermute | solution.py:115
  387.4 3.2 fusion.105
  390.7 13.2 %collective-permute-start.3 = (bf16[16,128,128]{2,1,0:T(8,128)(2,1)}, bf16[16,128,128]{2,1,0:T(8,128)(2,1)}, u32[]{:S(2)}, u32[]{:S(2)}) collective-permute-start(bf16[16,128,128]{2,1,0:T(8,128)(2,1)} %get-tuple-element.65), channel_id=1, source_target_pairs={{0,4},{1,5},{2,6},{3,7},{4,8},{5,9},{6,10},{7,11},{8,12},{9,13},{1... | collective-permute-start | bytes 1572872 | tf_op jit(solution)/shard_map/ppermute | solution.py:115
  403.8 4.1 collective-permute-done.9
  408.0 2.9 fusion.106
  412.9 14.9 %collective-permute-done.3 = bf16[16,128,128]{2,1,0:T(8,128)(2,1)} collective-permute-done((bf16[16,128,128]{2,1,0:T(8,128)(2,1)}, bf16[16,128,128]{2,1,0:T(8,128)(2,1)}, u32[]{:S(2)}, u32[]{:S(2)}) %collective-permute-start.3) | collective-permute-done | bytes 524320 | tf_op jit(solution)/shard_map/ppermute | solution.py:115
  427.8 3.2 fusion.107
  432.9 2.9 fusion.108
  435.8 3.6 collective-permute-start.11
  439.4 8.7 %collective-permute-done.4 = bf16[16,128,128]{2,1,0:T(8,128)(2,1)} collective-permute-done((bf16[16,128,128]{2,1,0:T(8,128)(2,1)}, bf16[16,128,128]{2,1,0:T(8,128)(2,1)}, u32[]{:S(2)}, u32[]{:S(2)}) %collective-permute-start.4) | collective-permute-done | bytes 524320 | tf_op jit(solution)/shard_map/ppermute | solution.py:115
  448.1 3.2 fusion.109
  451.3 4.5 collective-permute-start.5
  455.9 2.9 fusion.110
  458.8 2.1 collective-permute-start.12
  462.3 2.4 fusion.111
  464.7 3.7 collective-permute-start.6
  468.4 5.2 collective-permute-done.12
  475.4 5.6 %collective-permute-start.13 = (bf16[16,128,128]{2,1,0:T(8,128)(2,1)S(1)}, bf16[16,128,128]{2,1,0:T(8,128)(2,1)S(1)}, u32[]{:S(2)}, u32[]{:S(2)}) collective-permute-start(bf16[16,128,128]{2,1,0:T(8,128)(2,1)S(1)} %get-tuple-element.79), channel_id=1, source_target_pairs={{0,64},{1,65},{2,66},{3,67},{4,68},{5,69},{6,70},{7,71},{8,72},{9,... | collective-permute-start | bytes 1572872 | tf_op jit(solution)/shard_map/ppermute | solution.py:115
  481.3 3.5 collective-permute-done.6
  485.4 10.6 %collective-permute-done.13 = bf16[16,128,128]{2,1,0:T(8,128)(2,1)S(1)} collective-permute-done((bf16[16,128,128]{2,1,0:T(8,128)(2,1)S(1)}, bf16[16,128,128]{2,1,0:T(8,128)(2,1)S(1)}, u32[]{:S(2)}, u32[]{:S(2)}) %collective-permute-start.13) | collective-permute-done | bytes 524320 | tf_op jit(solution)/shard_map/ppermute | solution.py:115
  496.7 2.1 collective-permute-start.14
  499.3 2.3 convolution_multiply_fusion
  501.6 10.9 %collective-permute-done.14 = bf16[16,128,128]{2,1,0:T(8,128)(2,1)S(1)} collective-permute-done((bf16[16,128,128]{2,1,0:T(8,128)(2,1)S(1)}, bf16[16,128,128]{2,1,0:T(8,128)(2,1)S(1)}, u32[]{:S(2)}, u32[]{:S(2)}) %collective-permute-start.14) | collective-permute-done | bytes 524320 | tf_op jit(solution)/shard_map/ppermute | solution.py:115
  (189 shorter events, 60.6 us)
Async XLA Ops:
  7.2 263.9 %copy-start = (bf16[2048,32]{0,1:T(8,128)(2,1)S(1)}, bf16[2048,32]{0,1:T(8,128)(2,1)}, u32[]{:S(2)}) copy-start(bf16[2048,32]{0,1:T(8,128)(2,1)} %param.23) | copy-start | bytes 393220
  7.2 265.5 %all-gather.2.cloned.1.call-start = ((), (), s32[]{:S(2)}) async-start(), calls=%async_computation.2 | async-start | bytes 17825792 | tf_op jit(solution)/shard_map/all_gather | solution.py:205
  29.5 101.2 %copy-start.44 = (bf16[2,2048,512]{2,1,0:T(8,128)(2,1)S(1)}, bf16[2,2048,512]{2,1,0:T(8,128)(2,1)}, u32[]{:S(2)}) copy-start(bf16[2,2048,512]{2,1,0:T(8,128)(2,1)} %param.18) | copy-start | bytes 12582916
  127.9 2.7 copy-start.9
  165.1 13.8 %copy-start.40 = (f32[128,10]{0,1:T(8,128)S(1)}, f32[128,10]{0,1:T(8,128)}, u32[]{:S(2)}) copy-start(f32[128,10]{0,1:T(8,128)} %param.16) | copy-start | bytes 15364
  165.1 13.9 %copy-start.45 = (f32[16]{0:T(128)S(1)}, f32[16]{0:T(128)}, u32[]{:S(2)}) copy-start(f32[16]{0:T(128)} %param.25) | copy-start | bytes 196
  165.1 15.2 %copy-start.35 = (bf16[4,4096]{1,0:T(4,128)(2,1)S(1)}, bf16[4,4096]{1,0:T(4,128)(2,1)}, u32[]{:S(2)}) copy-start(bf16[4,4096]{1,0:T(4,128)(2,1)} %param.24) | copy-start | bytes 98308
  165.1 97.8 %all-to-all-start.1 = ((bf16[2,768,2048]{2,0,1:T(2,128)(2,1)}), bf16[2,768,2048]{2,0,1:T(2,128)(2,1)}, u32[]{:S(2)}, u32[]{:S(2)}) async-start(bf16[2,768,2048]{2,0,1:T(2,128)(2,1)} %copy.115), calls=%async_computation.1 | async-start | bytes 12582912 | tf_op jit(solution)/shard_map/all_to_all | solution.py:193
  179.0 113.8 %copy-start.33 = (pred[128,128]{1,0:T(8,128)(4,1)}, pred[128,128]{1,0:T(8,128)(4,1)S(1)}, u32[]{:S(2)}) copy-start(pred[128,128]{1,0:T(8,128)(4,1)S(1)} %get-tuple-element.83) | copy-start | bytes 49156
  269.7 1.8 copy-start.42
  271.0 9.9 %copy-start.30 = (bf16[128,2048]{1,0:T(8,128)(2,1)}, bf16[128,2048]{1,0:T(8,128)(2,1)S(1)}, u32[]{:S(2)}) copy-start(bf16[128,2048]{1,0:T(8,128)(2,1)S(1)} %get-tuple-element.54) | copy-start | bytes 1572868
  281.0 8.6 %collective-permute-start = (bf16[3,4096]{1,0:T(4,128)(2,1)S(1)}, bf16[3,4096]{1,0:T(4,128)(2,1)S(1)}, u32[]{:S(2)}, u32[]{:S(2)}) collective-permute-start(bf16[3,4096]{1,0:T(4,128)(2,1)S(1)} %slice.191), channel_id=1, source_target_pairs={{0,1},{1,2},{2,3},{3,4},{4,5},{5,6},{6,7},{7,8},{8,9},{9,10},{10,1... | collective-permute-start | bytes 73736 | tf_op jit(solution)/shard_map/ppermute | solution.py:10
  296.2 2.3 copy-start.23
  306.3 9.6 %copy-start.31 = (f32[1,2,2,2,2,2,16,2,2]{8,7,6,5,4,3,2,1,0:T(2,128)S(1)}, f32[1,2,2,2,2,2,16,2,2]{8,7,6,5,4,3,2,1,0:T(2,128)}, u32[]{:S(2)}) copy-start(f32[1,2,2,2,2,2,16,2,2]{8,7,6,5,4,3,2,1,0:T(2,128)} %copy.134) | copy-start | bytes 24580
  306.3 9.6 %copy-start.32 = (f32[1,2,2,2,2,2,16,2,2]{8,7,6,5,4,3,2,1,0:T(2,128)S(1)}, f32[1,2,2,2,2,2,16,2,2]{8,7,6,5,4,3,2,1,0:T(2,128)}, u32[]{:S(2)}) copy-start(f32[1,2,2,2,2,2,16,2,2]{8,7,6,5,4,3,2,1,0:T(2,128)} %copy.135) | copy-start | bytes 24580
  306.3 10.6 %copy-start.22 = (f32[1,2,2,2,16,8,8]{6,5,4,3,2,1,0:T(8,128)S(1)}, f32[1,2,2,2,16,8,8]{6,5,4,3,2,1,0:T(8,128)}, u32[]{:S(2)}) copy-start(f32[1,2,2,2,16,8,8]{6,5,4,3,2,1,0:T(8,128)} %copy-done.21) | copy-start | bytes 98308
  306.3 10.6 %copy-start.24 = (f32[1,2,2,2,16,8,8]{6,5,4,3,2,1,0:T(8,128)S(1)}, f32[1,2,2,2,16,8,8]{6,5,4,3,2,1,0:T(8,128)}, u32[]{:S(2)}) copy-start(f32[1,2,2,2,16,8,8]{6,5,4,3,2,1,0:T(8,128)} %copy-done.23) | copy-start | bytes 98308
  318.8 2.4 copy-start.18
  318.8 2.4 copy-start.20
  330.9 10.9 %copy-start.41 = (f32[16]{0:T(128)S(1)}, f32[16]{0:T(128)}, u32[]{:S(2)}) copy-start(f32[16]{0:T(128)} %slice_reduce_fusion.1) | copy-start | bytes 196
  332.8 19.4 %collective-permute-start.7 = (bf16[16,128,128]{2,1,0:T(8,128)(2,1)S(1)}, bf16[16,128,128]{2,1,0:T(8,128)(2,1)S(1)}, u32[]{:S(2)}, u32[]{:S(2)}) collective-permute-start(bf16[16,128,128]{2,1,0:T(8,128)(2,1)S(1)} %get-tuple-element.55), channel_id=1, source_target_pairs={{0,1},{1,2},{2,3},{3,4},{4,5},{5,6},{6,7},{7,8},{8,9},{9,10},{10,1... | collective-permute-start | bytes 1572872 | tf_op jit(solution)/shard_map/ppermute | solution.py:115
  344.6 7.7 %copy-start.6 = (f32[16,128,128]{2,1,0:T(8,128)}, f32[16,128,128]{2,1,0:T(8,128)S(1)}, u32[]{:S(2)}) copy-start(f32[16,128,128]{2,1,0:T(8,128)S(1)} %get-tuple-element.58) | copy-start | bytes 3145732
  344.6 19.0 %collective-permute-start.1 = (bf16[16,128,128]{2,1,0:T(8,128)(2,1)}, bf16[16,128,128]{2,1,0:T(8,128)(2,1)}, u32[]{:S(2)}, u32[]{:S(2)}) collective-permute-start(bf16[16,128,128]{2,1,0:T(8,128)(2,1)} %get-tuple-element.57), channel_id=1, source_target_pairs={{0,1},{1,2},{2,3},{3,4},{4,5},{5,6},{6,7},{7,8},{8,9},{9,10},{10,1... | collective-permute-start | bytes 1572872 | tf_op jit(solution)/shard_map/ppermute | solution.py:115
  354.2 20.6 %collective-permute-start.8 = (bf16[16,128,128]{2,1,0:T(8,128)(2,1)}, bf16[16,128,128]{2,1,0:T(8,128)(2,1)}, u32[]{:S(2)}, u32[]{:S(2)}) collective-permute-start(bf16[16,128,128]{2,1,0:T(8,128)(2,1)} %get-tuple-element.59), channel_id=1, source_target_pairs={{0,2},{1,3},{2,4},{3,5},{4,6},{5,7},{6,8},{7,9},{8,10},{9,11},{10,... | collective-permute-start | bytes 1572872 | tf_op jit(solution)/shard_map/ppermute | solution.py:115
  360.4 14.4 %copy-start.26 = (f32[16,128,128]{2,1,0:T(8,128)S(1)}, f32[16,128,128]{2,1,0:T(8,128)}, u32[]{:S(2)}) copy-start(f32[16,128,128]{2,1,0:T(8,128)} %get-tuple-element.60) | copy-start | bytes 3145732
  366.8 8.1 %copy-start.3 = (f32[16,128,128]{2,1,0:T(8,128)}, f32[16,128,128]{2,1,0:T(8,128)S(1)}, u32[]{:S(2)}) copy-start(f32[16,128,128]{2,1,0:T(8,128)S(1)} %get-tuple-element.62) | copy-start | bytes 3145732
  366.8 20.6 %collective-permute-start.2 = (bf16[16,128,128]{2,1,0:T(8,128)(2,1)}, bf16[16,128,128]{2,1,0:T(8,128)(2,1)}, u32[]{:S(2)}, u32[]{:S(2)}) collective-permute-start(bf16[16,128,128]{2,1,0:T(8,128)(2,1)} %get-tuple-element.61), channel_id=1, source_target_pairs={{0,2},{1,3},{2,4},{3,5},{4,6},{5,7},{6,8},{7,9},{8,10},{9,11},{10,... | collective-permute-start | bytes 1572872 | tf_op jit(solution)/shard_map/ppermute | solution.py:115
  377.8 30.2 %collective-permute-start.9 = (bf16[16,128,128]{2,1,0:T(8,128)(2,1)}, bf16[16,128,128]{2,1,0:T(8,128)(2,1)}, u32[]{:S(2)}, u32[]{:S(2)}) collective-permute-start(bf16[16,128,128]{2,1,0:T(8,128)(2,1)} %get-tuple-element.63), channel_id=1, source_target_pairs={{0,4},{1,5},{2,6},{3,7},{4,8},{5,9},{6,10},{7,11},{8,12},{9,13},{1... | collective-permute-start | bytes 1572872 | tf_op jit(solution)/shard_map/ppermute | solution.py:115
  387.4 20.6 %copy-start.27 = (f32[16,128,128]{2,1,0:T(8,128)S(1)}, f32[16,128,128]{2,1,0:T(8,128)}, u32[]{:S(2)}) copy-start(f32[16,128,128]{2,1,0:T(8,128)} %get-tuple-element.64) | copy-start | bytes 3145732
  390.6 17.3 %copy-start.4 = (f32[16,128,128]{2,1,0:T(8,128)}, f32[16,128,128]{2,1,0:T(8,128)S(1)}, u32[]{:S(2)}) copy-start(f32[16,128,128]{2,1,0:T(8,128)S(1)} %get-tuple-element.66) | copy-start | bytes 3145732
  390.7 37.1 %collective-permute-start.3 = (bf16[16,128,128]{2,1,0:T(8,128)(2,1)}, bf16[16,128,128]{2,1,0:T(8,128)(2,1)}, u32[]{:S(2)}, u32[]{:S(2)}) collective-permute-start(bf16[16,128,128]{2,1,0:T(8,128)(2,1)} %get-tuple-element.65), channel_id=1, source_target_pairs={{0,4},{1,5},{2,6},{3,7},{4,8},{5,9},{6,10},{7,11},{8,12},{9,13},{1... | collective-permute-start | bytes 1572872 | tf_op jit(solution)/shard_map/ppermute | solution.py:115
  410.9 22.0 %collective-permute-start.10 = (bf16[16,128,128]{2,1,0:T(8,128)(2,1)}, bf16[16,128,128]{2,1,0:T(8,128)(2,1)}, u32[]{:S(2)}, u32[]{:S(2)}) collective-permute-start(bf16[16,128,128]{2,1,0:T(8,128)(2,1)} %get-tuple-element.67), channel_id=1, source_target_pairs={{0,8},{1,9},{2,10},{3,11},{4,12},{5,13},{6,14},{7,15},{8,16},{9,17... | collective-permute-start | bytes 1572872 | tf_op jit(solution)/shard_map/ppermute | solution.py:115
  412.8 20.1 %copy-start.28 = (f32[16,128,128]{2,1,0:T(8,128)S(1)}, f32[16,128,128]{2,1,0:T(8,128)}, u32[]{:S(2)}) copy-start(f32[16,128,128]{2,1,0:T(8,128)} %get-tuple-element.68) | copy-start | bytes 3145732
  431.0 1.9 copy-start.5
  431.0 17.2 %collective-permute-start.4 = (bf16[16,128,128]{2,1,0:T(8,128)(2,1)}, bf16[16,128,128]{2,1,0:T(8,128)(2,1)}, u32[]{:S(2)}, u32[]{:S(2)}) collective-permute-start(bf16[16,128,128]{2,1,0:T(8,128)(2,1)} %get-tuple-element.69), channel_id=1, source_target_pairs={{0,8},{1,9},{2,10},{3,11},{4,12},{5,13},{6,14},{7,15},{8,16},{9,17... | collective-permute-start | bytes 1572872 | tf_op jit(solution)/shard_map/ppermute | solution.py:115
  435.8 20.0 %collective-permute-start.11 = (bf16[16,128,128]{2,1,0:T(8,128)(2,1)}, bf16[16,128,128]{2,1,0:T(8,128)(2,1)}, u32[]{:S(2)}, u32[]{:S(2)}) collective-permute-start(bf16[16,128,128]{2,1,0:T(8,128)(2,1)} %get-tuple-element.71), channel_id=1, source_target_pairs={{0,16},{1,17},{2,18},{3,19},{4,20},{5,21},{6,22},{7,23},{8,24},{9,... | collective-permute-start | bytes 1572872 | tf_op jit(solution)/shard_map/ppermute | solution.py:115
  439.4 16.4 %copy-start.29 = (f32[16,128,128]{2,1,0:T(8,128)S(1)}, f32[16,128,128]{2,1,0:T(8,128)}, u32[]{:S(2)}) copy-start(f32[16,128,128]{2,1,0:T(8,128)} %get-tuple-element.72) | copy-start | bytes 3145732
  451.3 4.5 copy-start.2
  451.3 11.0 %collective-permute-start.5 = (bf16[16,128,128]{2,1,0:T(8,128)(2,1)}, bf16[16,128,128]{2,1,0:T(8,128)(2,1)}, u32[]{:S(2)}, u32[]{:S(2)}) collective-permute-start(bf16[16,128,128]{2,1,0:T(8,128)(2,1)} %get-tuple-element.73), channel_id=1, source_target_pairs={{0,16},{1,17},{2,18},{3,19},{4,20},{5,21},{6,22},{7,23},{8,24},{9,... | collective-permute-start | bytes 1572872 | tf_op jit(solution)/shard_map/ppermute | solution.py:115
  458.8 14.8 %collective-permute-start.12 = (bf16[16,128,128]{2,1,0:T(8,128)(2,1)}, bf16[16,128,128]{2,1,0:T(8,128)(2,1)}, u32[]{:S(2)}, u32[]{:S(2)}) collective-permute-start(bf16[16,128,128]{2,1,0:T(8,128)(2,1)} %get-tuple-element.75), channel_id=1, source_target_pairs={{0,32},{1,33},{2,34},{3,35},{4,36},{5,37},{6,38},{7,39},{8,40},{9,... | collective-permute-start | bytes 1572872 | tf_op jit(solution)/shard_map/ppermute | solution.py:115
  460.9 12.7 %copy-start.25 = (f32[16,128,128]{2,1,0:T(8,128)S(1)}, f32[16,128,128]{2,1,0:T(8,128)}, u32[]{:S(2)}) copy-start(f32[16,128,128]{2,1,0:T(8,128)} %get-tuple-element.76) | copy-start | bytes 3145732
  464.7 20.1 %collective-permute-start.6 = (bf16[16,128,128]{2,1,0:T(8,128)(2,1)S(1)}, bf16[16,128,128]{2,1,0:T(8,128)(2,1)S(1)}, u32[]{:S(2)}, u32[]{:S(2)}) collective-permute-start(bf16[16,128,128]{2,1,0:T(8,128)(2,1)S(1)} %get-tuple-element.77), channel_id=1, source_target_pairs={{0,32},{1,33},{2,34},{3,35},{4,36},{5,37},{6,38},{7,39},{8,40},{9,... | collective-permute-start | bytes 1572872 | tf_op jit(solution)/shard_map/ppermute | solution.py:115
  475.4 20.6 %collective-permute-start.13 = (bf16[16,128,128]{2,1,0:T(8,128)(2,1)S(1)}, bf16[16,128,128]{2,1,0:T(8,128)(2,1)S(1)}, u32[]{:S(2)}, u32[]{:S(2)}) collective-permute-start(bf16[16,128,128]{2,1,0:T(8,128)(2,1)S(1)} %get-tuple-element.79), channel_id=1, source_target_pairs={{0,64},{1,65},{2,66},{3,67},{4,68},{5,69},{6,70},{7,71},{8,72},{9,... | collective-permute-start | bytes 1572872 | tf_op jit(solution)/shard_map/ppermute | solution.py:115
  495.9 3.3 copy-start.34
  496.7 15.8 %collective-permute-start.14 = (bf16[16,128,128]{2,1,0:T(8,128)(2,1)S(1)}, bf16[16,128,128]{2,1,0:T(8,128)(2,1)S(1)}, u32[]{:S(2)}, u32[]{:S(2)}) collective-permute-start(bf16[16,128,128]{2,1,0:T(8,128)(2,1)S(1)} %fusion.20), channel_id=1, source_target_pairs={{0,1},{1,2},{2,3},{3,4},{4,5},{5,6},{6,7},{7,8},{8,9},{9,10},{10,1... | collective-permute-start | bytes 1572872 | tf_op jit(solution)/shard_map/ppermute | solution.py:115
  501.6 13.4 %copy-start.37 = (f32[128,16]{0,1:T(8,128)S(1)}, f32[128,16]{0,1:T(8,128)}, u32[]{:S(2)}) copy-start(f32[128,16]{0,1:T(8,128)} %get-tuple-element.49) | copy-start | bytes 24580
  513.1 3.2 copy-start.43
  515.0 2.5 copy-start.1
  (15 other events, 17.9 us)
Sparse Core Ops, SparseCore 0:
  10.1 222.4 all-gather.1

commit v3 on v2

--- a/solution.py
+++ b/solution.py
@@ -74,11 +74,11 @@
 
 
 def run_experts(piece, gate_weight, up_weight, down_weight):
-    gate = jnp.einsum("esd,edf->esf", piece, gate_weight, preferred_element_type=jnp.float32)
-    upper = jnp.einsum("esd,edf->esf", piece, up_weight, preferred_element_type=jnp.float32)
+    gate = jnp.einsum("sed,edf->esf", piece, gate_weight, preferred_element_type=jnp.float32)
+    upper = jnp.einsum("sed,edf->esf", piece, up_weight, preferred_element_type=jnp.float32)
     hidden = (jax.nn.silu(gate) * upper).astype(jnp.bfloat16)
     return jnp.einsum(
-        "esf,efd->esd", hidden, down_weight, preferred_element_type=jnp.float32
+        "esf,efd->sed", hidden, down_weight, preferred_element_type=jnp.float32
     ).astype(jnp.bfloat16)
 
 
@@ -119,20 +119,24 @@
     place = lax.axis_index(axes)
     steps = 1
     while steps < count:
-        last = steps * 2 >= count
-        far_state = shifted_linear(state_increment.astype(jnp.bfloat16), axes, count, steps)
         reached = place >= steps
+        if steps * 2 >= count:
+            far_state = shifted_linear(state_increment.astype(jnp.bfloat16), axes, count, steps)
+        else:
+            far = shifted_linear(
+                jnp.stack([state_map, state_increment]).astype(jnp.bfloat16), axes, count, steps
+            ).astype(jnp.float32)
+            far_state = far[1]
+            joined_map = jnp.einsum(
+                "hij,hjk->hik", state_map, far[0], precision=lax.Precision.HIGHEST
+            )
         joined_state = (
             jnp.einsum(
                 "hij,hjv->hiv", state_map, far_state.astype(jnp.float32), precision=lax.Precision.HIGHEST
             )
             + state_increment
         )
-        if not last:
-            far_map = shifted_linear(state_map.astype(jnp.bfloat16), axes, count, steps)
-            joined_map = jnp.einsum(
-                "hij,hjk->hik", state_map, far_map.astype(jnp.float32), precision=lax.Precision.HIGHEST
-            )
+        if steps * 2 < count:
             state_map = jnp.where(reached, joined_map, state_map)
         state_increment = jnp.where(reached, joined_state, state_increment)
         steps *= 2
@@ -166,31 +170,28 @@
     normed_first = rms_scale(tokens_in, first_gain).astype(jnp.bfloat16)
     mix_weight = route_weight / jnp.sum(route_weight, axis=1, keepdims=True)
     flat_ids = expert_ids
-    target = (
-        flat_ids % local_experts * (n_dev * capacity)
-        + flat_ids // local_experts * capacity
-    )
+    target = flat_ids // local_experts * (capacity * local_experts) + flat_ids % local_experts
     onehot = (flat_ids[:, :, None] == jnp.arange(experts_all, dtype=jnp.int32)[None, None, :]).astype(
         jnp.int32
     )
     counted = jnp.sum(onehot, axis=1)
     before = jnp.cumsum(counted, axis=0) - counted
     slot_index = jnp.sum(before[:, None, :] * onehot, axis=2)
-    target = target + slot_index
+    target = target + slot_index * local_experts
     slots = jnp.arange(n_dev * local_experts * capacity, dtype=jnp.int32)
     hits = target[:, :, None] == slots[None, None, :]
     dispatch = jnp.any(hits, axis=1).astype(jnp.bfloat16)
     outgoing = jnp.einsum(
         "ts,td->sd", dispatch, normed_first, preferred_element_type=jnp.float32
     ).astype(jnp.bfloat16)
-    outgoing = outgoing.reshape(local_experts, n_dev * capacity, width)
+    outgoing = outgoing.reshape(n_dev * capacity, local_experts, width)
     served = run_experts(
-        lax.all_to_all(outgoing, ("outer", "inner"), split_axis=1, concat_axis=1, tiled=True),
+        lax.all_to_all(outgoing, ("outer", "inner"), split_axis=0, concat_axis=0, tiled=True),
         gate_weight,
         up_weight,
         down_weight,
     )
-    returned = lax.all_to_all(served, ("outer", "inner"), split_axis=1, concat_axis=1, tiled=True)
+    returned = lax.all_to_all(served, ("outer", "inner"), split_axis=0, concat_axis=0, tiled=True)
     returned = returned.reshape(-1, width)
     combine = jnp.sum(jnp.where(hits, mix_weight[:, :, None], 0.0), axis=1)
     combine_hi = combine.astype(jnp.bfloat16)

time: 530 us -> 583 us (1.10)
  the two profiles are of different devices: /device:TPU:1 before, /device:TPU:96 now
where the time goes in v3:
time: 583 us; the launch traced here: 577 us
  waiting for transfers between devices  249 us (43%)
  matrix products  97.6 us (17%)
  blocking collectives  88.5 us (15%)
  local copies, waits for them, and re-layouts  56.3 us (10%)
  starting transfers between devices  49.7 us (9%)
  other arithmetic  19.9 us (3%)
  between operations  15.7 us (3%)
    ppermute x8, waiting for transfers between devices, shifted_linear(): lax.ppermute(value, axes, [(source, source + steps) for source in range(c...  170 us
    all_to_all x1, blocking collectives, per_device(): lax.all_to_all(outgoing, ('outer', 'inner'), split_axis=0, concat_axis=0,...  88.5 us
    all_to_all x1, waiting for transfers between devices, per_device(): lax.all_to_all(served, ('outer', 'inner'), split_axis=0, concat_axis=0, t...  74.4 us
    all_to_all x1, starting transfers between devices, per_device(): lax.all_to_all(served, ('outer', 'inner'), split_axis=0, concat_axis=0, t...  29.6 us
    dot_general x1, matrix products, run_experts(): jnp.einsum('esf,efd->sed', hidden, down_weight, preferred_element_type=jn...  16.5 us
    unnamed x124, local copies, waits for them, and re-layouts  16.2 us
    ppermute x8, starting transfers between devices, shifted_linear(): lax.ppermute(value, axes, [(source, source + steps) for source in range(c...  14.7 us
    convert_element_type x1, local copies, waits for them, and re-layouts, run_experts(): return jnp.einsum('esf,efd->sed', hidden, down_weight, preferred_element_...  12.7 us
  transfers between devices with their start and end apart: 11, of which 10 were waited for; matrix products, arithmetic and copies ran while one was open for 14% of the time, Pallas kernels for 0%

profile of v3, /device:TPU:96, one launch (start us, length us, event | category | flops | bytes accessed | tf_op | source)
XLA Modules:
  0.0 576.9 jit_solution(4008753593729868606)
XLA Ops:
  13.5 5.6 convolution_convert_fusion
  19.1 11.1 %reshape.128 = bf16[768,2,2048]{2,1,0:T(2,128)(2,1)} reshape(bf16[1536,2048]{1,0:T(8,128)(2,1)} %convolution_convert_fusion) | data formatting | bytes 12582912 | tf_op jit(solution)/shard_map/reshape | solution.py:187
  30.1 88.5 %all_to_all.10 = bf16[768,2,2048]{2,1,0:T(2,128)(2,1)S(1)} all-to-all(bf16[768,2,2048]{2,1,0:T(2,128)(2,1)} %reshape.128), channel_id=1, replica_groups=mesh['outer'=8,'inner'=16] {'outer','inner'}, dimensions={0} | all-to-all | bytes 12582912 | tf_op jit(solution)/shard_map/all_to_all | solution.py:189
  118.6 2.7 copy-done.23
  121.3 5.3 fusion.3
  126.7 16.5 %convert_bitcast_fusion = bf16[768,2,2048]{2,0,1:T(8,128)(2,1)} fusion(bf16[2,512,2048]{2,1,0:T(8,128)(2,1)} %param.20, f32[2,768,512]{2,1,0:T(8,128)} %fusion.3, bf16[2,2048,512]{2,1,0:T(8,128)(2,1)} %param.19, bf16[768,2,2048]{2,1,0:T(2,128)(2,1)} %copy-done.23), kind=kOutput, calls=%fused_computation.4 | convolution fusion | flops 6450315264 | bytes 24117248 | tf_op jit(solution)/shard_map/esf,efd->sed/dot_general | solution.py:80
  143.2 12.7 %copy.88 = bf16[768,2,2048]{2,1,0:T(2,128)(2,1)} copy(bf16[768,2,2048]{2,0,1:T(8,128)(2,1)} %convert_bitcast_fusion) | data formatting | bytes 12582912 | tf_op jit(solution)/shard_map/convert_element_type | solution.py:82
  155.9 29.6 %all-to-all-start.1 = ((bf16[768,2,2048]{2,1,0:T(2,128)(2,1)}), bf16[768,2,2048]{2,1,0:T(2,128)(2,1)}, u32[]{:S(2)}, u32[]{:S(2)}) async-start(bf16[768,2,2048]{2,1,0:T(2,128)(2,1)} %copy.88), calls=%async_computation.1 | async-start | bytes 12582912 | tf_op jit(solution)/shard_map/all_to_all | solution.py:194
  186.9 74.4 %all-to-all-done.1 = bf16[768,2,2048]{2,1,0:T(2,128)(2,1)} async-done(((bf16[768,2,2048]{2,1,0:T(2,128)(2,1)}), bf16[768,2,2048]{2,1,0:T(2,128)(2,1)}, u32[]{:S(2)}, u32[]{:S(2)}) %all-to-all-start.1) | async-done | bytes 6291488 | tf_op jit(solution)/shard_map/all_to_all | solution.py:194
  261.3 10.2 %reshape.129 = bf16[1536,2048]{1,0:T(8,128)(2,1)} reshape(bf16[768,2,2048]{2,1,0:T(2,128)(2,1)} %all-to-all-done.1) | data formatting | bytes 12582912 | tf_op jit(solution)/shard_map/reshape | solution.py:195
  271.5 3.9 fusion.63
  279.2 8.2 %convolution_convert_fusion.1 = bf16[128,4096]{1,0:T(8,128)(2,1)S(1)} fusion(bf16[2048,4096]{1,0:T(8,128)(2,1)} %all-gather.2.cloned.1.call-done, bf16[128,2048]{1,0:T(8,128)(2,1)S(1)} %get-tuple-element.52, f32[2048]{0:T(1024)S(1)} %copy-done.49, f32[128]{0:T(128)S(1)} %add_rsqrt_fusion.3), kind=kOutput, calls=%fused_computation.9 | convolution fusion | flops 2149056512 | bytes 18358784 | tf_op jit(solution)/shard_map/dot_general | solution.py:204
  287.5 5.3 collective-permute-start
  293.5 3.6 collective-permute-done
  301.0 2.4 fusion.17
  314.9 4.8 fusion.93
  319.7 5.0 convolution_negate_fusion.5
  325.6 1.9 fusion.56
  327.7 1.8 convolution_negate_fusion.4
  340.7 2.0 convolution_subtract_fusion.1
  342.9 1.9 fusion.100
  345.9 1.9 collective-permute-start.1
  347.8 29.0 %collective-permute-done.1 = bf16[2,16,128,128]{3,2,1,0:T(8,128)(2,1)} collective-permute-done((bf16[2,16,128,128]{3,2,1,0:T(8,128)(2,1)S(1)}, bf16[2,16,128,128]{3,2,1,0:T(8,128)(2,1)}, u32[]{:S(2)}, u32[]{:S(2)}) %collective-permute-start.1) | collective-permute-done | bytes 1048608 | tf_op jit(solution)/shard_map/ppermute | solution.py:115
  376.8 1.7 convolution_select_fusion.5
  378.6 1.7 add_select_fusion.6
  381.5 2.1 collective-permute-start.2
  383.6 28.5 %collective-permute-done.2 = bf16[2,16,128,128]{3,2,1,0:T(8,128)(2,1)} collective-permute-done((bf16[2,16,128,128]{3,2,1,0:T(8,128)(2,1)S(1)}, bf16[2,16,128,128]{3,2,1,0:T(8,128)(2,1)}, u32[]{:S(2)}, u32[]{:S(2)}) %collective-permute-start.2) | collective-permute-done | bytes 1048608 | tf_op jit(solution)/shard_map/ppermute | solution.py:115
  412.1 1.7 convolution_select_fusion.4
  413.9 1.7 add_select_fusion.5
  416.8 1.9 collective-permute-start.3
  418.7 25.7 %collective-permute-done.3 = bf16[2,16,128,128]{3,2,1,0:T(8,128)(2,1)} collective-permute-done((bf16[2,16,128,128]{3,2,1,0:T(8,128)(2,1)S(1)}, bf16[2,16,128,128]{3,2,1,0:T(8,128)(2,1)}, u32[]{:S(2)}, u32[]{:S(2)}) %collective-permute-start.3) | collective-permute-done | bytes 1048608 | tf_op jit(solution)/shard_map/ppermute | solution.py:115
  446.2 1.7 add_select_fusion.4
  449.0 1.9 collective-permute-start.4
  451.0 25.3 %collective-permute-done.4 = bf16[2,16,128,128]{3,2,1,0:T(8,128)(2,1)} collective-permute-done((bf16[2,16,128,128]{3,2,1,0:T(8,128)(2,1)S(1)}, bf16[2,16,128,128]{3,2,1,0:T(8,128)(2,1)}, u32[]{:S(2)}, u32[]{:S(2)}) %collective-permute-start.4) | collective-permute-done | bytes 1048608 | tf_op jit(solution)/shard_map/ppermute | solution.py:115
  476.3 1.7 convolution_select_fusion.2
  478.0 1.9 add_select_fusion.3
  481.3 2.0 collective-permute-start.5
  483.4 14.5 %collective-permute-done.5 = bf16[2,16,128,128]{3,2,1,0:T(8,128)(2,1)} collective-permute-done((bf16[2,16,128,128]{3,2,1,0:T(8,128)(2,1)}, bf16[2,16,128,128]{3,2,1,0:T(8,128)(2,1)}, u32[]{:S(2)}, u32[]{:S(2)}) %collective-permute-start.5) | collective-permute-done | bytes 1048608 | tf_op jit(solution)/shard_map/ppermute | solution.py:115
  497.9 2.3 convolution_select_fusion.1
  500.3 1.7 add_select_fusion.2
  506.6 22.8 %collective-permute-done.6 = bf16[2,16,128,128]{3,2,1,0:T(8,128)(2,1)} collective-permute-done((bf16[2,16,128,128]{3,2,1,0:T(8,128)(2,1)}, bf16[2,16,128,128]{3,2,1,0:T(8,128)(2,1)}, u32[]{:S(2)}, u32[]{:S(2)}) %collective-permute-start.6) | collective-permute-done | bytes 1048608 | tf_op jit(solution)/shard_map/ppermute | solution.py:115
  529.4 1.7 fusion.99
  532.7 1.7 convolution_select_fusion
  534.4 12.4 %collective-permute-done.7 = bf16[16,128,128]{2,1,0:T(8,128)(2,1)S(1)} collective-permute-done((bf16[16,128,128]{2,1,0:T(8,128)(2,1)S(1)}, bf16[16,128,128]{2,1,0:T(8,128)(2,1)S(1)}, u32[]{:S(2)}, u32[]{:S(2)}) %collective-permute-start.7) | collective-permute-done | bytes 524320 | tf_op jit(solution)/shard_map/ppermute | solution.py:115
  547.5 2.2 collective-permute-start.8
  550.1 2.3 convolution_multiply_fusion
  552.5 12.2 %collective-permute-done.8 = bf16[16,128,128]{2,1,0:T(8,128)(2,1)S(1)} collective-permute-done((bf16[16,128,128]{2,1,0:T(8,128)(2,1)S(1)}, bf16[16,128,128]{2,1,0:T(8,128)(2,1)S(1)}, u32[]{:S(2)}, u32[]{:S(2)}) %collective-permute-start.8) | collective-permute-done | bytes 524320 | tf_op jit(solution)/shard_map/ppermute | solution.py:115
  565.4 1.9 convolution_bitcast_fusion
  (221 shorter events, 57.5 us)
Async XLA Ops:
  7.2 270.4 %copy-start = (bf16[2048,32]{0,1:T(8,128)(2,1)S(1)}, bf16[2048,32]{0,1:T(8,128)(2,1)}, u32[]{:S(2)}) copy-start(bf16[2048,32]{0,1:T(8,128)(2,1)} %param.23) | copy-start | bytes 393220
  7.2 272.1 %all-gather.2.cloned.1.call-start = ((), (), s32[]{:S(2)}) async-start(), calls=%async_computation.2 | async-start | bytes 17825792 | tf_op jit(solution)/shard_map/all_gather | solution.py:206
  30.1 91.2 %copy-start.57 = (bf16[2,2048,512]{2,1,0:T(8,128)(2,1)S(1)}, bf16[2,2048,512]{2,1,0:T(8,128)(2,1)}, u32[]{:S(2)}) copy-start(bf16[2,2048,512]{2,1,0:T(8,128)(2,1)} %param.18) | copy-start | bytes 12582916
  118.6 2.7 copy-start.23
  155.9 29.7 %copy-start.53 = (f32[128,10]{0,1:T(8,128)S(1)}, f32[128,10]{0,1:T(8,128)}, u32[]{:S(2)}) copy-start(f32[128,10]{0,1:T(8,128)} %param.16) | copy-start | bytes 15364
  155.9 29.8 %copy-start.58 = (f32[16]{0:T(128)S(1)}, f32[16]{0:T(128)}, u32[]{:S(2)}) copy-start(f32[16]{0:T(128)} %param.25) | copy-start | bytes 196
  155.9 31.0 %copy-start.48 = (bf16[4,4096]{1,0:T(4,128)(2,1)S(1)}, bf16[4,4096]{1,0:T(4,128)(2,1)}, u32[]{:S(2)}) copy-start(bf16[4,4096]{1,0:T(4,128)(2,1)} %param.24) | copy-start | bytes 98308
  155.9 105.5 %all-to-all-start.1 = ((bf16[768,2,2048]{2,1,0:T(2,128)(2,1)}), bf16[768,2,2048]{2,1,0:T(2,128)(2,1)}, u32[]{:S(2)}, u32[]{:S(2)}) async-start(bf16[768,2,2048]{2,1,0:T(2,128)(2,1)} %copy.88), calls=%async_computation.1 | async-start | bytes 12582912 | tf_op jit(solution)/shard_map/all_to_all | solution.py:194
  185.6 115.4 %copy-start.46 = (pred[128,128]{1,0:T(8,128)(4,1)}, pred[128,128]{1,0:T(8,128)(4,1)S(1)}, u32[]{:S(2)}) copy-start(pred[128,128]{1,0:T(8,128)(4,1)S(1)} %get-tuple-element.57) | copy-start | bytes 49156
  271.5 4.6 copy-start.2
  271.5 4.7 copy-start.24
  276.2 1.8 copy-start.55
  277.6 9.9 %copy-start.43 = (bf16[128,2048]{1,0:T(8,128)(2,1)}, bf16[128,2048]{1,0:T(8,128)(2,1)S(1)}, u32[]{:S(2)}) copy-start(bf16[128,2048]{1,0:T(8,128)(2,1)S(1)} %get-tuple-element.52) | copy-start | bytes 1572868
  287.5 9.6 %collective-permute-start = (bf16[3,4096]{1,0:T(4,128)(2,1)S(1)}, bf16[3,4096]{1,0:T(4,128)(2,1)S(1)}, u32[]{:S(2)}, u32[]{:S(2)}) collective-permute-start(bf16[3,4096]{1,0:T(4,128)(2,1)S(1)} %slice.239), channel_id=1, source_target_pairs={{0,1},{1,2},{2,3},{3,4},{4,5},{5,6},{6,7},{7,8},{8,9},{9,10},{10,1... | collective-permute-start | bytes 73736 | tf_op jit(solution)/shard_map/ppermute | solution.py:10
  304.8 2.2 copy-start.41
  314.8 9.8 %copy-start.44 = (f32[1,2,2,2,2,2,16,2,2]{8,7,6,5,4,3,2,1,0:T(2,128)S(1)}, f32[1,2,2,2,2,2,16,2,2]{8,7,6,5,4,3,2,1,0:T(2,128)}, u32[]{:S(2)}) copy-start(f32[1,2,2,2,2,2,16,2,2]{8,7,6,5,4,3,2,1,0:T(2,128)} %copy.106) | copy-start | bytes 24580
  314.8 9.8 %copy-start.45 = (f32[1,2,2,2,2,2,16,2,2]{8,7,6,5,4,3,2,1,0:T(2,128)S(1)}, f32[1,2,2,2,2,2,16,2,2]{8,7,6,5,4,3,2,1,0:T(2,128)}, u32[]{:S(2)}) copy-start(f32[1,2,2,2,2,2,16,2,2]{8,7,6,5,4,3,2,1,0:T(2,128)} %copy.107) | copy-start | bytes 24580
  314.8 10.8 %copy-start.40 = (f32[1,2,2,2,16,8,8]{6,5,4,3,2,1,0:T(8,128)S(1)}, f32[1,2,2,2,16,8,8]{6,5,4,3,2,1,0:T(8,128)}, u32[]{:S(2)}) copy-start(f32[1,2,2,2,16,8,8]{6,5,4,3,2,1,0:T(8,128)} %copy-done.39) | copy-start | bytes 98308
  314.8 10.8 %copy-start.42 = (f32[1,2,2,2,16,8,8]{6,5,4,3,2,1,0:T(8,128)S(1)}, f32[1,2,2,2,16,8,8]{6,5,4,3,2,1,0:T(8,128)}, u32[]{:S(2)}) copy-start(f32[1,2,2,2,16,8,8]{6,5,4,3,2,1,0:T(8,128)} %copy-done.41) | copy-start | bytes 98308
  327.5 2.4 copy-start.36
  327.6 2.4 copy-start.38
  336.0 1.5 copy-start.51
  336.0 1.5 copy-start.52
  338.1 2.6 copy-start.54
  339.4 3.5 copy-start.5
  340.7 4.1 copy-start.7
  345.9 31.0 %collective-permute-start.1 = (bf16[2,16,128,128]{3,2,1,0:T(8,128)(2,1)S(1)}, bf16[2,16,128,128]{3,2,1,0:T(8,128)(2,1)}, u32[]{:S(2)}, u32[]{:S(2)}) collective-permute-start(bf16[2,16,128,128]{3,2,1,0:T(8,128)(2,1)S(1)} %pad_maximum_fusion), channel_id=1, source_target_pairs={{0,1},{1,2},{2,3},{3,4},{4,5},{5,6},{6,7},{7,8},{8,9},{9,10},{10,1... | collective-permute-start | bytes 3145736 | tf_op jit(solution)/shard_map/ppermute | solution.py:115
  347.8 30.8 %copy-start.10 = (f32[16,128,128]{2,1,0:T(8,128)S(1)}, f32[16,128,128]{2,1,0:T(8,128)}, u32[]{:S(2)}) copy-start(f32[16,128,128]{2,1,0:T(8,128)} %copy-done.9) | copy-start | bytes 3145732
  381.5 30.7 %collective-permute-start.2 = (bf16[2,16,128,128]{3,2,1,0:T(8,128)(2,1)S(1)}, bf16[2,16,128,128]{3,2,1,0:T(8,128)(2,1)}, u32[]{:S(2)}, u32[]{:S(2)}) collective-permute-start(bf16[2,16,128,128]{3,2,1,0:T(8,128)(2,1)S(1)} %pad_maximum_fusion.1), channel_id=1, source_target_pairs={{0,2},{1,3},{2,4},{3,5},{4,6},{5,7},{6,8},{7,9},{8,10},{9,11},{10,... | collective-permute-start | bytes 3145736 | tf_op jit(solution)/shard_map/ppermute | solution.py:115
  383.6 30.3 %copy-start.14 = (f32[16,128,128]{2,1,0:T(8,128)S(1)}, f32[16,128,128]{2,1,0:T(8,128)}, u32[]{:S(2)}) copy-start(f32[16,128,128]{2,1,0:T(8,128)} %copy-done.13) | copy-start | bytes 3145732
  416.8 27.6 %collective-permute-start.3 = (bf16[2,16,128,128]{3,2,1,0:T(8,128)(2,1)S(1)}, bf16[2,16,128,128]{3,2,1,0:T(8,128)(2,1)}, u32[]{:S(2)}, u32[]{:S(2)}) collective-permute-start(bf16[2,16,128,128]{3,2,1,0:T(8,128)(2,1)S(1)} %pad_maximum_fusion.2), channel_id=1, source_target_pairs={{0,4},{1,5},{2,6},{3,7},{4,8},{5,9},{6,10},{7,11},{8,12},{9,13},{1... | collective-permute-start | bytes 3145736 | tf_op jit(solution)/shard_map/ppermute | solution.py:115
  418.7 27.5 %copy-start.16 = (f32[16,128,128]{2,1,0:T(8,128)S(1)}, f32[16,128,128]{2,1,0:T(8,128)}, u32[]{:S(2)}) copy-start(f32[16,128,128]{2,1,0:T(8,128)} %copy-done.15) | copy-start | bytes 3145732
  449.0 27.3 %collective-permute-start.4 = (bf16[2,16,128,128]{3,2,1,0:T(8,128)(2,1)S(1)}, bf16[2,16,128,128]{3,2,1,0:T(8,128)(2,1)}, u32[]{:S(2)}, u32[]{:S(2)}) collective-permute-start(bf16[2,16,128,128]{3,2,1,0:T(8,128)(2,1)S(1)} %pad_maximum_fusion.3), channel_id=1, source_target_pairs={{0,8},{1,9},{2,10},{3,11},{4,12},{5,13},{6,14},{7,15},{8,16},{9,17... | collective-permute-start | bytes 3145736 | tf_op jit(solution)/shard_map/ppermute | solution.py:115
  450.9 27.1 %copy-start.18 = (f32[16,128,128]{2,1,0:T(8,128)S(1)}, f32[16,128,128]{2,1,0:T(8,128)}, u32[]{:S(2)}) copy-start(f32[16,128,128]{2,1,0:T(8,128)} %copy-done.17) | copy-start | bytes 3145732
  477.9 2.2 copy-start.3
  481.3 19.0 %copy-start.4 = (f32[16,128,128]{2,1,0:T(8,128)S(1)}, f32[16,128,128]{2,1,0:T(8,128)}, u32[]{:S(2)}) copy-start(f32[16,128,128]{2,1,0:T(8,128)} %copy-done.3) | copy-start | bytes 3145732
  481.3 16.6 %collective-permute-start.5 = (bf16[2,16,128,128]{3,2,1,0:T(8,128)(2,1)}, bf16[2,16,128,128]{3,2,1,0:T(8,128)(2,1)}, u32[]{:S(2)}, u32[]{:S(2)}) collective-permute-start(bf16[2,16,128,128]{3,2,1,0:T(8,128)(2,1)} %pad_maximum_fusion.4), channel_id=1, source_target_pairs={{0,16},{1,17},{2,18},{3,19},{4,20},{5,21},{6,22},{7,23},{8,24},{9,... | collective-permute-start | bytes 3145736 | tf_op jit(solution)/shard_map/ppermute | solution.py:115
  483.4 16.9 %copy-start.20 = (f32[16,128,128]{2,1,0:T(8,128)S(1)}, f32[16,128,128]{2,1,0:T(8,128)}, u32[]{:S(2)}) copy-start(f32[16,128,128]{2,1,0:T(8,128)} %copy-done.19) | copy-start | bytes 3145732
  503.1 26.3 %copy-start.12 = (f32[16,128,128]{2,1,0:T(8,128)S(1)}, f32[16,128,128]{2,1,0:T(8,128)}, u32[]{:S(2)}) copy-start(f32[16,128,128]{2,1,0:T(8,128)} %copy-done.11) | copy-start | bytes 3145732
  504.2 25.2 %collective-permute-start.6 = (bf16[2,16,128,128]{3,2,1,0:T(8,128)(2,1)}, bf16[2,16,128,128]{3,2,1,0:T(8,128)(2,1)}, u32[]{:S(2)}, u32[]{:S(2)}) collective-permute-start(bf16[2,16,128,128]{3,2,1,0:T(8,128)(2,1)} %pad_maximum_fusion.5), channel_id=1, source_target_pairs={{0,32},{1,33},{2,34},{3,35},{4,36},{5,37},{6,38},{7,39},{8,40},{9,... | collective-permute-start | bytes 3145736 | tf_op jit(solution)/shard_map/ppermute | solution.py:115
  531.1 15.7 %collective-permute-start.7 = (bf16[16,128,128]{2,1,0:T(8,128)(2,1)S(1)}, bf16[16,128,128]{2,1,0:T(8,128)(2,1)S(1)}, u32[]{:S(2)}, u32[]{:S(2)}) collective-permute-start(bf16[16,128,128]{2,1,0:T(8,128)(2,1)S(1)} %get-tuple-element.53), channel_id=1, source_target_pairs={{0,64},{1,65},{2,66},{3,67},{4,68},{5,69},{6,70},{7,71},{8,72},{9,... | collective-permute-start | bytes 1572872 | tf_op jit(solution)/shard_map/ppermute | solution.py:115
  546.8 3.4 copy-start.47
  547.5 17.2 %collective-permute-start.8 = (bf16[16,128,128]{2,1,0:T(8,128)(2,1)S(1)}, bf16[16,128,128]{2,1,0:T(8,128)(2,1)S(1)}, u32[]{:S(2)}, u32[]{:S(2)}) collective-permute-start(bf16[16,128,128]{2,1,0:T(8,128)(2,1)S(1)} %fusion.20), channel_id=1, source_target_pairs={{0,1},{1,2},{2,3},{3,4},{4,5},{5,6},{6,7},{7,8},{8,9},{9,10},{10,1... | collective-permute-start | bytes 1572872 | tf_op jit(solution)/shard_map/ppermute | solution.py:115
  549.9 14.8 %copy-start.6 = (f32[16,128,128]{2,1,0:T(8,128)S(1)}, f32[16,128,128]{2,1,0:T(8,128)}, u32[]{:S(2)}) copy-start(f32[16,128,128]{2,1,0:T(8,128)} %copy-done.5) | copy-start | bytes 3145732
  549.9 14.8 %copy-start.8 = (f32[16,128,128]{2,1,0:T(8,128)S(1)}, f32[16,128,128]{2,1,0:T(8,128)}, u32[]{:S(2)}) copy-start(f32[16,128,128]{2,1,0:T(8,128)} %copy-done.7) | copy-start | bytes 3145732
  552.5 14.8 %copy-start.50 = (f32[128,16]{0,1:T(8,128)S(1)}, f32[128,16]{0,1:T(8,128)}, u32[]{:S(2)}) copy-start(f32[128,16]{0,1:T(8,128)} %get-tuple-element.47) | copy-start | bytes 24580
  565.4 3.2 copy-start.56
  567.3 2.5 copy-start.1
  (22 other events, 23.9 us)
Sparse Core Ops, SparseCore 0:
  10.1 184.9 all-gather.1

commit v4 on v1

--- a/solution.py
+++ b/solution.py
@@ -2,6 +2,9 @@
 import jax.numpy as jnp
 from jax import lax
 from jax.sharding import PartitionSpec as P
+from jax.experimental import pallas as pl
+from jax.experimental.pallas import tpu as pltpu
+import functools
 
 
 def shifted(value, axis, steps):
@@ -109,6 +112,109 @@
         + next_state
     )
     return (joined_map, joined_state)
+
+
+def shifted_linear(value, axes, count, steps):
+    return lax.ppermute(value, axes, [(source, source + steps) for source in range(count - steps)])
+
+
+def scan_kernel(count, axes, map_ref, state_ref, out_ref, own_map, own_state, send_map, send_state,
+                land_map, land_state, send_sems, recv_sems):
+    place = lax.axis_index(axes)
+    heads = map_ref.shape[0]
+    own_map[...] = map_ref[...]
+    own_state[...] = state_ref[...]
+    rounds = []
+    steps = 1
+    while steps < count:
+        rounds.append(steps)
+        steps *= 2
+    rounds.append(1)
+    total = len(rounds)
+
+    def target(steps):
+        other = place + steps
+        return (other // lax.axis_size(axes[1]), other % lax.axis_size(axes[1]))
+
+    for number, steps in enumerate(rounds):
+        with_map = number < total - 2
+        final = number == total - 1
+        send_state[number] = own_state[...].astype(jnp.bfloat16)
+        if with_map:
+            send_map[number] = own_map[...].astype(jnp.bfloat16)
+        copies = [
+            pltpu.make_async_remote_copy(
+                src_ref=send_state.at[number], dst_ref=land_state.at[number],
+                send_sem=send_sems.at[2 * number], recv_sem=recv_sems.at[2 * number],
+                device_id=target(steps), device_id_type=pl.DeviceIdType.MESH)
+        ]
+        if with_map:
+            copies.append(
+                pltpu.make_async_remote_copy(
+                    src_ref=send_map.at[number], dst_ref=land_map.at[number],
+                    send_sem=send_sems.at[2 * number + 1], recv_sem=recv_sems.at[2 * number + 1],
+                    device_id=target(steps), device_id_type=pl.DeviceIdType.MESH)
+            )
+
+        @pl.when(place + steps < count)
+        def _():
+            for copy in copies:
+                copy.start()
+
+        @pl.when(place >= steps)
+        def _():
+            for copy in copies:
+                copy.wait_recv()
+            if final:
+                out_ref[...] = land_state[number].astype(jnp.float32)
+            else:
+                def head(h, carry):
+                    mine = own_map[h]
+                    new_state = jnp.dot(mine, land_state[number, h].astype(jnp.float32),
+                                        preferred_element_type=jnp.float32,
+                                        precision=lax.Precision.HIGHEST) + own_state[h]
+                    if with_map:
+                        own_map[h] = jnp.dot(mine, land_map[number, h].astype(jnp.float32),
+                                             preferred_element_type=jnp.float32,
+                                             precision=lax.Precision.HIGHEST)
+                    own_state[h] = new_state
+                    return carry
+                lax.fori_loop(0, heads, head, 0)
+
+        if final:
+            @pl.when(place < steps)
+            def _():
+                out_ref[...] = jnp.zeros_like(out_ref)
+
+        @pl.when(place + steps < count)
+        def _():
+            for copy in copies:
+                copy.wait_send()
+
+
+def chained_state(state_map, state_increment, axes, count):
+    heads, size, width = state_increment.shape
+    rounds = 1
+    while (1 << (rounds - 1)) < count:
+        rounds += 1
+    block = pltpu.VMEM((rounds, heads, size, width), jnp.bfloat16)
+    return pl.pallas_call(
+        functools.partial(scan_kernel, count, axes),
+        out_shape=jax.ShapeDtypeStruct(state_increment.shape, jnp.float32),
+        in_specs=[pl.BlockSpec(memory_space=pltpu.VMEM)] * 2,
+        out_specs=pl.BlockSpec(memory_space=pltpu.VMEM),
+        scratch_shapes=[
+            pltpu.VMEM(state_map.shape, jnp.float32),
+            pltpu.VMEM(state_increment.shape, jnp.float32),
+            pltpu.VMEM((rounds, heads, size, size), jnp.bfloat16),
+            block,
+            pltpu.VMEM((rounds, heads, size, size), jnp.bfloat16),
+            block,
+            pltpu.SemaphoreType.DMA((2 * rounds,)),
+            pltpu.SemaphoreType.DMA((2 * rounds,)),
+        ],
+        compiler_params=pltpu.CompilerParams(has_side_effects=True, vmem_limit_bytes=48 * 1024 * 1024),
+    )(state_map, state_increment)
 
 
 def per_device(
@@ -239,13 +345,7 @@
     state_increment = jnp.einsum(
         "xbe,xbz->xez", trailing_keys, value_resolved, precision=lax.Precision.HIGHEST
     )
-    identity = (eye_heads, jnp.zeros_like(state_increment))
-    inner_pre = prefix_2((state_map, state_increment), "inner", join_maps, identity)
-    inclusive = join_maps(inner_pre, (state_map, state_increment))
-    group = spread_2(shortened(jnp.stack(inclusive)), "inner", n_inner - 1)
-    outer_pre = entering((group[0], group[1]), "outer", join_maps, identity)
-    prefix = join_maps(outer_pre, inner_pre)
-    initial_state = prefix[1]
+    initial_state = chained_state(state_map, state_increment, ("outer", "inner"), n_dev)
     updates = value_resolved - jnp.einsum(
         "mwx,mxd->mwd", key_resolved, initial_state, precision=lax.Precision.HIGHEST
     )

time: 731 us -> 573 us (0.78)
  the two profiles are of different devices: /device:TPU:83 before, /device:TPU:126 now
where the time goes in v4:
time: 573 us; the launch traced here: 568 us
  Pallas kernels  213 us (37%)
  blocking collectives  93.3 us (16%)
  waiting for transfers between devices  84.1 us (15%)
  matrix products  71.1 us (12%)
  local copies, waits for them, and re-layouts  55 us (10%)
  starting transfers between devices  19.8 us (3%)
  other arithmetic  16.2 us (3%)
  between operations  15.4 us (3%)
    pallas_call x1, Pallas kernels, chained_state(): pl.pallas_call(functools.partial(scan_kernel, count, axes), out_shape=jax...  213 us
    all_to_all x1, blocking collectives, per_device(): lax.all_to_all(outgoing, ('outer', 'inner'), split_axis=1, concat_axis=1,...  93.3 us
    all_to_all x1, waiting for transfers between devices, per_device(): lax.all_to_all(served, ('outer', 'inner'), split_axis=1, concat_axis=1, t...  80.7 us
    dot_general x1, matrix products, run_experts(): jnp.einsum('esf,efd->esd', hidden, down_weight, preferred_element_type=jn...  16.5 us
    all_to_all x1, starting transfers between devices, per_device(): lax.all_to_all(served, ('outer', 'inner'), split_axis=1, concat_axis=1, t...  16.5 us
    reshape x1, local copies, waits for them, and re-layouts, per_device(): outgoing = outgoing.reshape(local_experts, n_dev * capacity, width)  13 us
    convert_element_type x1, local copies, waits for them, and re-layouts, run_experts(): return jnp.einsum('esf,efd->esd', hidden, down_weight, preferred_element_...  12.6 us
  transfers between devices with their start and end apart: 3, of which 2 were waited for; matrix products, arithmetic and copies ran while one was open for 12% of the time, Pallas kernels for 0%

profile of v4, /device:TPU:126, one launch (start us, length us, event | category | flops | bytes accessed | tf_op | source)
XLA Modules:
  0.0 568.2 jit_solution(17926173894090188780)
XLA Ops:
  9.1 1.2 fusion.23
  10.3 1.1 select_reduce_fusion.1
  12.2 1.3 fusion
  13.5 2.9 convolution_convert_fusion
  16.4 13.0 %copy.115 = bf16[2,768,2048]{2,0,1:T(2,128)(2,1)S(1)} copy(bf16[2,768,2048]{2,1,0:T(8,128)(2,1)S(1)} %bitcast.135) | data formatting | bytes 12582912 | tf_op jit(solution)/shard_map/reshape | solution.py:264
  29.5 93.3 %all_to_all.10 = bf16[2,768,2048]{2,0,1:T(2,128)(2,1)S(1)} all-to-all(bf16[2,768,2048]{2,0,1:T(2,128)(2,1)S(1)} %copy.115), channel_id=1, replica_groups=mesh['outer'=8,'inner'=16] {'outer','inner'}, dimensions={1} | all-to-all | bytes 12582912 | tf_op jit(solution)/shard_map/all_to_all | solution.py:266
  122.8 2.6 copy-done.4
  125.4 5.3 fusion.3
  130.8 16.5 %convolution_convert_fusion.2 = bf16[2,768,2048]{2,1,0:T(8,128)(2,1)} fusion(bf16[2,512,2048]{2,1,0:T(8,128)(2,1)} %param.20, f32[2,768,512]{2,1,0:T(8,128)} %fusion.3, bf16[2,2048,512]{2,1,0:T(8,128)(2,1)} %param.19, bf16[2,768,2048]{2,0,1:T(2,128)(2,1)} %copy-done.4), kind=kOutput, calls=%fused_computation.9 | convolution fusion | flops 6450315264 | bytes 24117248 | tf_op jit(solution)/shard_map/esf,efd->esd/dot_general | solution.py:83
  147.3 12.6 %copy.118 = bf16[2,768,2048]{2,0,1:T(2,128)(2,1)} copy(bf16[2,768,2048]{2,1,0:T(8,128)(2,1)} %convolution_convert_fusion.2) | data formatting | bytes 12582912 | tf_op jit(solution)/shard_map/convert_element_type | solution.py:85
  159.9 16.5 %all-to-all-start.1 = ((bf16[2,768,2048]{2,0,1:T(2,128)(2,1)}), bf16[2,768,2048]{2,0,1:T(2,128)(2,1)}, u32[]{:S(2)}, u32[]{:S(2)}) async-start(bf16[2,768,2048]{2,0,1:T(2,128)(2,1)} %copy.118), calls=%async_computation.1 | async-start | bytes 12582912 | tf_op jit(solution)/shard_map/all_to_all | solution.py:271
  176.5 1.2 select_reduce_fusion
  177.8 80.7 %all-to-all-done.1 = bf16[2,768,2048]{2,0,1:T(2,128)(2,1)} async-done(((bf16[2,768,2048]{2,0,1:T(2,128)(2,1)}), bf16[2,768,2048]{2,0,1:T(2,128)(2,1)}, u32[]{:S(2)}, u32[]{:S(2)}) %all-to-all-start.1) | async-done | bytes 6291488 | tf_op jit(solution)/shard_map/all_to_all | solution.py:271
  258.5 5.7 copy.119
  264.2 1.0 fusion.59
  265.2 1.4 fusion.20
  268.2 8.2 %convolution_convert_fusion.1 = bf16[128,4096]{1,0:T(8,128)(2,1)S(1)} fusion(bf16[2048,4096]{1,0:T(8,128)(2,1)} %all-gather.2.cloned.1.call-done, bf16[128,2048]{1,0:T(8,128)(2,1)S(1)} %get-tuple-element.54, f32[2048]{0:T(1024)S(1)} %copy-done.34, f32[128]{0:T(128)S(1)} %add_rsqrt_fusion.3), kind=kOutput, calls=%fused_computation.8 | convolution fusion | flops 2149056512 | bytes 18358784 | tf_op jit(solution)/shard_map/dot_general | solution.py:281
  276.5 3.3 collective-permute-start
  280.5 2.7 collective-permute-done
  283.5 1.2 divide_multiply_fusion
  287.0 2.4 fusion.19
  291.6 1.4 fusion.31
  293.0 1.5 copy.122
  294.5 1.5 copy.123
  297.1 1.3 copy.138
  298.4 1.2 copy.126
  299.6 1.3 copy.139
  300.9 4.8 fusion.90
  305.7 4.8 convolution_negate_fusion.5
  310.5 0.9 select_maximum_fusion.5
  311.5 1.9 fusion.52
  313.5 1.8 convolution_negate_fusion.4
  315.8 1.0 fusion.50
  316.8 1.0 convolution_negate_fusion.3
  322.5 1.1 slice_bitcast_fusion
  323.6 1.1 slice.233
  325.4 2.6 copy.128
  328.0 2.6 copy.129
  331.8 1.3 fusion.26
  333.1 1.2 fusion.57
  334.3 1.9 fusion.96.state_ref
  336.2 2.0 convolution_subtract_fusion.1.map_ref
  338.3 213.3 %shard_map.149 = f32[16,128,128]{2,1,0:T(8,128)S(1)} custom-call(f32[16,128,128]{2,1,0:T(8,128)S(1)} %convolution_subtract_fusion.1.map_ref, f32[16,128,128]{2,1,0:T(8,128)S(1)} %fusion.96.state_ref), custom_call_target="tpu_custom_call" | custom-call | tf_op jit(solution)/shard_map/pallas_call | solution.py:201
  551.6 1.2 convolution_subtract_fusion
  553.6 2.3 convolution_multiply_fusion
  555.9 1.8 fusion.16
  557.8 1.9 multiply_reduce_fusion
  559.9 1.0 copy.133
  (148 shorter events, 18.9 us)
Async XLA Ops:
  7.2 259.4 %copy-start = (bf16[2048,32]{0,1:T(8,128)(2,1)S(1)}, bf16[2048,32]{0,1:T(8,128)(2,1)}, u32[]{:S(2)}) copy-start(bf16[2048,32]{0,1:T(8,128)(2,1)} %param.23) | copy-start | bytes 393220
  7.2 261.0 %all-gather.2.cloned.1.call-start = ((), (), s32[]{:S(2)}) async-start(), calls=%async_computation.2 | async-start | bytes 17825792 | tf_op jit(solution)/shard_map/all_gather | solution.py:283
  29.5 96.0 %copy-start.42 = (bf16[2,2048,512]{2,1,0:T(8,128)(2,1)S(1)}, bf16[2,2048,512]{2,1,0:T(8,128)(2,1)}, u32[]{:S(2)}) copy-start(bf16[2,2048,512]{2,1,0:T(8,128)(2,1)} %param.18) | copy-start | bytes 12582916
  122.8 2.6 copy-start.4
  159.9 16.5 %copy-start.38 = (f32[128,10]{0,1:T(8,128)S(1)}, f32[128,10]{0,1:T(8,128)}, u32[]{:S(2)}) copy-start(f32[128,10]{0,1:T(8,128)} %param.16) | copy-start | bytes 15364
  159.9 16.6 %copy-start.43 = (f32[16]{0:T(128)S(1)}, f32[16]{0:T(128)}, u32[]{:S(2)}) copy-start(f32[16]{0:T(128)} %param.25) | copy-start | bytes 196
  159.9 17.8 %copy-start.33 = (bf16[4,4096]{1,0:T(4,128)(2,1)S(1)}, bf16[4,4096]{1,0:T(4,128)(2,1)}, u32[]{:S(2)}) copy-start(bf16[4,4096]{1,0:T(4,128)(2,1)} %param.24) | copy-start | bytes 98308
  159.9 98.5 %all-to-all-start.1 = ((bf16[2,768,2048]{2,0,1:T(2,128)(2,1)}), bf16[2,768,2048]{2,0,1:T(2,128)(2,1)}, u32[]{:S(2)}, u32[]{:S(2)}) async-start(bf16[2,768,2048]{2,0,1:T(2,128)(2,1)} %copy.118), calls=%async_computation.1 | async-start | bytes 12582912 | tf_op jit(solution)/shard_map/all_to_all | solution.py:271
  176.5 110.6 %copy-start.31 = (pred[128,128]{1,0:T(8,128)(4,1)}, pred[128,128]{1,0:T(8,128)(4,1)S(1)}, u32[]{:S(2)}) copy-start(pred[128,128]{1,0:T(8,128)(4,1)S(1)} %get-tuple-element.57) | copy-start | bytes 49156
  264.1 1.0 copy-start.5
  265.2 1.4 copy-start.34
  265.2 1.8 copy-start.40
  266.6 9.9 %copy-start.27 = (bf16[128,2048]{1,0:T(8,128)(2,1)}, bf16[128,2048]{1,0:T(8,128)(2,1)S(1)}, u32[]{:S(2)}) copy-start(bf16[128,2048]{1,0:T(8,128)(2,1)S(1)} %get-tuple-element.54) | copy-start | bytes 1572868
  276.5 6.7 %collective-permute-start = (bf16[3,4096]{1,0:T(4,128)(2,1)S(1)}, bf16[3,4096]{1,0:T(4,128)(2,1)S(1)}, u32[]{:S(2)}, u32[]{:S(2)}) collective-permute-start(bf16[3,4096]{1,0:T(4,128)(2,1)S(1)} %slice.191), channel_id=1, source_target_pairs={{0,1},{1,2},{2,3},{3,4},{4,5},{5,6},{6,7},{7,8},{8,9},{9,10},{10,1... | collective-permute-start | bytes 73736 | tf_op jit(solution)/shard_map/ppermute | solution.py:13
  286.2 0.8 copy-start.6
  289.4 1.0 copy-start.2
  289.7 1.0 copy-start.10
  289.7 1.1 copy-start.12
  289.9 1.0 copy-start.14
  289.9 1.2 copy-start.16
  290.5 0.8 copy-start.18
  290.5 1.0 copy-start.20
  290.8 0.8 copy-start.22
  290.8 2.2 copy-start.24
  300.9 9.6 %copy-start.28 = (f32[1,2,2,2,2,2,16,2,2]{8,7,6,5,4,3,2,1,0:T(2,128)S(1)}, f32[1,2,2,2,2,2,16,2,2]{8,7,6,5,4,3,2,1,0:T(2,128)}, u32[]{:S(2)}) copy-start(f32[1,2,2,2,2,2,16,2,2]{8,7,6,5,4,3,2,1,0:T(2,128)} %copy.138) | copy-start | bytes 24580
  300.9 9.6 %copy-start.29 = (f32[1,2,2,2,2,2,16,2,2]{8,7,6,5,4,3,2,1,0:T(2,128)S(1)}, f32[1,2,2,2,2,2,16,2,2]{8,7,6,5,4,3,2,1,0:T(2,128)}, u32[]{:S(2)}) copy-start(f32[1,2,2,2,2,2,16,2,2]{8,7,6,5,4,3,2,1,0:T(2,128)} %copy.139) | copy-start | bytes 24580
  300.9 10.6 %copy-start.23 = (f32[1,2,2,2,16,8,8]{6,5,4,3,2,1,0:T(8,128)S(1)}, f32[1,2,2,2,16,8,8]{6,5,4,3,2,1,0:T(8,128)}, u32[]{:S(2)}) copy-start(f32[1,2,2,2,16,8,8]{6,5,4,3,2,1,0:T(8,128)} %copy-done.22) | copy-start | bytes 98308
  300.9 10.6 %copy-start.25 = (f32[1,2,2,2,16,8,8]{6,5,4,3,2,1,0:T(8,128)S(1)}, f32[1,2,2,2,16,8,8]{6,5,4,3,2,1,0:T(8,128)}, u32[]{:S(2)}) copy-start(f32[1,2,2,2,16,8,8]{6,5,4,3,2,1,0:T(8,128)} %copy-done.24) | copy-start | bytes 98308
  313.4 2.4 copy-start.19
  313.4 2.4 copy-start.21
  316.7 1.3 copy-start.15
  316.7 1.3 copy-start.17
  318.7 1.0 copy-start.11
  318.7 1.2 copy-start.13
  320.6 1.2 copy-start.3
  324.7 5.9 %copy-start.7 = (f32[128,8,128]{2,0,1:T(8,128)S(1)}, f32[128,8,128]{2,0,1:T(8,128)}, u32[]{:S(2)}) copy-start(f32[128,8,128]{2,0,1:T(8,128)} %copy-done.6) | copy-start | bytes 1572868
  324.7 5.9 %copy-start.36 = (f32[16,128]{1,0:T(8,128)S(1)}, f32[16,128]{1,0:T(8,128)}, u32[]{:S(2)}) copy-start(f32[16,128]{1,0:T(8,128)} %get-tuple-element.50) | copy-start | bytes 24580
  324.7 5.9 %copy-start.37 = (f32[16,128]{1,0:T(8,128)S(1)}, f32[16,128]{1,0:T(8,128)}, u32[]{:S(2)}) copy-start(f32[16,128]{1,0:T(8,128)} %get-tuple-element.51) | copy-start | bytes 24580
  325.3 5.8 %copy-start.8 = (f32[16,64,64]{2,1,0:T(8,128)S(1)}, f32[16,64,64]{2,1,0:T(8,128)}, u32[]{:S(2)}) copy-start(f32[16,64,64]{2,1,0:T(8,128)} %get-tuple-element.16) | copy-start | bytes 786436
  325.3 5.8 %copy-start.9 = (f32[16,64,64]{2,1,0:T(8,128)S(1)}, f32[16,64,64]{2,1,0:T(8,128)}, u32[]{:S(2)}) copy-start(f32[16,64,64]{2,1,0:T(8,128)} %get-tuple-element.17) | copy-start | bytes 786436
  330.5 1.2 copy-start.26
  333.1 3.2 copy-start.39
  338.3 214.5 %copy-start.30 = (f32[16,8,8,128]{3,1,2,0:T(8,128)S(1)}, f32[16,8,8,128]{3,1,2,0:T(8,128)}, u32[]{:S(2)}) copy-start(f32[16,8,8,128]{3,1,2,0:T(8,128)} %get-tuple-element.15) | copy-start | bytes 1572868
  552.8 0.8 copy-start.32
  553.3 2.6 copy-start.35
  555.9 3.8 copy-start.41
  555.9 5.0 copy-start.1
Sparse Core Ops, SparseCore 0:
  10.1 240.0 all-gather.1

commit v5 on v1

--- a/solution.py
+++ b/solution.py
@@ -2,6 +2,9 @@
 import jax.numpy as jnp
 from jax import lax
 from jax.sharding import PartitionSpec as P
+from jax.experimental import pallas as pl
+from jax.experimental.pallas import tpu as pltpu
+import functools
 
 
 def shifted(value, axis, steps):
@@ -109,6 +112,125 @@
         + next_state
     )
     return (joined_map, joined_state)
+
+
+def shifted_linear(value, axes, count, steps):
+    return lax.ppermute(value, axes, [(source, source + steps) for source in range(count - steps)])
+
+
+def scan_kernel(count, axes, groups, map_ref, state_ref, out_ref, own_map, own_state, send_map,
+                send_state, land_map, land_state, send_sems, recv_sems):
+    place = lax.axis_index(axes)
+    span = map_ref.shape[0] // groups
+    own_map[...] = map_ref[...]
+    own_state[...] = state_ref[...]
+    rounds = []
+    steps = 1
+    while steps < count:
+        rounds.append(steps)
+        steps *= 2
+    rounds.append(1)
+    total = len(rounds)
+    inner = lax.axis_size(axes[1])
+
+    def copies(number, group):
+        other = place + rounds[number]
+        heads = pl.ds(group * span, span)
+        found = [
+            pltpu.make_async_remote_copy(
+                src_ref=send_state.at[number, heads], dst_ref=land_state.at[number, heads],
+                send_sem=send_sems.at[number, group, 0], recv_sem=recv_sems.at[number, group, 0],
+                device_id=(other // inner, other % inner), device_id_type=pl.DeviceIdType.MESH)
+        ]
+        if number < total - 2:
+            found.append(
+                pltpu.make_async_remote_copy(
+                    src_ref=send_map.at[number, heads], dst_ref=land_map.at[number, heads],
+                    send_sem=send_sems.at[number, group, 1], recv_sem=recv_sems.at[number, group, 1],
+                    device_id=(other // inner, other % inner), device_id_type=pl.DeviceIdType.MESH)
+            )
+        return found
+
+    def joined(number, group):
+        def head(h, carry):
+            mine = own_map[h]
+            high = mine.astype(jnp.bfloat16)
+            low = (mine - high.astype(jnp.float32)).astype(jnp.bfloat16)
+
+            def apply(far):
+                return jnp.dot(high, far, preferred_element_type=jnp.float32) + jnp.dot(
+                    low, far, preferred_element_type=jnp.float32)
+
+            own_state[h] = apply(land_state[number, h]) + own_state[h]
+            if number < total - 2:
+                own_map[h] = apply(land_map[number, h])
+            return carry
+
+        lax.fori_loop(group * span, group * span + span, head, 0)
+
+    for number in range(total):
+        for group in range(groups):
+            heads = pl.ds(group * span, span)
+            if number > 0:
+                @pl.when(place >= rounds[number - 1])
+                def _():
+                    for copy in copies(number - 1, group):
+                        copy.wait_recv()
+                    joined(number - 1, group)
+            send_state[number, heads] = own_state[heads].astype(jnp.bfloat16)
+            if number < total - 2:
+                send_map[number, heads] = own_map[heads].astype(jnp.bfloat16)
+
+            @pl.when(place + rounds[number] < count)
+            def _():
+                for copy in copies(number, group):
+                    copy.start()
+
+    for group in range(groups):
+        heads = pl.ds(group * span, span)
+
+        @pl.when(place >= 1)
+        def _():
+            for copy in copies(total - 1, group):
+                copy.wait_recv()
+            out_ref[heads] = land_state[total - 1, heads].astype(jnp.float32)
+
+        @pl.when(place < 1)
+        def _():
+            out_ref[heads] = jnp.zeros_like(out_ref[heads])
+
+    for number in range(total):
+        @pl.when(place + rounds[number] < count)
+        def _():
+            for group in range(groups):
+                for copy in copies(number, group):
+                    copy.wait_send()
+
+
+def chained_state(state_map, state_increment, axes, count):
+    heads, size, width = state_increment.shape
+    rounds = 1
+    while (1 << (rounds - 1)) < count:
+        rounds += 1
+    groups = 4
+    block = pltpu.VMEM((rounds, heads, size, width), jnp.bfloat16)
+    return pl.pallas_call(
+        functools.partial(scan_kernel, count, axes, groups),
+        out_shape=jax.ShapeDtypeStruct(state_increment.shape, jnp.float32),
+        in_specs=[pl.BlockSpec(memory_space=pltpu.VMEM)] * 2,
+        out_specs=pl.BlockSpec(memory_space=pltpu.VMEM),
+        scratch_shapes=[
+            pltpu.VMEM(state_map.shape, jnp.float32),
+            pltpu.VMEM(state_increment.shape, jnp.float32),
+            pltpu.VMEM((rounds, heads, size, size), jnp.bfloat16),
+            block,
+            pltpu.VMEM((rounds, heads, size, size), jnp.bfloat16),
+            block,
+            pltpu.SemaphoreType.DMA((rounds, groups, 2)),
+            pltpu.SemaphoreType.DMA((rounds, groups, 2)),
+        ],
+        compiler_params=pltpu.CompilerParams(has_side_effects=True, vmem_limit_bytes=48 * 1024 * 1024),
+    )(state_map, state_increment)
 
 
 def per_device(
@@ -239,13 +361,7 @@
     state_increment = jnp.einsum(
         "xbe,xbz->xez", trailing_keys, value_resolved, precision=lax.Precision.HIGHEST
     )
-    identity = (eye_heads, jnp.zeros_like(state_increment))
-    inner_pre = prefix_2((state_map, state_increment), "inner", join_maps, identity)
-    inclusive = join_maps(inner_pre, (state_map, state_increment))
-    group = spread_2(shortened(jnp.stack(inclusive)), "inner", n_inner - 1)
-    outer_pre = entering((group[0], group[1]), "outer", join_maps, identity)
-    prefix = join_maps(outer_pre, inner_pre)
-    initial_state = prefix[1]
+    initial_state = chained_state(state_map, state_increment, ("outer", "inner"), n_dev)
     updates = value_resolved - jnp.einsum(
         "mwx,mxd->mwd", key_resolved, initial_state, precision=lax.Precision.HIGHEST
     )

time: 731 us -> 530 us (0.73)
  waiting for transfers between devices: 396 us -> 84.2 us
  Pallas kernels: 0 us -> 168 us
  matrix products: 125 us -> 71.1 us
    all_gather x4 -> x0, waiting for transfers between devices: 204 us -> none  [the longest x2 141 us: prefix_2(): lax.all_gather(a.astype(kind), axis)]
    pallas_call x0 -> x1, Pallas kernels: none -> 168 us  [chained_state(): pl.pallas_call(functools.partial(scan_kernel, count, axes, groups), out_s...]
    psum x1 -> x0, waiting for transfers between devices: 106 us -> none  [spread_2(): return lax.psum(kept, axis)]
    dot_general x29 -> x0, matrix products: 48.6 us -> none  [the longest x19 32.1 us: join_maps(): jnp.einsum('hij,hjv->hiv', next_map, first_state, precision=lax.Precision...]
  transfers between devices with their start and end apart: 8 -> 3, of which waited for: 7 -> 1; matrix products, arithmetic and copies ran while one was open for 11% -> 13% of each run, Pallas kernels for 0% -> 0%
where the time goes in v5:
time: 530 us; the launch traced here: 525 us
  Pallas kernels  168 us (32%)
  blocking collectives  95.9 us (18%)
  waiting for transfers between devices  84.2 us (16%)
  matrix products  71.1 us (13%)
  local copies, waits for them, and re-layouts  55 us (10%)
  starting transfers between devices  19.6 us (4%)
  other arithmetic  16.2 us (3%)
  between operations  15.4 us (3%)
    pallas_call x1, Pallas kernels, chained_state(): pl.pallas_call(functools.partial(scan_kernel, count, axes, groups), out_s...  168 us
    all_to_all x1, blocking collectives, per_device(): lax.all_to_all(outgoing, ('outer', 'inner'), split_axis=1, concat_axis=1,...  95.9 us
    all_to_all x1, waiting for transfers between devices, per_device(): lax.all_to_all(served, ('outer', 'inner'), split_axis=1, concat_axis=1, t...  83.5 us
    dot_general x1, matrix products, run_experts(): jnp.einsum('esf,efd->esd', hidden, down_weight, preferred_element_type=jn...  16.5 us
    all_to_all x1, starting transfers between devices, per_device(): lax.all_to_all(served, ('outer', 'inner'), split_axis=1, concat_axis=1, t...  14.5 us
    reshape x1, local copies, waits for them, and re-layouts, per_device(): outgoing = outgoing.reshape(local_experts, n_dev * capacity, width)  13 us
    convert_element_type x1, local copies, waits for them, and re-layouts, run_experts(): return jnp.einsum('esf,efd->esd', hidden, down_weight, preferred_element_...  12.6 us
  transfers between devices with their start and end apart: 3, of which 1 were waited for; matrix products, arithmetic and copies ran while one was open for 13% of the time, Pallas kernels for 0%

profile of v5, /device:TPU:83, one launch (start us, length us, event | category | flops | bytes accessed | tf_op | source)
XLA Modules:
  0.0 525.3 jit_solution(17286758272722852745)
XLA Ops:
  7.9 0.9 convert_reduce_fusion
  9.1 1.2 fusion.23
  10.3 1.1 select_reduce_fusion.1
  12.2 1.3 fusion
  13.5 2.9 convolution_convert_fusion
  16.4 13.0 %copy.115 = bf16[2,768,2048]{2,0,1:T(2,128)(2,1)S(1)} copy(bf16[2,768,2048]{2,1,0:T(8,128)(2,1)S(1)} %bitcast.135) | data formatting | bytes 12582912 | tf_op jit(solution)/shard_map/reshape | solution.py:280
  29.5 95.9 %all_to_all.10 = bf16[2,768,2048]{2,0,1:T(2,128)(2,1)S(1)} all-to-all(bf16[2,768,2048]{2,0,1:T(2,128)(2,1)S(1)} %copy.115), channel_id=1, replica_groups=mesh['outer'=8,'inner'=16] {'outer','inner'}, dimensions={1} | all-to-all | bytes 12582912 | tf_op jit(solution)/shard_map/all_to_all | solution.py:282
  125.4 2.6 copy-done.4
  128.0 5.3 %fusion.3 = f32[2,768,512]{2,1,0:T(8,128)} fusion(bf16[2,2048,512]{2,1,0:T(8,128)(2,1)S(1)} %copy-done.42, bf16[2,768,2048]{2,0,1:T(2,128)(2,1)S(1)} %all_to_all.10), kind=kOutput, calls=%fused_computation.6 | convolution fusion | flops 3221225472 | bytes 13631488 | tf_op jit(solution)/shard_map/esd,edf->esf/dot_general | solution.py:80
  133.3 16.5 %convolution_convert_fusion.2 = bf16[2,768,2048]{2,1,0:T(8,128)(2,1)} fusion(bf16[2,512,2048]{2,1,0:T(8,128)(2,1)} %param.20, f32[2,768,512]{2,1,0:T(8,128)} %fusion.3, bf16[2,2048,512]{2,1,0:T(8,128)(2,1)} %param.19, bf16[2,768,2048]{2,0,1:T(2,128)(2,1)} %copy-done.4), kind=kOutput, calls=%fused_computation.9 | convolution fusion | flops 6450315264 | bytes 24117248 | tf_op jit(solution)/shard_map/esf,efd->esd/dot_general | solution.py:83
  149.8 12.6 %copy.118 = bf16[2,768,2048]{2,0,1:T(2,128)(2,1)} copy(bf16[2,768,2048]{2,1,0:T(8,128)(2,1)} %convolution_convert_fusion.2) | data formatting | bytes 12582912 | tf_op jit(solution)/shard_map/convert_element_type | solution.py:85
  162.5 14.5 %all-to-all-start.1 = ((bf16[2,768,2048]{2,0,1:T(2,128)(2,1)}), bf16[2,768,2048]{2,0,1:T(2,128)(2,1)}, u32[]{:S(2)}, u32[]{:S(2)}) async-start(bf16[2,768,2048]{2,0,1:T(2,128)(2,1)} %copy.118), calls=%async_computation.1 | async-start | bytes 12582912 | tf_op jit(solution)/shard_map/all_to_all | solution.py:287
  177.1 1.2 select_reduce_fusion
  178.3 83.5 %all-to-all-done.1 = bf16[2,768,2048]{2,0,1:T(2,128)(2,1)} async-done(((bf16[2,768,2048]{2,0,1:T(2,128)(2,1)}), bf16[2,768,2048]{2,0,1:T(2,128)(2,1)}, u32[]{:S(2)}, u32[]{:S(2)}) %all-to-all-start.1) | async-done | bytes 6291488 | tf_op jit(solution)/shard_map/all_to_all | solution.py:287
  261.8 5.7 %copy.119 = bf16[2,768,2048]{2,1,0:T(8,128)(2,1)S(1)} copy(bf16[2,768,2048]{2,0,1:T(2,128)(2,1)} %all-to-all-done.1) | data formatting | bytes 12582912 | tf_op jit(solution)/shard_map/all_to_all | solution.py:287
  267.5 1.0 fusion.59
  268.6 1.4 fusion.20
  271.6 8.2 %convolution_convert_fusion.1 = bf16[128,4096]{1,0:T(8,128)(2,1)S(1)} fusion(bf16[2048,4096]{1,0:T(8,128)(2,1)} %all-gather.2.cloned.1.call-done, bf16[128,2048]{1,0:T(8,128)(2,1)S(1)} %get-tuple-element.54, f32[2048]{0:T(1024)S(1)} %copy-done.34, f32[128]{0:T(128)S(1)} %add_rsqrt_fusion.3), kind=kOutput, calls=%fused_computation.8 | convolution fusion | flops 2149056512 | bytes 18358784 | tf_op jit(solution)/shard_map/dot_general | solution.py:297
  279.9 5.2 collective-permute-start
  286.0 1.2 divide_multiply_fusion
  289.6 2.4 fusion.19
  294.2 1.4 fusion.31
  295.6 1.5 copy.122
  297.1 1.5 copy.123
  299.7 1.3 copy.138
  301.0 1.2 copy.126
  302.2 1.3 copy.139
  303.5 4.8 fusion.90
  308.3 4.8 convolution_negate_fusion.5
  313.1 0.9 select_maximum_fusion.5
  314.1 1.9 fusion.52
  316.1 1.8 convolution_negate_fusion.4
  318.4 1.0 fusion.50
  319.4 1.0 convolution_negate_fusion.3
  325.1 1.1 slice_bitcast_fusion
  326.2 1.1 slice.233
  327.9 2.6 copy.128
  330.6 2.6 copy.129
  334.4 1.3 fusion.26
  335.7 1.2 fusion.57
  336.9 1.9 fusion.96.state_ref
  338.8 2.0 convolution_subtract_fusion.1.map_ref
  340.9 167.8 %shard_map.149 = f32[16,128,128]{2,1,0:T(8,128)S(1)} custom-call(f32[16,128,128]{2,1,0:T(8,128)S(1)} %convolution_subtract_fusion.1.map_ref, f32[16,128,128]{2,1,0:T(8,128)S(1)} %fusion.96.state_ref), custom_call_target="tpu_custom_call" | custom-call | tf_op jit(solution)/shard_map/pallas_call | solution.py:217
  508.7 1.2 convolution_subtract_fusion
  510.7 2.3 convolution_multiply_fusion
  513.1 1.8 fusion.16
  514.9 1.9 multiply_reduce_fusion
  517.0 1.0 copy.133
  (148 shorter events, 18.0 us)
Async XLA Ops:
  7.2 262.8 %copy-start = (bf16[2048,32]{0,1:T(8,128)(2,1)S(1)}, bf16[2048,32]{0,1:T(8,128)(2,1)}, u32[]{:S(2)}) copy-start(bf16[2048,32]{0,1:T(8,128)(2,1)} %param.23) | copy-start | bytes 393220
  7.2 264.4 %all-gather.2.cloned.1.call-start = ((), (), s32[]{:S(2)}) async-start(), calls=%async_computation.2 | async-start | bytes 17825792 | tf_op jit(solution)/shard_map/all_gather | solution.py:299
  29.4 98.5 %copy-start.42 = (bf16[2,2048,512]{2,1,0:T(8,128)(2,1)S(1)}, bf16[2,2048,512]{2,1,0:T(8,128)(2,1)}, u32[]{:S(2)}) copy-start(bf16[2,2048,512]{2,1,0:T(8,128)(2,1)} %param.18) | copy-start | bytes 12582916
  125.4 2.6 copy-start.4
  162.5 14.5 %copy-start.38 = (f32[128,10]{0,1:T(8,128)S(1)}, f32[128,10]{0,1:T(8,128)}, u32[]{:S(2)}) copy-start(f32[128,10]{0,1:T(8,128)} %param.16) | copy-start | bytes 15364
  162.5 14.6 %copy-start.43 = (f32[16]{0:T(128)S(1)}, f32[16]{0:T(128)}, u32[]{:S(2)}) copy-start(f32[16]{0:T(128)} %param.25) | copy-start | bytes 196
  162.5 15.8 %copy-start.33 = (bf16[4,4096]{1,0:T(4,128)(2,1)S(1)}, bf16[4,4096]{1,0:T(4,128)(2,1)}, u32[]{:S(2)}) copy-start(bf16[4,4096]{1,0:T(4,128)(2,1)} %param.24) | copy-start | bytes 98308
  162.5 99.3 %all-to-all-start.1 = ((bf16[2,768,2048]{2,0,1:T(2,128)(2,1)}), bf16[2,768,2048]{2,0,1:T(2,128)(2,1)}, u32[]{:S(2)}, u32[]{:S(2)}) async-start(bf16[2,768,2048]{2,0,1:T(2,128)(2,1)} %copy.118), calls=%async_computation.1 | async-start | bytes 12582912 | tf_op jit(solution)/shard_map/all_to_all | solution.py:287
  177.0 112.6 %copy-start.31 = (pred[128,128]{1,0:T(8,128)(4,1)}, pred[128,128]{1,0:T(8,128)(4,1)S(1)}, u32[]{:S(2)}) copy-start(pred[128,128]{1,0:T(8,128)(4,1)S(1)} %get-tuple-element.57) | copy-start | bytes 49156
  267.5 1.0 copy-start.5
  268.6 1.4 copy-start.34
  268.6 1.8 copy-start.40
  269.9 9.9 %copy-start.27 = (bf16[128,2048]{1,0:T(8,128)(2,1)}, bf16[128,2048]{1,0:T(8,128)(2,1)S(1)}, u32[]{:S(2)}) copy-start(bf16[128,2048]{1,0:T(8,128)(2,1)S(1)} %get-tuple-element.54) | copy-start | bytes 1572868
  279.9 5.9 %collective-permute-start = (bf16[3,4096]{1,0:T(4,128)(2,1)S(1)}, bf16[3,4096]{1,0:T(4,128)(2,1)S(1)}, u32[]{:S(2)}, u32[]{:S(2)}) collective-permute-start(bf16[3,4096]{1,0:T(4,128)(2,1)S(1)} %slice.191), channel_id=1, source_target_pairs={{0,1},{1,2},{2,3},{3,4},{4,5},{5,6},{6,7},{7,8},{8,9},{9,10},{10,1... | collective-permute-start | bytes 73736 | tf_op jit(solution)/shard_map/ppermute | solution.py:13
  288.8 0.8 copy-start.6
  292.0 1.0 copy-start.2
  292.3 1.0 copy-start.10
  292.3 1.1 copy-start.12
  292.5 1.0 copy-start.14
  292.5 1.2 copy-start.16
  293.1 0.8 copy-start.18
  293.1 1.0 copy-start.20
  293.4 0.8 copy-start.22
  293.4 2.2 copy-start.24
  303.5 9.6 %copy-start.28 = (f32[1,2,2,2,2,2,16,2,2]{8,7,6,5,4,3,2,1,0:T(2,128)S(1)}, f32[1,2,2,2,2,2,16,2,2]{8,7,6,5,4,3,2,1,0:T(2,128)}, u32[]{:S(2)}) copy-start(f32[1,2,2,2,2,2,16,2,2]{8,7,6,5,4,3,2,1,0:T(2,128)} %copy.138) | copy-start | bytes 24580
  303.5 9.6 %copy-start.29 = (f32[1,2,2,2,2,2,16,2,2]{8,7,6,5,4,3,2,1,0:T(2,128)S(1)}, f32[1,2,2,2,2,2,16,2,2]{8,7,6,5,4,3,2,1,0:T(2,128)}, u32[]{:S(2)}) copy-start(f32[1,2,2,2,2,2,16,2,2]{8,7,6,5,4,3,2,1,0:T(2,128)} %copy.139) | copy-start | bytes 24580
  303.5 10.6 %copy-start.23 = (f32[1,2,2,2,16,8,8]{6,5,4,3,2,1,0:T(8,128)S(1)}, f32[1,2,2,2,16,8,8]{6,5,4,3,2,1,0:T(8,128)}, u32[]{:S(2)}) copy-start(f32[1,2,2,2,16,8,8]{6,5,4,3,2,1,0:T(8,128)} %copy-done.22) | copy-start | bytes 98308
  303.5 10.6 %copy-start.25 = (f32[1,2,2,2,16,8,8]{6,5,4,3,2,1,0:T(8,128)S(1)}, f32[1,2,2,2,16,8,8]{6,5,4,3,2,1,0:T(8,128)}, u32[]{:S(2)}) copy-start(f32[1,2,2,2,16,8,8]{6,5,4,3,2,1,0:T(8,128)} %copy-done.24) | copy-start | bytes 98308
  316.0 2.4 copy-start.19
  316.0 2.4 copy-start.21
  319.3 1.3 copy-start.15
  319.3 1.3 copy-start.17
  321.3 1.0 copy-start.11
  321.3 1.2 copy-start.13
  323.2 1.2 copy-start.3
  327.3 5.9 %copy-start.7 = (f32[128,8,128]{2,0,1:T(8,128)S(1)}, f32[128,8,128]{2,0,1:T(8,128)}, u32[]{:S(2)}) copy-start(f32[128,8,128]{2,0,1:T(8,128)} %copy-done.6) | copy-start | bytes 1572868
  327.3 5.9 %copy-start.36 = (f32[16,128]{1,0:T(8,128)S(1)}, f32[16,128]{1,0:T(8,128)}, u32[]{:S(2)}) copy-start(f32[16,128]{1,0:T(8,128)} %get-tuple-element.50) | copy-start | bytes 24580
  327.3 5.9 %copy-start.37 = (f32[16,128]{1,0:T(8,128)S(1)}, f32[16,128]{1,0:T(8,128)}, u32[]{:S(2)}) copy-start(f32[16,128]{1,0:T(8,128)} %get-tuple-element.51) | copy-start | bytes 24580
  327.9 5.8 %copy-start.8 = (f32[16,64,64]{2,1,0:T(8,128)S(1)}, f32[16,64,64]{2,1,0:T(8,128)}, u32[]{:S(2)}) copy-start(f32[16,64,64]{2,1,0:T(8,128)} %get-tuple-element.16) | copy-start | bytes 786436
  327.9 5.8 %copy-start.9 = (f32[16,64,64]{2,1,0:T(8,128)S(1)}, f32[16,64,64]{2,1,0:T(8,128)}, u32[]{:S(2)}) copy-start(f32[16,64,64]{2,1,0:T(8,128)} %get-tuple-element.17) | copy-start | bytes 786436
  333.1 1.2 copy-start.26
  335.7 3.2 copy-start.39
  340.9 169.0 %copy-start.30 = (f32[16,8,8,128]{3,1,2,0:T(8,128)S(1)}, f32[16,8,8,128]{3,1,2,0:T(8,128)}, u32[]{:S(2)}) copy-start(f32[16,8,8,128]{3,1,2,0:T(8,128)} %get-tuple-element.15) | copy-start | bytes 1572868
  509.9 0.8 copy-start.32
  510.5 2.6 copy-start.35
  513.0 3.8 copy-start.41
  513.0 5.0 copy-start.1
Sparse Core Ops, SparseCore 0:
  10.1 217.0 all-gather.1

commit v6 on v5

--- a/solution.py
+++ b/solution.py
@@ -257,6 +257,13 @@
     local_experts = gate_weight.shape[0]
     experts_all = local_experts * n_dev
     capacity = max(2, 6 * tok_count * top_count // (5 * experts_all))
+    rows_half = mixer_weight.shape[0] // 2
+    side = lax.axis_index("outer") % 2
+    own_rows = lax.dynamic_slice_in_dim(mixer_weight, side * rows_half, rows_half, axis=0)
+    own_half = lax.all_gather(own_rows, "inner", axis=1, tiled=True)
+    other_half = lax.ppermute(
+        own_half, "outer", [(source, source ^ 1) for source in range(n_outer)]
+    )
     normed_first = rms_scale(tokens_in, first_gain).astype(jnp.bfloat16)
     mix_weight = route_weight / jnp.sum(route_weight, axis=1, keepdims=True)
     flat_ids = expert_ids
@@ -295,8 +302,12 @@
     hidden_out = (tokens_in.astype(jnp.float32) + mixture).astype(jnp.bfloat16)
     normed_second = rms_scale(hidden_out, second_gain).astype(jnp.bfloat16)
     mixed = jnp.dot(
-        normed_second,
-        lax.all_gather(mixer_weight, "inner", axis=1, tiled=True),
+        lax.dynamic_slice_in_dim(normed_second, side * rows_half, rows_half, axis=1),
+        own_half,
+        preferred_element_type=jnp.float32,
+    ) + jnp.dot(
+        lax.dynamic_slice_in_dim(normed_second, (1 - side) * rows_half, rows_half, axis=1),
+        other_half,
         preferred_element_type=jnp.float32,
     )
     projected = mixed.astype(jnp.bfloat16)

time: 530 us -> 512 us (0.966)
  waiting for transfers between devices: 84.2 us -> 71.1 us
    all_to_all x1, waiting for transfers between devices: 83.5 us -> 69 us  [per_device(): lax.all_to_all(served, ('outer', 'inner'), split_axis=1, concat_axis=1, t...]
    unnamed x94 -> x102, local copies, waits for them, and re-layouts: 10.1 us -> 11.5 us
  transfers between devices with their start and end apart: 3 -> 4, of which waited for: 1 -> 2; matrix products, arithmetic and copies ran while one was open for 13% -> 14% of each run, Pallas kernels for 0% -> 0%
where the time goes in v6:
time: 512 us; the launch traced here: 507 us
  Pallas kernels  166 us (32%)
  blocking collectives  92.4 us (18%)
  matrix products  71.8 us (14%)
  waiting for transfers between devices  71.1 us (14%)
  local copies, waits for them, and re-layouts  55.6 us (11%)
  starting transfers between devices  17.8 us (3%)
  other arithmetic  16.4 us (3%)
  between operations  15.3 us (3%)
    pallas_call x1, Pallas kernels, chained_state(): pl.pallas_call(functools.partial(scan_kernel, count, axes, groups), out_s...  166 us
    all_to_all x1, blocking collectives, per_device(): lax.all_to_all(outgoing, ('outer', 'inner'), split_axis=1, concat_axis=1,...  92.4 us
    all_to_all x1, waiting for transfers between devices, per_device(): lax.all_to_all(served, ('outer', 'inner'), split_axis=1, concat_axis=1, t...  69 us
    dot_general x1, matrix products, run_experts(): jnp.einsum('esf,efd->esd', hidden, down_weight, preferred_element_type=jn...  16.8 us
    all_to_all x1, starting transfers between devices, per_device(): lax.all_to_all(served, ('outer', 'inner'), split_axis=1, concat_axis=1, t...  14.4 us
    reshape x1, local copies, waits for them, and re-layouts, per_device(): outgoing = outgoing.reshape(local_experts, n_dev * capacity, width)  13 us
    convert_element_type x1, local copies, waits for them, and re-layouts, run_experts(): return jnp.einsum('esf,efd->esd', hidden, down_weight, preferred_element_...  12.6 us
    unnamed x102, local copies, waits for them, and re-layouts  11.5 us
  transfers between devices with their start and end apart: 4, of which 2 were waited for; matrix products, arithmetic and copies ran while one was open for 14% of the time, Pallas kernels for 0%

profile of v6, /device:TPU:83, one launch (start us, length us, event | category | flops | bytes accessed | tf_op | source)
XLA Modules:
  0.0 507.0 jit_solution(13777133615436998052)
XLA Ops:
  7.3 1.1 copy-done
  10.4 1.2 fusion.24
  11.6 1.1 select_reduce_fusion.1
  13.5 1.3 fusion
  14.8 1.9 convolution_convert_fusion
  16.7 13.0 %copy.115 = bf16[2,768,2048]{2,0,1:T(2,128)(2,1)S(1)} copy(bf16[2,768,2048]{2,1,0:T(8,128)(2,1)S(1)} %bitcast.137) | data formatting | bytes 12582912 | tf_op jit(solution)/shard_map/reshape | solution.py:287
  29.8 92.4 %all_to_all.10 = bf16[2,768,2048]{2,0,1:T(2,128)(2,1)S(1)} all-to-all(bf16[2,768,2048]{2,0,1:T(2,128)(2,1)S(1)} %copy.115), channel_id=1, replica_groups=mesh['outer'=8,'inner'=16] {'outer','inner'}, dimensions={1} | all-to-all | bytes 12582912 | tf_op jit(solution)/shard_map/all_to_all | solution.py:289
  122.2 2.6 copy-done.5
  124.8 5.4 %fusion.3 = f32[2,768,512]{2,1,0:T(8,128)} fusion(bf16[2,2048,512]{2,1,0:T(8,128)(2,1)S(1)} %copy-done.46, bf16[2,768,2048]{2,0,1:T(2,128)(2,1)S(1)} %all_to_all.10), kind=kOutput, calls=%fused_computation.6 | convolution fusion | flops 3221225472 | bytes 13631488 | tf_op jit(solution)/shard_map/esd,edf->esf/dot_general | solution.py:80
  130.1 16.8 %convolution_convert_fusion.1 = bf16[2,768,2048]{2,1,0:T(8,128)(2,1)} fusion(bf16[2,512,2048]{2,1,0:T(8,128)(2,1)} %param.20, f32[2,768,512]{2,1,0:T(8,128)} %fusion.3, bf16[2,2048,512]{2,1,0:T(8,128)(2,1)} %param.19, bf16[2,768,2048]{2,0,1:T(2,128)(2,1)} %copy-done.5), kind=kOutput, calls=%fused_computation.10 | convolution fusion | flops 6450315264 | bytes 24117248 | tf_op jit(solution)/shard_map/esf,efd->esd/dot_general | solution.py:83
  146.9 12.6 %copy.118 = bf16[2,768,2048]{2,0,1:T(2,128)(2,1)} copy(bf16[2,768,2048]{2,1,0:T(8,128)(2,1)} %convolution_convert_fusion.1) | data formatting | bytes 12582912 | tf_op jit(solution)/shard_map/convert_element_type | solution.py:85
  159.6 14.4 %all-to-all-start.1 = ((bf16[2,768,2048]{2,0,1:T(2,128)(2,1)}), bf16[2,768,2048]{2,0,1:T(2,128)(2,1)}, u32[]{:S(2)}, u32[]{:S(2)}) async-start(bf16[2,768,2048]{2,0,1:T(2,128)(2,1)} %copy.118), calls=%async_computation.1 | async-start | bytes 12582912 | tf_op jit(solution)/shard_map/all_to_all | solution.py:294
  175.1 1.2 select_reduce_fusion
  176.3 69.0 %all-to-all-done.1 = bf16[2,768,2048]{2,0,1:T(2,128)(2,1)} async-done(((bf16[2,768,2048]{2,0,1:T(2,128)(2,1)}), bf16[2,768,2048]{2,0,1:T(2,128)(2,1)}, u32[]{:S(2)}, u32[]{:S(2)}) %all-to-all-start.1) | async-done | bytes 6291488 | tf_op jit(solution)/shard_map/all_to_all | solution.py:294
  245.3 5.7 %copy.119 = bf16[2,768,2048]{2,1,0:T(8,128)(2,1)S(1)} copy(bf16[2,768,2048]{2,0,1:T(2,128)(2,1)} %all-to-all-done.1) | data formatting | bytes 12582912 | tf_op jit(solution)/shard_map/all_to_all | solution.py:294
  251.0 1.0 fusion.63
  252.1 1.4 fusion.21
  256.0 4.6 fusion.60
  260.7 4.7 fusion.5
  265.4 2.5 collective-permute-start.1
  268.6 2.0 collective-permute-done.1
  270.9 1.2 divide_multiply_fusion
  274.6 2.4 fusion.20
  279.1 1.4 fusion.32
  280.6 1.5 copy.123
  282.1 1.5 copy.122
  284.7 1.3 copy.138
  285.9 1.3 copy.139
  287.2 1.2 copy.126
  288.5 4.7 fusion.93
  293.2 4.9 convolution_negate_fusion.5
  299.2 1.9 fusion.53
  301.1 1.8 convolution_negate_fusion.4
  304.4 1.0 convolution_negate_fusion.3
  308.3 1.1 convolution_negate_fusion.1
  309.7 1.1 slice_bitcast_fusion
  313.6 1.3 copy.128
  314.9 2.6 copy.129
  318.2 1.3 fusion.58
  319.5 1.3 fusion.27
  320.9 2.3 convolution_multiply_fusion
  323.2 1.9 fusion.100.state_ref
  325.2 2.0 convolution_subtract_fusion.1.map_ref
  327.2 166.5 %shard_map.149 = f32[16,128,128]{2,1,0:T(8,128)S(1)} custom-call(f32[16,128,128]{2,1,0:T(8,128)S(1)} %convolution_subtract_fusion.1.map_ref, f32[16,128,128]{2,1,0:T(8,128)S(1)} %fusion.100.state_ref), custom_call_target="tpu_custom_call" | custom-call | tf_op jit(solution)/shard_map/pallas_call | solution.py:217
  493.7 1.2 convolution_subtract_fusion
  494.9 1.8 fusion.17
  496.8 1.9 multiply_reduce_fusion
  498.9 1.0 copy.133
  (162 shorter events, 22.2 us)
Async XLA Ops:
  7.2 1.2 copy-start
  7.2 7.6 %copy-start.6 = (bf16[128,2048]{1,0:T(8,128)(2,1)S(1)}, bf16[128,2048]{1,0:T(8,128)(2,1)}, u32[]{:S(2)}) copy-start(bf16[128,2048]{1,0:T(8,128)(2,1)} %param.14) | copy-start | bytes 1572868
  7.2 7.6 %copy-start.41 = (f32[2048]{0:T(1024)S(1)}, f32[2048]{0:T(1024)}, u32[]{:S(2)}) copy-start(f32[2048]{0:T(1024)} %param.17) | copy-start | bytes 24580
  7.2 166.8 %all-gather.2.cloned.1.call-start = ((), (), s32[]{:S(2)}) async-start(), calls=%async_computation.2 | async-start | bytes 8912896 | tf_op jit(solution)/shard_map/all_gather | solution.py:263
  29.8 95.0 %copy-start.46 = (bf16[2,2048,512]{2,1,0:T(8,128)(2,1)S(1)}, bf16[2,2048,512]{2,1,0:T(8,128)(2,1)}, u32[]{:S(2)}) copy-start(bf16[2,2048,512]{2,1,0:T(8,128)(2,1)} %param.18) | copy-start | bytes 12582916
  122.2 2.6 copy-start.5
  159.6 15.4 %copy-start.40 = (f32[128,10]{0,1:T(8,128)S(1)}, f32[128,10]{0,1:T(8,128)}, u32[]{:S(2)}) copy-start(f32[128,10]{0,1:T(8,128)} %param.16) | copy-start | bytes 15364
  159.6 15.5 %copy-start.47 = (f32[16]{0:T(128)S(1)}, f32[16]{0:T(128)}, u32[]{:S(2)}) copy-start(f32[16]{0:T(128)} %param.25) | copy-start | bytes 196
  159.6 16.7 %copy-start.35 = (bf16[4,4096]{1,0:T(4,128)(2,1)S(1)}, bf16[4,4096]{1,0:T(4,128)(2,1)}, u32[]{:S(2)}) copy-start(bf16[4,4096]{1,0:T(4,128)(2,1)} %param.24) | copy-start | bytes 98308
  159.6 85.8 %all-to-all-start.1 = ((bf16[2,768,2048]{2,0,1:T(2,128)(2,1)}), bf16[2,768,2048]{2,0,1:T(2,128)(2,1)}, u32[]{:S(2)}, u32[]{:S(2)}) async-start(bf16[2,768,2048]{2,0,1:T(2,128)(2,1)} %copy.118), calls=%async_computation.1 | async-start | bytes 12582912 | tf_op jit(solution)/shard_map/all_to_all | solution.py:294
  174.0 86.7 %collective-permute-start = (bf16[1024,4096]{1,0:T(8,128)(2,1)}, bf16[1024,4096]{1,0:T(8,128)(2,1)}, u32[]{:S(2)}, u32[]{:S(2)}) collective-permute-start(bf16[1024,4096]{1,0:T(8,128)(2,1)} %all-gather.2.cloned.1.call-done), channel_id=1, source_target_pairs={{0,16},{16,0},{32,48},{48,32},{64,80},{80,64},{96,112},{112,96},{1... | collective-permute-start | bytes 25165832 | tf_op jit(solution)/shard_map/ppermute | solution.py:264
  175.0 99.6 %copy-start.33 = (pred[128,128]{1,0:T(8,128)(4,1)}, pred[128,128]{1,0:T(8,128)(4,1)S(1)}, u32[]{:S(2)}) copy-start(pred[128,128]{1,0:T(8,128)(4,1)S(1)} %get-tuple-element.57) | copy-start | bytes 49156
  252.1 2.2 copy-start.42
  252.1 2.4 copy-start.36
  252.1 2.7 copy-start.44
  265.4 5.2 %collective-permute-start.1 = (bf16[3,4096]{1,0:T(4,128)(2,1)S(1)}, bf16[3,4096]{1,0:T(4,128)(2,1)S(1)}, u32[]{:S(2)}, u32[]{:S(2)}) collective-permute-start(bf16[3,4096]{1,0:T(4,128)(2,1)S(1)} %slice.191), channel_id=1, source_target_pairs={{0,1},{1,2},{2,3},{3,4},{4,5},{5,6},{6,7},{7,8},{8,9},{9,10},{10,1... | collective-permute-start | bytes 73736 | tf_op jit(solution)/shard_map/ppermute | solution.py:13
  272.2 39.2 %copy-start.2 = (f32[128,4096]{1,0:T(8,128)}, f32[128,4096]{1,0:T(8,128)S(1)}, u32[]{:S(2)}) copy-start(f32[128,4096]{1,0:T(8,128)S(1)} %divide_multiply_fusion) | copy-start | bytes 6291460
  277.0 1.0 copy-start.3
  277.2 1.1 copy-start.13
  277.5 1.1 copy-start.15
  277.5 1.2 copy-start.17
  278.0 1.0 copy-start.21
  278.3 2.2 copy-start.25
  288.5 9.7 %copy-start.29 = (f32[1,2,2,2,2,2,16,2,2]{8,7,6,5,4,3,2,1,0:T(2,128)S(1)}, f32[1,2,2,2,2,2,16,2,2]{8,7,6,5,4,3,2,1,0:T(2,128)}, u32[]{:S(2)}) copy-start(f32[1,2,2,2,2,2,16,2,2]{8,7,6,5,4,3,2,1,0:T(2,128)} %copy.138) | copy-start | bytes 24580
  288.5 9.7 %copy-start.30 = (f32[1,2,2,2,2,2,16,2,2]{8,7,6,5,4,3,2,1,0:T(2,128)S(1)}, f32[1,2,2,2,2,2,16,2,2]{8,7,6,5,4,3,2,1,0:T(2,128)}, u32[]{:S(2)}) copy-start(f32[1,2,2,2,2,2,16,2,2]{8,7,6,5,4,3,2,1,0:T(2,128)} %copy.139) | copy-start | bytes 24580
  293.2 6.0 %copy-start.24 = (f32[1,2,2,2,16,8,8]{6,5,4,3,2,1,0:T(8,128)S(1)}, f32[1,2,2,2,16,8,8]{6,5,4,3,2,1,0:T(8,128)}, u32[]{:S(2)}) copy-start(f32[1,2,2,2,16,8,8]{6,5,4,3,2,1,0:T(8,128)} %copy-done.23) | copy-start | bytes 98308
  293.2 6.0 %copy-start.26 = (f32[1,2,2,2,16,8,8]{6,5,4,3,2,1,0:T(8,128)S(1)}, f32[1,2,2,2,16,8,8]{6,5,4,3,2,1,0:T(8,128)}, u32[]{:S(2)}) copy-start(f32[1,2,2,2,16,8,8]{6,5,4,3,2,1,0:T(8,128)} %copy-done.25) | copy-start | bytes 98308
  301.1 2.3 copy-start.20
  301.1 2.3 copy-start.22
  304.4 1.3 copy-start.16
  304.4 1.3 copy-start.18
  306.4 1.0 copy-start.12
  306.4 1.2 copy-start.14
  308.3 2.4 copy-start.4
  309.6 1.8 copy-start.32
  311.4 2.1 slice-start
  312.9 4.6 copy-start.8
  312.9 4.6 copy-start.38
  312.9 4.6 copy-start.39
  314.9 3.3 copy-start.9
  314.9 3.3 copy-start.10
  317.5 1.9 copy-start.27
  318.1 2.6 copy-start.28
  319.5 1.4 copy-start.34
  320.9 4.3 copy-start.43
  327.2 167.7 %copy-start.37 = (f32[128,16]{0,1:T(8,128)S(1)}, f32[128,16]{0,1:T(8,128)}, u32[]{:S(2)}) copy-start(f32[128,16]{0,1:T(8,128)} %get-tuple-element.49) | copy-start | bytes 24580
  494.9 3.8 copy-start.45
  494.9 5.0 copy-start.1
  (5 other events, 4.2 us)
Sparse Core Ops, SparseCore 0:
  10.7 135.4 all-gather.1

commit v7 on v6

--- a/solution.py
+++ b/solution.py
@@ -212,7 +212,7 @@
     rounds = 1
     while (1 << (rounds - 1)) < count:
         rounds += 1
-    groups = 4
+    groups = 8
     block = pltpu.VMEM((rounds, heads, size, width), jnp.bfloat16)
     return pl.pallas_call(
         functools.partial(scan_kernel, count, axes, groups),

time: 512 us -> 514 us (level)
  no operation moved by 1% of the time
where the time goes in v7:
time: 514 us; the launch traced here: 506 us
  Pallas kernels  166 us (32%)
  blocking collectives  92.4 us (18%)
  matrix products  71.8 us (14%)
  waiting for transfers between devices  71.1 us (14%)
  local copies, waits for them, and re-layouts  55.6 us (11%)
  starting transfers between devices  17.8 us (3%)
  other arithmetic  16.4 us (3%)
  between operations  15.3 us (3%)
    pallas_call x1, Pallas kernels, chained_state(): pl.pallas_call(functools.partial(scan_kernel, count, axes, groups), out_s...  166 us
    all_to_all x1, blocking collectives, per_device(): lax.all_to_all(outgoing, ('outer', 'inner'), split_axis=1, concat_axis=1,...  92.4 us
    all_to_all x1, waiting for transfers between devices, per_device(): lax.all_to_all(served, ('outer', 'inner'), split_axis=1, concat_axis=1, t...  69 us
    dot_general x1, matrix products, run_experts(): jnp.einsum('esf,efd->esd', hidden, down_weight, preferred_element_type=jn...  16.8 us
    all_to_all x1, starting transfers between devices, per_device(): lax.all_to_all(served, ('outer', 'inner'), split_axis=1, concat_axis=1, t...  14.4 us
    reshape x1, local copies, waits for them, and re-layouts, per_device(): outgoing = outgoing.reshape(local_experts, n_dev * capacity, width)  13 us
    convert_element_type x1, local copies, waits for them, and re-layouts, run_experts(): return jnp.einsum('esf,efd->esd', hidden, down_weight, preferred_element_...  12.6 us
    unnamed x102, local copies, waits for them, and re-layouts  11.5 us
  transfers between devices with their start and end apart: 4, of which 2 were waited for; matrix products, arithmetic and copies ran while one was open for 14% of the time, Pallas kernels for 0%

profile of v7, /device:TPU:83, one launch (start us, length us, event | category | flops | bytes accessed | tf_op | source)
XLA Modules:
  0.0 506.5 jit_solution(5856016327426905036)
XLA Ops:
  7.3 1.1 copy-done
  10.4 1.2 fusion.24
  11.6 1.1 select_reduce_fusion.1
  13.5 1.3 fusion
  14.8 1.9 convolution_convert_fusion
  16.7 13.0 %copy.115 = bf16[2,768,2048]{2,0,1:T(2,128)(2,1)S(1)} copy(bf16[2,768,2048]{2,1,0:T(8,128)(2,1)S(1)} %bitcast.137) | data formatting | bytes 12582912 | tf_op jit(solution)/shard_map/reshape | solution.py:287
  29.8 92.4 %all_to_all.10 = bf16[2,768,2048]{2,0,1:T(2,128)(2,1)S(1)} all-to-all(bf16[2,768,2048]{2,0,1:T(2,128)(2,1)S(1)} %copy.115), channel_id=1, replica_groups=mesh['outer'=8,'inner'=16] {'outer','inner'}, dimensions={1} | all-to-all | bytes 12582912 | tf_op jit(solution)/shard_map/all_to_all | solution.py:289
  122.2 2.6 copy-done.5
  124.8 5.4 %fusion.3 = f32[2,768,512]{2,1,0:T(8,128)} fusion(bf16[2,2048,512]{2,1,0:T(8,128)(2,1)S(1)} %copy-done.46, bf16[2,768,2048]{2,0,1:T(2,128)(2,1)S(1)} %all_to_all.10), kind=kOutput, calls=%fused_computation.6 | convolution fusion | flops 3221225472 | bytes 13631488 | tf_op jit(solution)/shard_map/esd,edf->esf/dot_general | solution.py:80
  130.1 16.8 %convolution_convert_fusion.1 = bf16[2,768,2048]{2,1,0:T(8,128)(2,1)} fusion(bf16[2,512,2048]{2,1,0:T(8,128)(2,1)} %param.20, f32[2,768,512]{2,1,0:T(8,128)} %fusion.3, bf16[2,2048,512]{2,1,0:T(8,128)(2,1)} %param.19, bf16[2,768,2048]{2,0,1:T(2,128)(2,1)} %copy-done.5), kind=kOutput, calls=%fused_computation.10 | convolution fusion | flops 6450315264 | bytes 24117248 | tf_op jit(solution)/shard_map/esf,efd->esd/dot_general | solution.py:83
  146.9 12.6 %copy.118 = bf16[2,768,2048]{2,0,1:T(2,128)(2,1)} copy(bf16[2,768,2048]{2,1,0:T(8,128)(2,1)} %convolution_convert_fusion.1) | data formatting | bytes 12582912 | tf_op jit(solution)/shard_map/convert_element_type | solution.py:85
  159.6 14.4 %all-to-all-start.1 = ((bf16[2,768,2048]{2,0,1:T(2,128)(2,1)}), bf16[2,768,2048]{2,0,1:T(2,128)(2,1)}, u32[]{:S(2)}, u32[]{:S(2)}) async-start(bf16[2,768,2048]{2,0,1:T(2,128)(2,1)} %copy.118), calls=%async_computation.1 | async-start | bytes 12582912 | tf_op jit(solution)/shard_map/all_to_all | solution.py:294
  175.1 1.2 select_reduce_fusion
  176.3 69.0 %all-to-all-done.1 = bf16[2,768,2048]{2,0,1:T(2,128)(2,1)} async-done(((bf16[2,768,2048]{2,0,1:T(2,128)(2,1)}), bf16[2,768,2048]{2,0,1:T(2,128)(2,1)}, u32[]{:S(2)}, u32[]{:S(2)}) %all-to-all-start.1) | async-done | bytes 6291488 | tf_op jit(solution)/shard_map/all_to_all | solution.py:294
  245.3 5.7 %copy.119 = bf16[2,768,2048]{2,1,0:T(8,128)(2,1)S(1)} copy(bf16[2,768,2048]{2,0,1:T(2,128)(2,1)} %all-to-all-done.1) | data formatting | bytes 12582912 | tf_op jit(solution)/shard_map/all_to_all | solution.py:294
  251.0 1.0 fusion.63
  252.1 1.4 fusion.21
  256.0 4.6 fusion.60
  260.7 4.7 fusion.5
  265.4 2.5 collective-permute-start.1
  268.6 2.0 collective-permute-done.1
  270.9 1.2 divide_multiply_fusion
  274.6 2.4 fusion.20
  279.1 1.4 fusion.32
  280.6 1.5 copy.123
  282.1 1.5 copy.122
  284.7 1.3 copy.138
  285.9 1.3 copy.139
  287.2 1.2 copy.126
  288.5 4.7 fusion.93
  293.2 4.9 convolution_negate_fusion.5
  299.2 1.9 fusion.53
  301.1 1.8 convolution_negate_fusion.4
  304.4 1.0 convolution_negate_fusion.3
  308.3 1.1 convolution_negate_fusion.1
  309.7 1.1 slice_bitcast_fusion
  313.6 1.3 copy.128
  314.9 2.6 copy.129
  318.2 1.3 fusion.58
  319.5 1.3 fusion.27
  320.9 2.3 convolution_multiply_fusion
  323.2 1.9 fusion.100.state_ref
  325.2 2.0 convolution_subtract_fusion.1.map_ref
  327.2 166.0 %shard_map.149 = f32[16,128,128]{2,1,0:T(8,128)S(1)} custom-call(f32[16,128,128]{2,1,0:T(8,128)S(1)} %convolution_subtract_fusion.1.map_ref, f32[16,128,128]{2,1,0:T(8,128)S(1)} %fusion.100.state_ref), custom_call_target="tpu_custom_call" | custom-call | tf_op jit(solution)/shard_map/pallas_call | solution.py:217
  493.2 1.2 convolution_subtract_fusion
  494.4 1.8 fusion.17
  496.3 1.9 multiply_reduce_fusion
  498.4 1.0 copy.133
  (162 shorter events, 22.2 us)
Async XLA Ops:
  7.2 1.2 copy-start
  7.2 7.6 %copy-start.6 = (bf16[128,2048]{1,0:T(8,128)(2,1)S(1)}, bf16[128,2048]{1,0:T(8,128)(2,1)}, u32[]{:S(2)}) copy-start(bf16[128,2048]{1,0:T(8,128)(2,1)} %param.14) | copy-start | bytes 1572868
  7.2 7.6 %copy-start.41 = (f32[2048]{0:T(1024)S(1)}, f32[2048]{0:T(1024)}, u32[]{:S(2)}) copy-start(f32[2048]{0:T(1024)} %param.17) | copy-start | bytes 24580
  7.2 166.8 %all-gather.2.cloned.1.call-start = ((), (), s32[]{:S(2)}) async-start(), calls=%async_computation.2 | async-start | bytes 8912896 | tf_op jit(solution)/shard_map/all_gather | solution.py:263
  29.8 95.0 %copy-start.46 = (bf16[2,2048,512]{2,1,0:T(8,128)(2,1)S(1)}, bf16[2,2048,512]{2,1,0:T(8,128)(2,1)}, u32[]{:S(2)}) copy-start(bf16[2,2048,512]{2,1,0:T(8,128)(2,1)} %param.18) | copy-start | bytes 12582916
  122.2 2.6 copy-start.5
  159.6 15.4 %copy-start.40 = (f32[128,10]{0,1:T(8,128)S(1)}, f32[128,10]{0,1:T(8,128)}, u32[]{:S(2)}) copy-start(f32[128,10]{0,1:T(8,128)} %param.16) | copy-start | bytes 15364
  159.6 15.5 %copy-start.47 = (f32[16]{0:T(128)S(1)}, f32[16]{0:T(128)}, u32[]{:S(2)}) copy-start(f32[16]{0:T(128)} %param.25) | copy-start | bytes 196
  159.6 16.7 %copy-start.35 = (bf16[4,4096]{1,0:T(4,128)(2,1)S(1)}, bf16[4,4096]{1,0:T(4,128)(2,1)}, u32[]{:S(2)}) copy-start(bf16[4,4096]{1,0:T(4,128)(2,1)} %param.24) | copy-start | bytes 98308
  159.6 85.8 %all-to-all-start.1 = ((bf16[2,768,2048]{2,0,1:T(2,128)(2,1)}), bf16[2,768,2048]{2,0,1:T(2,128)(2,1)}, u32[]{:S(2)}, u32[]{:S(2)}) async-start(bf16[2,768,2048]{2,0,1:T(2,128)(2,1)} %copy.118), calls=%async_computation.1 | async-start | bytes 12582912 | tf_op jit(solution)/shard_map/all_to_all | solution.py:294
  174.0 86.7 %collective-permute-start = (bf16[1024,4096]{1,0:T(8,128)(2,1)}, bf16[1024,4096]{1,0:T(8,128)(2,1)}, u32[]{:S(2)}, u32[]{:S(2)}) collective-permute-start(bf16[1024,4096]{1,0:T(8,128)(2,1)} %all-gather.2.cloned.1.call-done), channel_id=1, source_target_pairs={{0,16},{16,0},{32,48},{48,32},{64,80},{80,64},{96,112},{112,96},{1... | collective-permute-start | bytes 25165832 | tf_op jit(solution)/shard_map/ppermute | solution.py:264
  175.0 99.6 %copy-start.33 = (pred[128,128]{1,0:T(8,128)(4,1)}, pred[128,128]{1,0:T(8,128)(4,1)S(1)}, u32[]{:S(2)}) copy-start(pred[128,128]{1,0:T(8,128)(4,1)S(1)} %get-tuple-element.57) | copy-start | bytes 49156
  252.1 2.2 copy-start.42
  252.1 2.4 copy-start.36
  252.1 2.7 copy-start.44
  265.4 5.2 %collective-permute-start.1 = (bf16[3,4096]{1,0:T(4,128)(2,1)S(1)}, bf16[3,4096]{1,0:T(4,128)(2,1)S(1)}, u32[]{:S(2)}, u32[]{:S(2)}) collective-permute-start(bf16[3,4096]{1,0:T(4,128)(2,1)S(1)} %slice.191), channel_id=1, source_target_pairs={{0,1},{1,2},{2,3},{3,4},{4,5},{5,6},{6,7},{7,8},{8,9},{9,10},{10,1... | collective-permute-start | bytes 73736 | tf_op jit(solution)/shard_map/ppermute | solution.py:13
  272.2 39.2 %copy-start.2 = (f32[128,4096]{1,0:T(8,128)}, f32[128,4096]{1,0:T(8,128)S(1)}, u32[]{:S(2)}) copy-start(f32[128,4096]{1,0:T(8,128)S(1)} %divide_multiply_fusion) | copy-start | bytes 6291460
  277.0 1.0 copy-start.3
  277.2 1.1 copy-start.13
  277.5 1.1 copy-start.15
  277.5 1.2 copy-start.17
  278.0 1.0 copy-start.21
  278.3 2.2 copy-start.25
  288.5 9.7 %copy-start.29 = (f32[1,2,2,2,2,2,16,2,2]{8,7,6,5,4,3,2,1,0:T(2,128)S(1)}, f32[1,2,2,2,2,2,16,2,2]{8,7,6,5,4,3,2,1,0:T(2,128)}, u32[]{:S(2)}) copy-start(f32[1,2,2,2,2,2,16,2,2]{8,7,6,5,4,3,2,1,0:T(2,128)} %copy.138) | copy-start | bytes 24580
  288.5 9.7 %copy-start.30 = (f32[1,2,2,2,2,2,16,2,2]{8,7,6,5,4,3,2,1,0:T(2,128)S(1)}, f32[1,2,2,2,2,2,16,2,2]{8,7,6,5,4,3,2,1,0:T(2,128)}, u32[]{:S(2)}) copy-start(f32[1,2,2,2,2,2,16,2,2]{8,7,6,5,4,3,2,1,0:T(2,128)} %copy.139) | copy-start | bytes 24580
  293.2 6.0 %copy-start.24 = (f32[1,2,2,2,16,8,8]{6,5,4,3,2,1,0:T(8,128)S(1)}, f32[1,2,2,2,16,8,8]{6,5,4,3,2,1,0:T(8,128)}, u32[]{:S(2)}) copy-start(f32[1,2,2,2,16,8,8]{6,5,4,3,2,1,0:T(8,128)} %copy-done.23) | copy-start | bytes 98308
  293.2 6.0 %copy-start.26 = (f32[1,2,2,2,16,8,8]{6,5,4,3,2,1,0:T(8,128)S(1)}, f32[1,2,2,2,16,8,8]{6,5,4,3,2,1,0:T(8,128)}, u32[]{:S(2)}) copy-start(f32[1,2,2,2,16,8,8]{6,5,4,3,2,1,0:T(8,128)} %copy-done.25) | copy-start | bytes 98308
  301.1 2.3 copy-start.20
  301.1 2.3 copy-start.22
  304.4 1.3 copy-start.16
  304.4 1.3 copy-start.18
  306.4 1.0 copy-start.12
  306.4 1.2 copy-start.14
  308.3 2.4 copy-start.4
  309.6 1.8 copy-start.32
  311.4 2.1 slice-start
  312.9 4.6 copy-start.8
  312.9 4.6 copy-start.38
  312.9 4.6 copy-start.39
  314.9 3.3 copy-start.9
  314.9 3.3 copy-start.10
  317.5 1.9 copy-start.27
  318.1 2.6 copy-start.28
  319.5 1.4 copy-start.34
  320.9 4.3 copy-start.43
  327.2 167.2 %copy-start.37 = (f32[128,16]{0,1:T(8,128)S(1)}, f32[128,16]{0,1:T(8,128)}, u32[]{:S(2)}) copy-start(f32[128,16]{0,1:T(8,128)} %get-tuple-element.49) | copy-start | bytes 24580
  494.4 3.8 copy-start.45
  494.4 5.0 copy-start.1
  (5 other events, 4.2 us)
Sparse Core Ops, SparseCore 0:
  10.7 135.4 all-gather.1

commit v8 on v6

--- a/solution.py
+++ b/solution.py
@@ -95,8 +95,8 @@
     corner = -jnp.einsum(
         "...ij,...jk->...ik",
         second,
-        jnp.einsum("...ij,...jk->...ik", system[..., half:, :half], first, precision=lax.Precision.HIGHEST),
-        precision=lax.Precision.HIGHEST,
+        jnp.einsum("...ij,...jk->...ik", system[..., half:, :half], first, precision=lax.Precision.HIGH),
+        precision=lax.Precision.HIGH,
     )
     top = jnp.concatenate([first, jnp.zeros_like(first)], axis=-1)
     bottom = jnp.concatenate([corner, second], axis=-1)
@@ -348,7 +348,7 @@
     key_major = keys.transpose(1, 0, 2)
     query_leading = queries.transpose(1, 0, 2)
     value_major = values.transpose(1, 0, 2)
-    key_inner = jnp.einsum("htd,hid->hti", key_major, key_major, precision=lax.Precision.HIGHEST)
+    key_inner = jnp.einsum("htd,hid->hti", key_major, key_major, precision=lax.Precision.HIGH)
     lower_part = jnp.where(lower_strict, decay_mat * key_inner, 0.0) * strength[:, :, None]
     system = lower_part + jnp.eye(tok_count, dtype=jnp.float32)
     growth = jnp.exp(cumulative)
@@ -356,10 +356,10 @@
     scaled_values = value_major * strength[:, :, None]
     inverse = unit_lower_inverse(system)
     key_resolved = jnp.einsum(
-        "hts,hsd->htd", inverse, scaled_keys, precision=lax.Precision.HIGHEST
+        "hts,hsd->htd", inverse, scaled_keys, precision=lax.Precision.HIGH
     )
     value_resolved = jnp.einsum(
-        "hts,hsd->htd", inverse, scaled_values, precision=lax.Precision.HIGHEST
+        "hts,hsd->htd", inverse, scaled_values, precision=lax.Precision.HIGH
     )
     tail = jnp.exp(cumulative[:, -1:] - cumulative)
     trailing_keys = key_major * tail[:, :, None]
@@ -367,25 +367,25 @@
         jnp.eye(head_dim, dtype=jnp.float32), (value_heads, head_dim, head_dim)
     )
     state_map = growth[:, -1][:, None, None] * eye_heads - jnp.einsum(
-        "htk,htj->hkj", trailing_keys, key_resolved, precision=lax.Precision.HIGHEST
+        "htk,htj->hkj", trailing_keys, key_resolved, precision=lax.Precision.HIGH
     )
     state_increment = jnp.einsum(
-        "xbe,xbz->xez", trailing_keys, value_resolved, precision=lax.Precision.HIGHEST
+        "xbe,xbz->xez", trailing_keys, value_resolved, precision=lax.Precision.HIGH
     )
     initial_state = chained_state(state_map, state_increment, ("outer", "inner"), n_dev)
     updates = value_resolved - jnp.einsum(
-        "mwx,mxd->mwd", key_resolved, initial_state, precision=lax.Precision.HIGHEST
+        "mwx,mxd->mwd", key_resolved, initial_state, precision=lax.Precision.HIGH
     )
     query_key = (
-        jnp.einsum("htd,hid->hti", query_leading, key_major, precision=lax.Precision.HIGHEST)
+        jnp.einsum("htd,hid->hti", query_leading, key_major, precision=lax.Precision.HIGH)
         * decay_mat
     )
     carried = (
-        jnp.einsum("mwx,mxd->mwd", query_leading, initial_state, precision=lax.Precision.HIGHEST)
+        jnp.einsum("mwx,mxd->mwd", query_leading, initial_state, precision=lax.Precision.HIGH)
         * growth[:, :, None]
     )
     attended = carried + jnp.einsum(
-        "hti,hiv->htv", query_key, updates, precision=lax.Precision.HIGHEST
+        "hti,hiv->htv", query_key, updates, precision=lax.Precision.HIGH
     )
     attended = attended.transpose(1, 0, 2)
     core_out = (

time: 512 us -> 497 us (0.971)
  matrix products: 71.8 us -> 56.7 us
  transfers between devices with their start and end apart: 4 -> 4, of which waited for: 2 -> 2; matrix products, arithmetic and copies ran while one was open for 14% -> 15% of each run, Pallas kernels for 0% -> 0%
where the time goes in v8:
time: 497 us; the launch traced here: 492 us
  Pallas kernels  166 us (33%)
  blocking collectives  92.3 us (19%)
  waiting for transfers between devices  71.1 us (14%)
  matrix products  56.7 us (11%)
  local copies, waits for them, and re-layouts  56.2 us (11%)
  starting transfers between devices  17.8 us (4%)
  other arithmetic  16.4 us (3%)
  between operations  15.3 us (3%)
    pallas_call x1, Pallas kernels, chained_state(): pl.pallas_call(functools.partial(scan_kernel, count, axes, groups), out_s...  166 us
    all_to_all x1, blocking collectives, per_device(): lax.all_to_all(outgoing, ('outer', 'inner'), split_axis=1, concat_axis=1,...  92.3 us
    all_to_all x1, waiting for transfers between devices, per_device(): lax.all_to_all(served, ('outer', 'inner'), split_axis=1, concat_axis=1, t...  69.3 us
    dot_general x1, matrix products, run_experts(): jnp.einsum('esf,efd->esd', hidden, down_weight, preferred_element_type=jn...  16.8 us
    all_to_all x1, starting transfers between devices, per_device(): lax.all_to_all(served, ('outer', 'inner'), split_axis=1, concat_axis=1, t...  14.4 us
    reshape x1, local copies, waits for them, and re-layouts, per_device(): outgoing = outgoing.reshape(local_experts, n_dev * capacity, width)  13 us
    convert_element_type x1, local copies, waits for them, and re-layouts, run_experts(): return jnp.einsum('esf,efd->esd', hidden, down_weight, preferred_element_...  12.6 us
    unnamed x102, local copies, waits for them, and re-layouts  12.1 us
  transfers between devices with their start and end apart: 4, of which 2 were waited for; matrix products, arithmetic and copies ran while one was open for 15% of the time, Pallas kernels for 0%

profile of v8, /device:TPU:83, one launch (start us, length us, event | category | flops | bytes accessed | tf_op | source)
XLA Modules:
  0.0 492.2 jit_solution(11090749946543722905)
XLA Ops:
  7.3 1.1 copy-done
  9.2 0.9 convert_reduce_fusion
  10.4 1.2 fusion.24
  11.6 1.1 select_reduce_fusion.1
  13.5 1.3 fusion
  14.8 1.9 convolution_convert_fusion
  16.7 13.0 %copy.115 = bf16[2,768,2048]{2,0,1:T(2,128)(2,1)S(1)} copy(bf16[2,768,2048]{2,1,0:T(8,128)(2,1)S(1)} %bitcast.137) | data formatting | bytes 12582912 | tf_op jit(solution)/shard_map/reshape | solution.py:287
  29.8 92.3 %all_to_all.10 = bf16[2,768,2048]{2,0,1:T(2,128)(2,1)S(1)} all-to-all(bf16[2,768,2048]{2,0,1:T(2,128)(2,1)S(1)} %copy.115), channel_id=1, replica_groups=mesh['outer'=8,'inner'=16] {'outer','inner'}, dimensions={1} | all-to-all | bytes 12582912 | tf_op jit(solution)/shard_map/all_to_all | solution.py:289
  122.1 2.6 copy-done.5
  124.7 5.4 %fusion.3 = f32[2,768,512]{2,1,0:T(8,128)} fusion(bf16[2,2048,512]{2,1,0:T(8,128)(2,1)S(1)} %copy-done.46, bf16[2,768,2048]{2,0,1:T(2,128)(2,1)S(1)} %all_to_all.10), kind=kOutput, calls=%fused_computation.6 | convolution fusion | flops 3221225472 | bytes 13631488 | tf_op jit(solution)/shard_map/esd,edf->esf/dot_general | solution.py:80
  130.0 16.8 %convolution_convert_fusion.1 = bf16[2,768,2048]{2,1,0:T(8,128)(2,1)} fusion(bf16[2,512,2048]{2,1,0:T(8,128)(2,1)} %param.20, f32[2,768,512]{2,1,0:T(8,128)} %fusion.3, bf16[2,2048,512]{2,1,0:T(8,128)(2,1)} %param.19, bf16[2,768,2048]{2,0,1:T(2,128)(2,1)} %copy-done.5), kind=kOutput, calls=%fused_computation.10 | convolution fusion | flops 6450315264 | bytes 24117248 | tf_op jit(solution)/shard_map/esf,efd->esd/dot_general | solution.py:83
  146.8 12.6 %copy.118 = bf16[2,768,2048]{2,0,1:T(2,128)(2,1)} copy(bf16[2,768,2048]{2,1,0:T(8,128)(2,1)} %convolution_convert_fusion.1) | data formatting | bytes 12582912 | tf_op jit(solution)/shard_map/convert_element_type | solution.py:85
  159.5 14.4 %all-to-all-start.1 = ((bf16[2,768,2048]{2,0,1:T(2,128)(2,1)}), bf16[2,768,2048]{2,0,1:T(2,128)(2,1)}, u32[]{:S(2)}, u32[]{:S(2)}) async-start(bf16[2,768,2048]{2,0,1:T(2,128)(2,1)} %copy.118), calls=%async_computation.1 | async-start | bytes 12582912 | tf_op jit(solution)/shard_map/all_to_all | solution.py:294
  174.6 1.2 select_reduce_fusion
  175.9 69.3 %all-to-all-done.1 = bf16[2,768,2048]{2,0,1:T(2,128)(2,1)} async-done(((bf16[2,768,2048]{2,0,1:T(2,128)(2,1)}), bf16[2,768,2048]{2,0,1:T(2,128)(2,1)}, u32[]{:S(2)}, u32[]{:S(2)}) %all-to-all-start.1) | async-done | bytes 6291488 | tf_op jit(solution)/shard_map/all_to_all | solution.py:294
  245.2 5.7 %copy.119 = bf16[2,768,2048]{2,1,0:T(8,128)(2,1)S(1)} copy(bf16[2,768,2048]{2,0,1:T(2,128)(2,1)} %all-to-all-done.1) | data formatting | bytes 12582912 | tf_op jit(solution)/shard_map/all_to_all | solution.py:294
  250.9 1.0 fusion.63
  252.0 1.4 fusion.21
  255.9 4.6 fusion.60
  260.6 4.7 fusion.5
  265.3 2.7 collective-permute-start.1
  268.7 1.7 collective-permute-done.1
  270.8 1.2 divide_multiply_fusion
  272.0 0.9 slice_bitcast_fusion.12
  274.4 1.3 fusion.20
  277.9 1.4 fusion.32
  279.3 1.5 copy.123
  280.8 1.5 copy.122
  282.5 0.9 fusion.65
  283.4 1.3 copy.138
  284.7 1.3 copy.139
  286.0 1.2 copy.126
  287.2 3.1 fusion.93
  290.3 3.0 convolution_negate_fusion.5
  293.3 0.9 select_maximum_fusion.5
  294.4 1.0 fusion.53
  295.4 1.2 convolution_negate_fusion.4
  301.5 1.1 slice_bitcast_fusion
  303.6 0.9 copy.120
  304.9 1.3 copy.128
  306.2 2.6 copy.129
  311.3 1.2 convolution_multiply_fusion
  312.6 1.0 fusion.100.state_ref
  313.6 1.1 convolution_subtract_fusion.1.map_ref
  314.8 166.4 %shard_map.149 = f32[16,128,128]{2,1,0:T(8,128)S(1)} custom-call(f32[16,128,128]{2,1,0:T(8,128)S(1)} %convolution_subtract_fusion.1.map_ref, f32[16,128,128]{2,1,0:T(8,128)S(1)} %fusion.100.state_ref), custom_call_target="tpu_custom_call" | custom-call | tf_op jit(solution)/shard_map/pallas_call | solution.py:217
  481.9 1.0 fusion.17
  482.9 1.1 multiply_reduce_fusion
  484.1 1.0 copy.133
  (162 shorter events, 19.3 us)
Async XLA Ops:
  7.2 1.2 copy-start
  7.2 7.6 %copy-start.6 = (bf16[128,2048]{1,0:T(8,128)(2,1)S(1)}, bf16[128,2048]{1,0:T(8,128)(2,1)}, u32[]{:S(2)}) copy-start(bf16[128,2048]{1,0:T(8,128)(2,1)} %param.14) | copy-start | bytes 1572868
  7.2 7.6 %copy-start.41 = (f32[2048]{0:T(1024)S(1)}, f32[2048]{0:T(1024)}, u32[]{:S(2)}) copy-start(f32[2048]{0:T(1024)} %param.17) | copy-start | bytes 24580
  7.2 166.7 %all-gather.2.cloned.1.call-start = ((), (), s32[]{:S(2)}) async-start(), calls=%async_computation.2 | async-start | bytes 8912896 | tf_op jit(solution)/shard_map/all_gather | solution.py:263
  29.8 94.9 %copy-start.46 = (bf16[2,2048,512]{2,1,0:T(8,128)(2,1)S(1)}, bf16[2,2048,512]{2,1,0:T(8,128)(2,1)}, u32[]{:S(2)}) copy-start(bf16[2,2048,512]{2,1,0:T(8,128)(2,1)} %param.18) | copy-start | bytes 12582916
  122.1 2.6 copy-start.5
  159.4 15.1 %copy-start.40 = (f32[128,10]{0,1:T(8,128)S(1)}, f32[128,10]{0,1:T(8,128)}, u32[]{:S(2)}) copy-start(f32[128,10]{0,1:T(8,128)} %param.16) | copy-start | bytes 15364
  159.4 15.2 %copy-start.47 = (f32[16]{0:T(128)S(1)}, f32[16]{0:T(128)}, u32[]{:S(2)}) copy-start(f32[16]{0:T(128)} %param.25) | copy-start | bytes 196
  159.4 16.4 %copy-start.35 = (bf16[4,4096]{1,0:T(4,128)(2,1)S(1)}, bf16[4,4096]{1,0:T(4,128)(2,1)}, u32[]{:S(2)}) copy-start(bf16[4,4096]{1,0:T(4,128)(2,1)} %param.24) | copy-start | bytes 98308
  159.5 85.8 %all-to-all-start.1 = ((bf16[2,768,2048]{2,0,1:T(2,128)(2,1)}), bf16[2,768,2048]{2,0,1:T(2,128)(2,1)}, u32[]{:S(2)}, u32[]{:S(2)}) async-start(bf16[2,768,2048]{2,0,1:T(2,128)(2,1)} %copy.118), calls=%async_computation.1 | async-start | bytes 12582912 | tf_op jit(solution)/shard_map/all_to_all | solution.py:294
  173.9 86.7 %collective-permute-start = (bf16[1024,4096]{1,0:T(8,128)(2,1)}, bf16[1024,4096]{1,0:T(8,128)(2,1)}, u32[]{:S(2)}, u32[]{:S(2)}) collective-permute-start(bf16[1024,4096]{1,0:T(8,128)(2,1)} %all-gather.2.cloned.1.call-done), channel_id=1, source_target_pairs={{0,16},{16,0},{32,48},{48,32},{64,80},{80,64},{96,112},{112,96},{1... | collective-permute-start | bytes 25165832 | tf_op jit(solution)/shard_map/ppermute | solution.py:264
  174.6 99.8 %copy-start.33 = (pred[128,128]{1,0:T(8,128)(4,1)}, pred[128,128]{1,0:T(8,128)(4,1)S(1)}, u32[]{:S(2)}) copy-start(pred[128,128]{1,0:T(8,128)(4,1)S(1)} %get-tuple-element.57) | copy-start | bytes 49156
  251.9 2.2 copy-start.42
  252.0 2.4 copy-start.36
  252.0 2.7 copy-start.44
  265.3 5.2 %collective-permute-start.1 = (bf16[3,4096]{1,0:T(4,128)(2,1)S(1)}, bf16[3,4096]{1,0:T(4,128)(2,1)S(1)}, u32[]{:S(2)}, u32[]{:S(2)}) collective-permute-start(bf16[3,4096]{1,0:T(4,128)(2,1)S(1)} %slice.191), channel_id=1, source_target_pairs={{0,1},{1,2},{2,3},{3,4},{4,5},{5,6},{6,7},{7,8},{8,9},{9,10},{10,1... | collective-permute-start | bytes 73736 | tf_op jit(solution)/shard_map/ppermute | solution.py:13
  272.0 31.0 %copy-start.2 = (f32[128,4096]{1,0:T(8,128)}, f32[128,4096]{1,0:T(8,128)S(1)}, u32[]{:S(2)}) copy-start(f32[128,4096]{1,0:T(8,128)S(1)} %divide_multiply_fusion) | copy-start | bytes 6291460
  275.8 1.0 copy-start.3
  276.0 1.1 copy-start.13
  276.2 1.1 copy-start.15
  276.2 1.2 copy-start.17
  276.8 1.0 copy-start.21
  277.1 2.2 copy-start.25
  287.2 6.1 %copy-start.29 = (f32[1,2,2,2,2,2,16,2,2]{8,7,6,5,4,3,2,1,0:T(2,128)S(1)}, f32[1,2,2,2,2,2,16,2,2]{8,7,6,5,4,3,2,1,0:T(2,128)}, u32[]{:S(2)}) copy-start(f32[1,2,2,2,2,2,16,2,2]{8,7,6,5,4,3,2,1,0:T(2,128)} %copy.138) | copy-start | bytes 24580
  287.2 6.1 %copy-start.30 = (f32[1,2,2,2,2,2,16,2,2]{8,7,6,5,4,3,2,1,0:T(2,128)S(1)}, f32[1,2,2,2,2,2,16,2,2]{8,7,6,5,4,3,2,1,0:T(2,128)}, u32[]{:S(2)}) copy-start(f32[1,2,2,2,2,2,16,2,2]{8,7,6,5,4,3,2,1,0:T(2,128)} %copy.139) | copy-start | bytes 24580
  290.3 4.1 copy-start.24
  290.3 4.1 copy-start.26
  295.4 1.7 copy-start.20
  295.4 1.7 copy-start.22
  297.7 1.0 copy-start.16
  297.7 1.2 copy-start.18
  299.3 1.0 copy-start.12
  299.3 1.2 copy-start.14
  300.9 1.8 copy-start.4
  301.5 1.5 copy-start.32
  303.0 1.8 slice-start
  304.5 4.3 copy-start.8
  304.5 4.3 copy-start.38
  304.5 4.3 copy-start.39
  306.2 3.3 copy-start.9
  306.2 3.3 copy-start.10
  308.8 1.4 copy-start.27
  309.5 1.7 copy-start.28
  310.3 1.0 copy-start.34
  311.3 2.3 copy-start.43
  314.8 167.1 %copy-start.37 = (f32[128,16]{0,1:T(8,128)S(1)}, f32[128,16]{0,1:T(8,128)}, u32[]{:S(2)}) copy-start(f32[128,16]{0,1:T(8,128)} %get-tuple-element.49) | copy-start | bytes 24580
  481.8 2.1 copy-start.45
  481.9 3.3 copy-start.1
  (5 other events, 4.2 us)
Sparse Core Ops, SparseCore 0:
  10.7 135.3 all-gather.1

commit v9 on v8

--- a/solution.py
+++ b/solution.py
@@ -87,20 +87,28 @@
 
 def unit_lower_inverse(system):
     size = system.shape[-1]
-    if size == 1:
-        return jnp.ones_like(system)
-    half = size // 2
-    both = unit_lower_inverse(jnp.stack([system[..., :half, :half], system[..., half:, half:]]))
-    first, second = both[0], both[1]
-    corner = -jnp.einsum(
-        "...ij,...jk->...ik",
-        second,
-        jnp.einsum("...ij,...jk->...ik", system[..., half:, :half], first, precision=lax.Precision.HIGH),
-        precision=lax.Precision.HIGH,
-    )
-    top = jnp.concatenate([first, jnp.zeros_like(first)], axis=-1)
-    bottom = jnp.concatenate([corner, second], axis=-1)
-    return jnp.concatenate([top, bottom], axis=-2)
+    rows = lax.broadcasted_iota(jnp.int32, (size, size), 0)
+    cols = lax.broadcasted_iota(jnp.int32, (size, size), 1)
+    lower = system - jnp.eye(size, dtype=system.dtype)
+    levels = size.bit_length() - 1
+
+    def level(number, inverse):
+        width = jnp.left_shift(1, number)
+        corner = (
+            (rows // (2 * width) == cols // (2 * width))
+            & ((rows // width) % 2 == 1)
+            & ((cols // width) % 2 == 0)
+        )
+        part = jnp.where(corner, lower, 0.0)
+        return inverse - jnp.einsum(
+            "...ij,...jk->...ik",
+            inverse,
+            jnp.einsum("...ij,...jk->...ik", part, inverse, precision=lax.Precision.HIGH),
+            precision=lax.Precision.HIGH,
+        )
+
+    start = jnp.broadcast_to(jnp.eye(size, dtype=system.dtype), system.shape)
+    return lax.fori_loop(0, levels, level, start)
 
 
 def join_maps(earlier, later):

time: 497 us -> 494 us (level)
  local copies, waits for them, and re-layouts: 56.2 us -> 46.2 us
    and x0 -> x7, other arithmetic: none -> 9.79 us  [level(): (rows // (2 * width) == cols // (2 * width)) & (rows // width % 2 == 1)]
    unnamed x102 -> x43, local copies, waits for them, and re-layouts: 12.1 us -> 6.6 us
    dot_general x12 -> x14, matrix products: 11.6 us -> 12.7 us  [the longest x7 8.46 us: level(): jnp.einsum('...ij,...jk->...ik', part, inverse, precision=lax.Precision.H...]
  transfers between devices with their start and end apart: 4 -> 4, of which waited for: 2 -> 2; matrix products, arithmetic and copies ran while one was open for 15% -> 14% of each run, Pallas kernels for 0% -> 0%
where the time goes in v9:
time: 494 us; the launch traced here: 489 us
  Pallas kernels  167 us (34%)
  blocking collectives  92.7 us (19%)
  waiting for transfers between devices  72.1 us (15%)
  matrix products  58.5 us (12%)
  local copies, waits for them, and re-layouts  46.2 us (9%)
  other arithmetic  20.4 us (4%)
  starting transfers between devices  17.3 us (4%)
  between operations  14.9 us (3%)
    pallas_call x1, Pallas kernels, chained_state(): pl.pallas_call(functools.partial(scan_kernel, count, axes, groups), out_s...  167 us
    all_to_all x1, blocking collectives, per_device(): lax.all_to_all(outgoing, ('outer', 'inner'), split_axis=1, concat_axis=1,...  92.7 us
    all_to_all x1, waiting for transfers between devices, per_device(): lax.all_to_all(served, ('outer', 'inner'), split_axis=1, concat_axis=1, t...  69.3 us
    dot_general x1, matrix products, run_experts(): jnp.einsum('esf,efd->esd', hidden, down_weight, preferred_element_type=jn...  16.8 us
    all_to_all x1, starting transfers between devices, per_device(): lax.all_to_all(served, ('outer', 'inner'), split_axis=1, concat_axis=1, t...  14.4 us
    reshape x1, local copies, waits for them, and re-layouts, per_device(): outgoing = outgoing.reshape(local_experts, n_dev * capacity, width)  13 us
    convert_element_type x1, local copies, waits for them, and re-layouts, run_experts(): return jnp.einsum('esf,efd->esd', hidden, down_weight, preferred_element_...  12.6 us
  transfers between devices with their start and end apart: 4, of which 2 were waited for; matrix products, arithmetic and copies ran while one was open for 14% of the time, Pallas kernels for 0%

profile of v9, /device:TPU:83, one launch (start us, length us, event | category | flops | bytes accessed | tf_op | source)
XLA Modules:
  0.0 489.3 jit_solution(9484362351352484474)
XLA Ops:
  7.3 1.1 copy-done
  10.4 1.2 fusion.58
  11.6 1.1 select_reduce_fusion.1
  13.5 1.3 fusion.33
  14.8 1.9 convolution_convert_fusion
  16.7 13.0 %copy.96 = bf16[2,768,2048]{2,0,1:T(2,128)(2,1)S(1)} copy(bf16[2,768,2048]{2,1,0:T(8,128)(2,1)S(1)} %bitcast.87) | data formatting | bytes 12582912 | tf_op jit(solution)/shard_map/reshape | solution.py:295
  29.8 92.7 %all_to_all.10 = bf16[2,768,2048]{2,0,1:T(2,128)(2,1)S(1)} all-to-all(bf16[2,768,2048]{2,0,1:T(2,128)(2,1)S(1)} %copy.96), channel_id=1, replica_groups=mesh['outer'=8,'inner'=16] {'outer','inner'}, dimensions={1} | all-to-all | bytes 12582912 | tf_op jit(solution)/shard_map/all_to_all | solution.py:297
  122.4 2.6 copy-done.2
  125.0 5.4 %fusion.36 = f32[2,768,512]{2,1,0:T(8,128)} fusion(bf16[2,2048,512]{2,1,0:T(8,128)(2,1)S(1)} %copy-done.17, bf16[2,768,2048]{2,0,1:T(2,128)(2,1)S(1)} %all_to_all.10), kind=kOutput, calls=%fused_computation.56 | convolution fusion | flops 3221225472 | bytes 13631488 | tf_op jit(solution)/shard_map/esd,edf->esf/dot_general | solution.py:80
  130.4 16.8 %convolution_convert_fusion.1 = bf16[2,768,2048]{2,1,0:T(8,128)(2,1)} fusion(bf16[2,512,2048]{2,1,0:T(8,128)(2,1)} %param.22, f32[2,768,512]{2,1,0:T(8,128)} %fusion.36, bf16[2,2048,512]{2,1,0:T(8,128)(2,1)} %param.21, bf16[2,768,2048]{2,0,1:T(2,128)(2,1)} %copy-done.2), kind=kOutput, calls=%fused_computation.60 | convolution fusion | flops 6450315264 | bytes 24117248 | tf_op jit(solution)/shard_map/esf,efd->esd/dot_general | solution.py:83
  147.1 12.6 %copy.99 = bf16[2,768,2048]{2,0,1:T(2,128)(2,1)} copy(bf16[2,768,2048]{2,1,0:T(8,128)(2,1)} %convolution_convert_fusion.1) | data formatting | bytes 12582912 | tf_op jit(solution)/shard_map/convert_element_type | solution.py:85
  159.8 14.4 %all-to-all-start.1 = ((bf16[2,768,2048]{2,0,1:T(2,128)(2,1)}), bf16[2,768,2048]{2,0,1:T(2,128)(2,1)}, u32[]{:S(2)}, u32[]{:S(2)}) async-start(bf16[2,768,2048]{2,0,1:T(2,128)(2,1)} %copy.99), calls=%async_computation.1 | async-start | bytes 12582912 | tf_op jit(solution)/shard_map/all_to_all | solution.py:302
  175.0 1.2 select_reduce_fusion
  176.3 69.3 %all-to-all-done.1 = bf16[2,768,2048]{2,0,1:T(2,128)(2,1)} async-done(((bf16[2,768,2048]{2,0,1:T(2,128)(2,1)}), bf16[2,768,2048]{2,0,1:T(2,128)(2,1)}, u32[]{:S(2)}, u32[]{:S(2)}) %all-to-all-start.1) | async-done | bytes 6291488 | tf_op jit(solution)/shard_map/all_to_all | solution.py:302
  245.6 5.7 %copy.100 = bf16[2,768,2048]{2,1,0:T(8,128)(2,1)S(1)} copy(bf16[2,768,2048]{2,0,1:T(2,128)(2,1)} %all-to-all-done.1) | data formatting | bytes 12582912 | tf_op jit(solution)/shard_map/all_to_all | solution.py:302
  251.3 1.0 fusion.70
  252.3 1.4 fusion.55
  255.6 4.7 fusion.67
  260.3 4.7 fusion.38
  265.0 2.3 collective-permute-start.1
  267.5 2.7 collective-permute-done.1
  270.6 1.2 divide_multiply_fusion
  271.9 1.1 slice.78
  275.8 1.3 fusion.54
  277.3 23.5 %while.18 = (s32[]{:T(128)}, f32[16,128,128]{1,2,0:T(8,128)S(1)}, f32[16,128,128]{2,1,0:T(8,128)S(1)}, s32[]{:T(128)}, s32[]{:T(128)}) while((s32[]{:T(128)}, f32[16,128,128]{1,2,0:T(8,128)S(1)}, f32[16,128,128]{2,1,0:T(8,128)S(1)}, s32[]{:T(128)}, s32[]{:T(128)}) %tuple.71), condition=%wide.region_12.13_spmd.clone.clone, body=%wide.region_11.12_spmd.clone.clone.sunk | while | flops 404111360 | bytes 8421501 | solution.py:111
  277.6 1.4 fusion.134
  279.0 1.2 fusion.135
  280.9 1.4 fusion.134
  282.3 1.2 fusion.135
  284.3 1.4 fusion.134
  285.7 1.2 fusion.135
  287.6 1.4 fusion.134
  289.0 1.2 fusion.135
  290.9 1.4 fusion.134
  292.3 1.2 fusion.135
  294.2 1.4 fusion.134
  295.6 1.2 fusion.135
  297.6 1.4 fusion.134
  299.0 1.2 fusion.135
  300.8 2.6 copy.106
  303.4 1.6 copy.107
  306.6 1.3 fusion.61
  308.1 1.3 convolution_multiply_fusion
  309.3 1.0 fusion.92.state_ref
  310.4 1.1 convolution_subtract_fusion.1.map_ref
  311.5 166.7 %shard_map.149 = f32[16,128,128]{2,1,0:T(8,128)S(1)} custom-call(f32[16,128,128]{2,1,0:T(8,128)S(1)} %convolution_subtract_fusion.1.map_ref, f32[16,128,128]{2,1,0:T(8,128)S(1)} %fusion.92.state_ref), custom_call_target="tpu_custom_call" | custom-call | tf_op jit(solution)/shard_map/pallas_call | solution.py:225
  479.9 1.1 multiply_reduce_fusion
  481.2 1.0 copy.112
  (98 shorter events, 17.3 us)
Async XLA Ops:
  7.2 1.2 copy-start
  7.2 7.6 %copy-start.3 = (bf16[128,2048]{1,0:T(8,128)(2,1)S(1)}, bf16[128,2048]{1,0:T(8,128)(2,1)}, u32[]{:S(2)}) copy-start(bf16[128,2048]{1,0:T(8,128)(2,1)} %param.16) | copy-start | bytes 1572868
  7.2 7.6 %copy-start.13 = (f32[2048]{0:T(1024)S(1)}, f32[2048]{0:T(1024)}, u32[]{:S(2)}) copy-start(f32[2048]{0:T(1024)} %param.19) | copy-start | bytes 24580
  7.2 167.0 %all-gather.2.cloned.1.call-start = ((), (), s32[]{:S(2)}) async-start(), calls=%async_computation.2 | async-start | bytes 8912896 | tf_op jit(solution)/shard_map/all_gather | solution.py:271
  29.8 95.2 %copy-start.17 = (bf16[2,2048,512]{2,1,0:T(8,128)(2,1)S(1)}, bf16[2,2048,512]{2,1,0:T(8,128)(2,1)}, u32[]{:S(2)}) copy-start(bf16[2,2048,512]{2,1,0:T(8,128)(2,1)} %param.20) | copy-start | bytes 12582916
  122.4 2.6 copy-start.2
  159.8 15.1 %copy-start.12 = (f32[128,10]{0,1:T(8,128)S(1)}, f32[128,10]{0,1:T(8,128)}, u32[]{:S(2)}) copy-start(f32[128,10]{0,1:T(8,128)} %param.18) | copy-start | bytes 15364
  159.8 15.2 %copy-start.18 = (f32[16]{0:T(128)S(1)}, f32[16]{0:T(128)}, u32[]{:S(2)}) copy-start(f32[16]{0:T(128)} %param.27) | copy-start | bytes 196
  159.8 16.4 %copy-start.10 = (bf16[4,4096]{1,0:T(4,128)(2,1)S(1)}, bf16[4,4096]{1,0:T(4,128)(2,1)}, u32[]{:S(2)}) copy-start(bf16[4,4096]{1,0:T(4,128)(2,1)} %param.26) | copy-start | bytes 98308
  159.8 85.8 %all-to-all-start.1 = ((bf16[2,768,2048]{2,0,1:T(2,128)(2,1)}), bf16[2,768,2048]{2,0,1:T(2,128)(2,1)}, u32[]{:S(2)}, u32[]{:S(2)}) async-start(bf16[2,768,2048]{2,0,1:T(2,128)(2,1)} %copy.99), calls=%async_computation.1 | async-start | bytes 12582912 | tf_op jit(solution)/shard_map/all_to_all | solution.py:302
  174.2 86.1 %collective-permute-start = (bf16[1024,4096]{1,0:T(8,128)(2,1)}, bf16[1024,4096]{1,0:T(8,128)(2,1)}, u32[]{:S(2)}, u32[]{:S(2)}) collective-permute-start(bf16[1024,4096]{1,0:T(8,128)(2,1)} %all-gather.2.cloned.1.call-done), channel_id=1, source_target_pairs={{0,16},{16,0},{32,48},{48,32},{64,80},{80,64},{96,112},{112,96},{1... | collective-permute-start | bytes 25165832 | tf_op jit(solution)/shard_map/ppermute | solution.py:272
  252.3 2.2 copy-start.14
  252.3 2.4 copy-start.11
  252.3 2.7 copy-start.15
  253.7 0.8 copy-start.9
  265.0 5.2 %collective-permute-start.1 = (bf16[3,4096]{1,0:T(4,128)(2,1)S(1)}, bf16[3,4096]{1,0:T(4,128)(2,1)S(1)}, u32[]{:S(2)}, u32[]{:S(2)}) collective-permute-start(bf16[3,4096]{1,0:T(4,128)(2,1)S(1)} %slice.67), channel_id=1, source_target_pairs={{0,1},{1,2},{2,3},{3,4},{4,5},{5,6},{6,7},{7,8},{8,9},{9,10},{10,1... | collective-permute-start | bytes 73736 | tf_op jit(solution)/shard_map/ppermute | solution.py:13
  275.1 0.8 copy-start.4
  275.2 2.0 copy-start.6
  300.8 4.2 copy-start.5
  305.6 2.3 copy-start.8
  306.6 1.5 copy-start.7
  478.9 2.1 copy-start.16
  478.9 3.3 copy-start.1
Sparse Core Ops, SparseCore 0:
  10.7 135.7 all-gather.1

commit v10 on v9

--- a/solution.py
+++ b/solution.py
@@ -300,13 +300,14 @@
         down_weight,
     )
     returned = lax.all_to_all(served, ("outer", "inner"), split_axis=1, concat_axis=1, tiled=True)
-    returned = returned.reshape(-1, width)
     combine = jnp.sum(jnp.where(hits, mix_weight[:, :, None], 0.0), axis=1)
     combine_hi = combine.astype(jnp.bfloat16)
     combine_lo = (combine - combine_hi.astype(jnp.float32)).astype(jnp.bfloat16)
-    mixture = jnp.dot(combine_hi, returned, preferred_element_type=jnp.float32) + jnp.dot(
-        combine_lo, returned, preferred_element_type=jnp.float32
-    )
+    combine_hi = combine_hi.reshape(tok_count, local_experts, n_dev * capacity)
+    combine_lo = combine_lo.reshape(tok_count, local_experts, n_dev * capacity)
+    mixture = jnp.einsum(
+        "tes,esd->td", combine_hi, returned, preferred_element_type=jnp.float32
+    ) + jnp.einsum("tes,esd->td", combine_lo, returned, preferred_element_type=jnp.float32)
     hidden_out = (tokens_in.astype(jnp.float32) + mixture).astype(jnp.bfloat16)
     normed_second = rms_scale(hidden_out, second_gain).astype(jnp.bfloat16)
     mixed = jnp.dot(

time: 494 us -> 499 us (1.010)
  matrix products: 58.5 us -> 69.5 us
  local copies, waits for them, and re-layouts: 46.2 us -> 40.8 us
    dot_general x2, matrix products: 2.39 us -> 13.4 us  [the longest x1 6.79 us: per_device(): jnp.einsum('tes,esd->td', combine_lo, returned, preferred_element_type=jn...]
    all_to_all x1 -> x0, local copies, waits for them, and re-layouts: 5.68 us -> none  [per_device(): lax.all_to_all(served, ('outer', 'inner'), split_axis=1, concat_axis=1, t...]
  transfers between devices with their start and end apart: 4 -> 4, of which waited for: 2 -> 2; matrix products, arithmetic and copies ran while one was open for 14% -> 15% of each run, Pallas kernels for 0% -> 0%
where the time goes in v10:
time: 499 us; the launch traced here: 495 us
  Pallas kernels  167 us (33%)
  blocking collectives  92.7 us (19%)
  waiting for transfers between devices  71.8 us (14%)
  matrix products  69.5 us (14%)
  local copies, waits for them, and re-layouts  40.8 us (8%)
  other arithmetic  20.4 us (4%)
  starting transfers between devices  17.3 us (3%)
  between operations  15.1 us (3%)
    pallas_call x1, Pallas kernels, chained_state(): pl.pallas_call(functools.partial(scan_kernel, count, axes, groups), out_s...  167 us
    all_to_all x1, blocking collectives, per_device(): lax.all_to_all(outgoing, ('outer', 'inner'), split_axis=1, concat_axis=1,...  92.7 us
    all_to_all x1, waiting for transfers between devices, per_device(): lax.all_to_all(served, ('outer', 'inner'), split_axis=1, concat_axis=1, t...  69 us
    dot_general x1, matrix products, run_experts(): jnp.einsum('esf,efd->esd', hidden, down_weight, preferred_element_type=jn...  16.8 us
    all_to_all x1, starting transfers between devices, per_device(): lax.all_to_all(served, ('outer', 'inner'), split_axis=1, concat_axis=1, t...  14.4 us
    reshape x1, local copies, waits for them, and re-layouts, per_device(): outgoing = outgoing.reshape(local_experts, n_dev * capacity, width)  13 us
    convert_element_type x1, local copies, waits for them, and re-layouts, run_experts(): return jnp.einsum('esf,efd->esd', hidden, down_weight, preferred_element_...  12.6 us
  transfers between devices with their start and end apart: 4, of which 2 were waited for; matrix products, arithmetic and copies ran while one was open for 15% of the time, Pallas kernels for 0%

profile of v10, /device:TPU:83, one launch (start us, length us, event | category | flops | bytes accessed | tf_op | source)
XLA Modules:
  0.0 494.8 jit_solution(15418182418796663517)
XLA Ops:
  7.3 1.1 copy-done
  10.4 1.2 fusion.75
  11.6 1.1 select_reduce_fusion.1
  13.5 1.3 fusion.33
  14.8 1.9 convolution_convert_fusion
  16.7 13.0 %copy.80 = bf16[2,768,2048]{2,0,1:T(2,128)(2,1)S(1)} copy(bf16[2,768,2048]{2,1,0:T(8,128)(2,1)S(1)} %bitcast.93) | data formatting | bytes 12582912 | tf_op jit(solution)/shard_map/reshape | solution.py:295
  29.8 92.7 %all_to_all.10 = bf16[2,768,2048]{2,0,1:T(2,128)(2,1)S(1)} all-to-all(bf16[2,768,2048]{2,0,1:T(2,128)(2,1)S(1)} %copy.80), channel_id=1, replica_groups=mesh['outer'=8,'inner'=16] {'outer','inner'}, dimensions={1} | all-to-all | bytes 12582912 | tf_op jit(solution)/shard_map/all_to_all | solution.py:297
  122.4 2.6 copy-done.2
  125.0 5.4 %fusion.40 = f32[2,768,512]{2,1,0:T(8,128)} fusion(bf16[2,2048,512]{2,1,0:T(8,128)(2,1)S(1)} %copy-done.17, bf16[2,768,2048]{2,0,1:T(2,128)(2,1)S(1)} %all_to_all.10), kind=kOutput, calls=%fused_computation.60 | convolution fusion | flops 3221225472 | bytes 13631488 | tf_op jit(solution)/shard_map/esd,edf->esf/dot_general | solution.py:80
  130.4 16.8 %convolution_convert_fusion.1 = bf16[2,768,2048]{2,1,0:T(8,128)(2,1)} fusion(bf16[2,512,2048]{2,1,0:T(8,128)(2,1)} %param.22, f32[2,768,512]{2,1,0:T(8,128)} %fusion.40, bf16[2,2048,512]{2,1,0:T(8,128)(2,1)} %param.21, bf16[2,768,2048]{2,0,1:T(2,128)(2,1)} %copy-done.2), kind=kOutput, calls=%fused_computation.64 | convolution fusion | flops 6450315264 | bytes 24117248 | tf_op jit(solution)/shard_map/esf,efd->esd/dot_general | solution.py:83
  147.1 12.6 %copy.83 = bf16[2,768,2048]{2,0,1:T(2,128)(2,1)} copy(bf16[2,768,2048]{2,1,0:T(8,128)(2,1)} %convolution_convert_fusion.1) | data formatting | bytes 12582912 | tf_op jit(solution)/shard_map/convert_element_type | solution.py:85
  159.8 14.4 %all-to-all-start.1 = ((bf16[2,768,2048]{2,0,1:T(2,128)(2,1)}), bf16[2,768,2048]{2,0,1:T(2,128)(2,1)}, u32[]{:S(2)}, u32[]{:S(2)}) async-start(bf16[2,768,2048]{2,0,1:T(2,128)(2,1)} %copy.83), calls=%async_computation.1 | async-start | bytes 12582912 | tf_op jit(solution)/shard_map/all_to_all | solution.py:302
  174.8 1.2 select_reduce_fusion
  176.5 69.0 %all-to-all-done.1 = bf16[2,768,2048]{2,0,1:T(2,128)(2,1)} async-done(((bf16[2,768,2048]{2,0,1:T(2,128)(2,1)}), bf16[2,768,2048]{2,0,1:T(2,128)(2,1)}, u32[]{:S(2)}, u32[]{:S(2)}) %all-to-all-start.1) | async-done | bytes 6291488 | tf_op jit(solution)/shard_map/all_to_all | solution.py:302
  245.6 6.6 %fusion.43 = f32[128,2048]{1,0:T(8,128)S(1)} fusion(bf16[2,768,2048]{2,0,1:T(2,128)(2,1)} %all-to-all-done.1, f32[128,2,768]{0,2,1:T(8,128)S(1)} %bitcast.96), kind=kOutput, calls=%fused_computation.66 | convolution fusion | flops 805502976 | bytes 8126464 | tf_op jit(solution)/shard_map/tes,esd->td/dot_general | solution.py:308
  252.3 6.8 %fusion.72 = (f32[128]{0:T(128)S(1)}, bf16[128,2048]{1,0:T(8,128)(2,1)S(1)}) fusion(f32[128,2048]{1,0:T(8,128)S(1)} %fusion.43, bf16[2,768,2048]{2,0,1:T(2,128)(2,1)} %all-to-all-done.1, f32[128,2,768]{0,2,1:T(8,128)S(1)} %bitcast.97, bf16[128,2048]{1,0:T(8,128)(2,1)S(1)} %copy-done.3), kind=kOutput, calls=%fused_computation.100 | convolution fusion | flops 807927680 | bytes 9175552 | tf_op jit(solution)/shard_map/tes,esd->td/dot_general | solution.py:310
  261.0 4.7 fusion.84
  265.7 4.7 fusion.42
  270.4 2.3 collective-permute-start.1
  272.8 2.8 collective-permute-done.1
  275.9 1.2 divide_multiply_fusion
  277.2 1.1 slice.78
  281.2 1.3 fusion.71
  282.7 23.5 %while.18 = (s32[]{:T(128)}, f32[16,128,128]{1,2,0:T(8,128)S(1)}, f32[16,128,128]{2,1,0:T(8,128)S(1)}, s32[]{:T(128)}, s32[]{:T(128)}) while((s32[]{:T(128)}, f32[16,128,128]{1,2,0:T(8,128)S(1)}, f32[16,128,128]{2,1,0:T(8,128)S(1)}, s32[]{:T(128)}, s32[]{:T(128)}) %tuple.69), condition=%wide.region_12.13_spmd.clone.clone, body=%wide.region_11.12_spmd.clone.clone.sunk | while | flops 404111360 | bytes 8421501 | solution.py:111
  283.0 1.4 fusion.148
  284.4 1.2 fusion.149
  286.3 1.4 fusion.148
  287.7 1.2 fusion.149
  289.6 1.4 fusion.148
  291.0 1.2 fusion.149
  292.9 1.4 fusion.148
  294.3 1.2 fusion.149
  296.3 1.4 fusion.148
  297.7 1.2 fusion.149
  299.6 1.4 fusion.148
  301.0 1.2 fusion.149
  302.9 1.4 fusion.148
  304.3 1.2 fusion.149
  306.2 2.6 copy.93
  308.8 1.6 copy.94
  312.0 1.3 fusion.78
  313.4 1.3 convolution_multiply_fusion
  314.7 1.0 fusion.108.state_ref
  315.7 1.1 convolution_subtract_fusion.1.map_ref
  316.9 166.6 %shard_map.149 = f32[16,128,128]{2,1,0:T(8,128)S(1)} custom-call(f32[16,128,128]{2,1,0:T(8,128)S(1)} %convolution_subtract_fusion.1.map_ref, f32[16,128,128]{2,1,0:T(8,128)S(1)} %fusion.108.state_ref), custom_call_target="tpu_custom_call" | custom-call | tf_op jit(solution)/shard_map/pallas_call | solution.py:225
  484.2 1.0 fusion.67
  485.2 1.1 multiply_reduce_fusion
  486.5 1.0 copy.99
  (98 shorter events, 16.5 us)
Async XLA Ops:
  7.2 1.2 copy-start
  7.2 7.6 %copy-start.3 = (bf16[128,2048]{1,0:T(8,128)(2,1)S(1)}, bf16[128,2048]{1,0:T(8,128)(2,1)}, u32[]{:S(2)}) copy-start(bf16[128,2048]{1,0:T(8,128)(2,1)} %param.16) | copy-start | bytes 1572868
  7.2 7.6 %copy-start.13 = (f32[2048]{0:T(1024)S(1)}, f32[2048]{0:T(1024)}, u32[]{:S(2)}) copy-start(f32[2048]{0:T(1024)} %param.19) | copy-start | bytes 24580
  7.2 167.0 %all-gather.2.cloned.1.call-start = ((), (), s32[]{:S(2)}) async-start(), calls=%async_computation.2 | async-start | bytes 8912896 | tf_op jit(solution)/shard_map/all_gather | solution.py:271
  29.8 95.2 %copy-start.17 = (bf16[2,2048,512]{2,1,0:T(8,128)(2,1)S(1)}, bf16[2,2048,512]{2,1,0:T(8,128)(2,1)}, u32[]{:S(2)}) copy-start(bf16[2,2048,512]{2,1,0:T(8,128)(2,1)} %param.20) | copy-start | bytes 12582916
  122.4 2.6 copy-start.2
  159.8 15.0 %copy-start.12 = (f32[128,10]{0,1:T(8,128)S(1)}, f32[128,10]{0,1:T(8,128)}, u32[]{:S(2)}) copy-start(f32[128,10]{0,1:T(8,128)} %param.18) | copy-start | bytes 15364
  159.8 16.7 %copy-start.18 = (f32[16]{0:T(128)S(1)}, f32[16]{0:T(128)}, u32[]{:S(2)}) copy-start(f32[16]{0:T(128)} %param.27) | copy-start | bytes 196
  159.8 16.7 %copy-start.10 = (bf16[4,4096]{1,0:T(4,128)(2,1)S(1)}, bf16[4,4096]{1,0:T(4,128)(2,1)}, u32[]{:S(2)}) copy-start(bf16[4,4096]{1,0:T(4,128)(2,1)} %param.26) | copy-start | bytes 98308
  159.8 85.8 %all-to-all-start.1 = ((bf16[2,768,2048]{2,0,1:T(2,128)(2,1)}), bf16[2,768,2048]{2,0,1:T(2,128)(2,1)}, u32[]{:S(2)}, u32[]{:S(2)}) async-start(bf16[2,768,2048]{2,0,1:T(2,128)(2,1)} %copy.83), calls=%async_computation.1 | async-start | bytes 12582912 | tf_op jit(solution)/shard_map/all_to_all | solution.py:302
  174.2 91.4 %collective-permute-start = (bf16[1024,4096]{1,0:T(8,128)(2,1)}, bf16[1024,4096]{1,0:T(8,128)(2,1)}, u32[]{:S(2)}, u32[]{:S(2)}) collective-permute-start(bf16[1024,4096]{1,0:T(8,128)(2,1)} %all-gather.2.cloned.1.call-done), channel_id=1, source_target_pairs={{0,16},{16,0},{32,48},{48,32},{64,80},{80,64},{96,112},{112,96},{1... | collective-permute-start | bytes 25165832 | tf_op jit(solution)/shard_map/ppermute | solution.py:272
  252.2 7.6 %copy-start.14 = (f32[2048]{0:T(1024)S(1)}, f32[2048]{0:T(1024)}, u32[]{:S(2)}) copy-start(f32[2048]{0:T(1024)} %param.23) | copy-start | bytes 24580
  252.2 7.8 %copy-start.11 = (bf16[2048,32]{0,1:T(8,128)(2,1)S(1)}, bf16[2048,32]{0,1:T(8,128)(2,1)}, u32[]{:S(2)}) copy-start(bf16[2048,32]{0,1:T(8,128)(2,1)} %param.25) | copy-start | bytes 393220
  252.2 8.1 %copy-start.15 = (f32[16]{0:T(128)S(1)}, f32[16]{0:T(128)}, u32[]{:S(2)}) copy-start(f32[16]{0:T(128)} %param.28) | copy-start | bytes 196
  259.0 0.8 copy-start.9
  270.4 5.2 %collective-permute-start.1 = (bf16[3,4096]{1,0:T(4,128)(2,1)S(1)}, bf16[3,4096]{1,0:T(4,128)(2,1)S(1)}, u32[]{:S(2)}, u32[]{:S(2)}) collective-permute-start(bf16[3,4096]{1,0:T(4,128)(2,1)S(1)} %slice.67), channel_id=1, source_target_pairs={{0,1},{1,2},{2,3},{3,4},{4,5},{5,6},{6,7},{7,8},{8,9},{9,10},{10,1... | collective-permute-start | bytes 73736 | tf_op jit(solution)/shard_map/ppermute | solution.py:13
  280.4 0.8 copy-start.4
  280.5 2.0 copy-start.6
  306.2 4.2 copy-start.5
  311.0 2.3 copy-start.8
  312.0 1.5 copy-start.7
  484.2 2.1 copy-start.16
  484.2 3.3 copy-start.1
Sparse Core Ops, SparseCore 0:
  10.7 135.7 all-gather.1

commit v11 on v9

--- a/solution.py
+++ b/solution.py
@@ -107,8 +107,9 @@
             precision=lax.Precision.HIGH,
         )
 
-    start = jnp.broadcast_to(jnp.eye(size, dtype=system.dtype), system.shape)
-    return lax.fori_loop(0, levels, level, start)
+    first = ((rows // 2 == cols // 2) & (rows % 2 == 1) & (cols % 2 == 0))
+    start = jnp.eye(size, dtype=system.dtype) - jnp.where(first, lower, 0.0)
+    return lax.fori_loop(1, levels, level, start)
 
 
 def join_maps(earlier, later):

time: 494 us -> 491 us (level)
  transfers between devices with their start and end apart: 4 -> 4, of which waited for: 2 -> 2; matrix products, arithmetic and copies ran while one was open for 14% -> 15% of each run, Pallas kernels for 0% -> 0%
where the time goes in v11:
time: 491 us; the launch traced here: 486 us
  Pallas kernels  167 us (34%)
  blocking collectives  92.3 us (19%)
  waiting for transfers between devices  71.9 us (15%)
  matrix products  56.8 us (12%)
  local copies, waits for them, and re-layouts  46.3 us (9%)
  other arithmetic  19.2 us (4%)
  starting transfers between devices  17.4 us (4%)
  between operations  14.9 us (3%)
    pallas_call x1, Pallas kernels, chained_state(): pl.pallas_call(functools.partial(scan_kernel, count, axes, groups), out_s...  167 us
    all_to_all x1, blocking collectives, per_device(): lax.all_to_all(outgoing, ('outer', 'inner'), split_axis=1, concat_axis=1,...  92.3 us
    all_to_all x1, waiting for transfers between devices, per_device(): lax.all_to_all(served, ('outer', 'inner'), split_axis=1, concat_axis=1, t...  69.1 us
    dot_general x1, matrix products, run_experts(): jnp.einsum('esf,efd->esd', hidden, down_weight, preferred_element_type=jn...  16.8 us
    all_to_all x1, starting transfers between devices, per_device(): lax.all_to_all(served, ('outer', 'inner'), split_axis=1, concat_axis=1, t...  14.4 us
    reshape x1, local copies, waits for them, and re-layouts, per_device(): outgoing = outgoing.reshape(local_experts, n_dev * capacity, width)  13 us
    convert_element_type x1, local copies, waits for them, and re-layouts, run_experts(): return jnp.einsum('esf,efd->esd', hidden, down_weight, preferred_element_...  12.6 us
  transfers between devices with their start and end apart: 4, of which 2 were waited for; matrix products, arithmetic and copies ran while one was open for 15% of the time, Pallas kernels for 0%

profile of v11, /device:TPU:83, one launch (start us, length us, event | category | flops | bytes accessed | tf_op | source)
XLA Modules:
  0.0 486.0 jit_solution(10430775051684441562)
XLA Ops:
  7.3 1.1 copy-done
  10.4 1.2 fusion.58
  11.6 1.1 select_reduce_fusion.1
  13.5 1.3 fusion.33
  14.8 1.9 convolution_convert_fusion
  16.7 13.0 %copy.96 = bf16[2,768,2048]{2,0,1:T(2,128)(2,1)S(1)} copy(bf16[2,768,2048]{2,1,0:T(8,128)(2,1)S(1)} %bitcast.87) | data formatting | bytes 12582912 | tf_op jit(solution)/shard_map/reshape | solution.py:296
  29.8 92.3 %all_to_all.10 = bf16[2,768,2048]{2,0,1:T(2,128)(2,1)S(1)} all-to-all(bf16[2,768,2048]{2,0,1:T(2,128)(2,1)S(1)} %copy.96), channel_id=1, replica_groups=mesh['outer'=8,'inner'=16] {'outer','inner'}, dimensions={1} | all-to-all | bytes 12582912 | tf_op jit(solution)/shard_map/all_to_all | solution.py:298
  122.1 2.6 copy-done.4
  124.6 5.4 %fusion.36 = f32[2,768,512]{2,1,0:T(8,128)} fusion(bf16[2,2048,512]{2,1,0:T(8,128)(2,1)S(1)} %copy-done.17, bf16[2,768,2048]{2,0,1:T(2,128)(2,1)S(1)} %all_to_all.10), kind=kOutput, calls=%fused_computation.56 | convolution fusion | flops 3221225472 | bytes 13631488 | tf_op jit(solution)/shard_map/esd,edf->esf/dot_general | solution.py:80
  130.0 16.8 %convolution_convert_fusion.1 = bf16[2,768,2048]{2,1,0:T(8,128)(2,1)} fusion(bf16[2,512,2048]{2,1,0:T(8,128)(2,1)} %param.22, f32[2,768,512]{2,1,0:T(8,128)} %fusion.36, bf16[2,2048,512]{2,1,0:T(8,128)(2,1)} %param.21, bf16[2,768,2048]{2,0,1:T(2,128)(2,1)} %copy-done.4), kind=kOutput, calls=%fused_computation.60 | convolution fusion | flops 6450315264 | bytes 24117248 | tf_op jit(solution)/shard_map/esf,efd->esd/dot_general | solution.py:83
  146.8 12.6 %copy.99 = bf16[2,768,2048]{2,0,1:T(2,128)(2,1)} copy(bf16[2,768,2048]{2,1,0:T(8,128)(2,1)} %convolution_convert_fusion.1) | data formatting | bytes 12582912 | tf_op jit(solution)/shard_map/convert_element_type | solution.py:85
  159.4 14.4 %all-to-all-start.1 = ((bf16[2,768,2048]{2,0,1:T(2,128)(2,1)}), bf16[2,768,2048]{2,0,1:T(2,128)(2,1)}, u32[]{:S(2)}, u32[]{:S(2)}) async-start(bf16[2,768,2048]{2,0,1:T(2,128)(2,1)} %copy.99), calls=%async_computation.1 | async-start | bytes 12582912 | tf_op jit(solution)/shard_map/all_to_all | solution.py:303
  174.8 1.2 select_reduce_fusion
  176.1 69.1 %all-to-all-done.1 = bf16[2,768,2048]{2,0,1:T(2,128)(2,1)} async-done(((bf16[2,768,2048]{2,0,1:T(2,128)(2,1)}), bf16[2,768,2048]{2,0,1:T(2,128)(2,1)}, u32[]{:S(2)}, u32[]{:S(2)}) %all-to-all-start.1) | async-done | bytes 6291488 | tf_op jit(solution)/shard_map/all_to_all | solution.py:303
  245.2 5.7 %copy.100 = bf16[2,768,2048]{2,1,0:T(8,128)(2,1)S(1)} copy(bf16[2,768,2048]{2,0,1:T(2,128)(2,1)} %all-to-all-done.1) | data formatting | bytes 12582912 | tf_op jit(solution)/shard_map/all_to_all | solution.py:303
  250.9 1.0 fusion.70
  252.0 1.4 fusion.55
  255.3 4.7 fusion.67
  259.9 4.7 fusion.38
  264.7 2.3 collective-permute-start.1
  267.2 2.7 collective-permute-done.1
  270.2 1.2 divide_multiply_fusion
  271.5 1.1 slice.78
  275.5 1.4 select_subtract_fusion
  277.3 20.4 %while.18 = (s32[]{:T(128)}, f32[16,128,128]{1,2,0:T(8,128)S(1)}, f32[16,128,128]{2,1,0:T(8,128)S(1)}, s32[]{:T(128)}, s32[]{:T(128)}) while((s32[]{:T(128)}, f32[16,128,128]{1,2,0:T(8,128)S(1)}, f32[16,128,128]{2,1,0:T(8,128)S(1)}, s32[]{:T(128)}, s32[]{:T(128)}) %tuple.75), condition=%wide.region_12.13_spmd.clone.clone, body=%wide.region_11.12_spmd.clone.clone.sunk | while | flops 404111360 | bytes 8421493 | solution.py:112
  277.8 1.4 fusion.136
  279.2 1.2 fusion.137
  281.1 1.4 fusion.136
  282.5 1.2 fusion.137
  284.5 1.4 fusion.136
  285.9 1.2 fusion.137
  287.8 1.4 fusion.136
  289.2 1.2 fusion.137
  291.1 1.4 fusion.136
  292.5 1.2 fusion.137
  294.4 1.4 fusion.136
  295.8 1.2 fusion.137
  297.7 2.6 copy.106
  300.3 1.6 copy.107
  302.5 1.0 fusion.93
  303.5 1.3 fusion.61
  305.0 1.3 convolution_multiply_fusion
  306.2 1.0 fusion.94.state_ref
  307.3 1.1 convolution_subtract_fusion.1.map_ref
  308.4 166.5 %shard_map.149 = f32[16,128,128]{2,1,0:T(8,128)S(1)} custom-call(f32[16,128,128]{2,1,0:T(8,128)S(1)} %convolution_subtract_fusion.1.map_ref, f32[16,128,128]{2,1,0:T(8,128)S(1)} %fusion.94.state_ref), custom_call_target="tpu_custom_call" | custom-call | tf_op jit(solution)/shard_map/pallas_call | solution.py:226
  475.6 1.0 fusion.50
  476.6 1.1 multiply_reduce_fusion
  477.9 1.0 copy.112
  (97 shorter events, 15.0 us)
Async XLA Ops:
  7.2 1.2 copy-start
  7.2 7.6 %copy-start.5 = (bf16[128,2048]{1,0:T(8,128)(2,1)S(1)}, bf16[128,2048]{1,0:T(8,128)(2,1)}, u32[]{:S(2)}) copy-start(bf16[128,2048]{1,0:T(8,128)(2,1)} %param.16) | copy-start | bytes 1572868
  7.2 7.6 %copy-start.13 = (f32[2048]{0:T(1024)S(1)}, f32[2048]{0:T(1024)}, u32[]{:S(2)}) copy-start(f32[2048]{0:T(1024)} %param.19) | copy-start | bytes 24580
  7.2 166.6 %all-gather.2.cloned.1.call-start = ((), (), s32[]{:S(2)}) async-start(), calls=%async_computation.2 | async-start | bytes 8912896 | tf_op jit(solution)/shard_map/all_gather | solution.py:272
  29.8 94.9 %copy-start.17 = (bf16[2,2048,512]{2,1,0:T(8,128)(2,1)S(1)}, bf16[2,2048,512]{2,1,0:T(8,128)(2,1)}, u32[]{:S(2)}) copy-start(bf16[2,2048,512]{2,1,0:T(8,128)(2,1)} %param.20) | copy-start | bytes 12582916
  122.1 2.6 copy-start.4
  159.4 15.1 %copy-start.12 = (f32[128,10]{0,1:T(8,128)S(1)}, f32[128,10]{0,1:T(8,128)}, u32[]{:S(2)}) copy-start(f32[128,10]{0,1:T(8,128)} %param.18) | copy-start | bytes 15364
  159.4 15.2 %copy-start.18 = (f32[16]{0:T(128)S(1)}, f32[16]{0:T(128)}, u32[]{:S(2)}) copy-start(f32[16]{0:T(128)} %param.27) | copy-start | bytes 196
  159.4 16.6 %copy-start.10 = (bf16[4,4096]{1,0:T(4,128)(2,1)S(1)}, bf16[4,4096]{1,0:T(4,128)(2,1)}, u32[]{:S(2)}) copy-start(bf16[4,4096]{1,0:T(4,128)(2,1)} %param.26) | copy-start | bytes 98308
  159.4 85.8 %all-to-all-start.1 = ((bf16[2,768,2048]{2,0,1:T(2,128)(2,1)}), bf16[2,768,2048]{2,0,1:T(2,128)(2,1)}, u32[]{:S(2)}, u32[]{:S(2)}) async-start(bf16[2,768,2048]{2,0,1:T(2,128)(2,1)} %copy.99), calls=%async_computation.1 | async-start | bytes 12582912 | tf_op jit(solution)/shard_map/all_to_all | solution.py:303
  173.9 86.1 %collective-permute-start = (bf16[1024,4096]{1,0:T(8,128)(2,1)}, bf16[1024,4096]{1,0:T(8,128)(2,1)}, u32[]{:S(2)}, u32[]{:S(2)}) collective-permute-start(bf16[1024,4096]{1,0:T(8,128)(2,1)} %all-gather.2.cloned.1.call-done), channel_id=1, source_target_pairs={{0,16},{16,0},{32,48},{48,32},{64,80},{80,64},{96,112},{112,96},{1... | collective-permute-start | bytes 25165832 | tf_op jit(solution)/shard_map/ppermute | solution.py:273
  251.9 2.2 copy-start.14
  251.9 2.4 copy-start.11
  251.9 2.7 copy-start.15
  253.3 0.8 copy-start.9
  264.7 5.3 %collective-permute-start.1 = (bf16[3,4096]{1,0:T(4,128)(2,1)S(1)}, bf16[3,4096]{1,0:T(4,128)(2,1)S(1)}, u32[]{:S(2)}, u32[]{:S(2)}) collective-permute-start(bf16[3,4096]{1,0:T(4,128)(2,1)S(1)} %slice.67), channel_id=1, source_target_pairs={{0,1},{1,2},{2,3},{3,4},{4,5},{5,6},{6,7},{7,8},{8,9},{9,10},{10,1... | collective-permute-start | bytes 73736 | tf_op jit(solution)/shard_map/ppermute | solution.py:13
  274.7 0.8 copy-start.6
  274.8 2.1 copy-start.2
  297.7 4.2 copy-start.7
  302.5 2.3 copy-start.8
  303.5 1.5 copy-start.3
  475.6 2.1 copy-start.16
  475.6 3.3 copy-start.1
Sparse Core Ops, SparseCore 0:
  10.7 135.3 all-gather.1

commit v12 on v11

--- a/solution.py
+++ b/solution.py
@@ -344,6 +344,19 @@
         )
     )
     values = filtered[:, 2 * key_heads * head_dim :].reshape(tok_count, value_heads, head_dim)
+    key_heads_major = keys.transpose(1, 0, 2)
+    key_pairs = jnp.repeat(
+        jnp.einsum("htd,hsd->hts", key_heads_major, key_heads_major, precision=lax.Precision.HIGH),
+        ratio,
+        axis=0,
+    )
+    query_pairs = jnp.repeat(
+        jnp.einsum(
+            "htd,hsd->hts", queries.transpose(1, 0, 2), key_heads_major, precision=lax.Precision.HIGH
+        ),
+        ratio,
+        axis=0,
+    )
     queries = jnp.repeat(queries, ratio, axis=1)
     keys = jnp.repeat(keys, ratio, axis=1)
     strength = jax.nn.sigmoid(gating[:, :value_heads]).T
@@ -357,7 +370,7 @@
     key_major = keys.transpose(1, 0, 2)
     query_leading = queries.transpose(1, 0, 2)
     value_major = values.transpose(1, 0, 2)
-    key_inner = jnp.einsum("htd,hid->hti", key_major, key_major, precision=lax.Precision.HIGH)
+    key_inner = key_pairs
     lower_part = jnp.where(lower_strict, decay_mat * key_inner, 0.0) * strength[:, :, None]
     system = lower_part + jnp.eye(tok_count, dtype=jnp.float32)
     growth = jnp.exp(cumulative)
@@ -385,10 +398,7 @@
     updates = value_resolved - jnp.einsum(
         "mwx,mxd->mwd", key_resolved, initial_state, precision=lax.Precision.HIGH
     )
-    query_key = (
-        jnp.einsum("htd,hid->hti", query_leading, key_major, precision=lax.Precision.HIGH)
-        * decay_mat
-    )
+    query_key = query_pairs * decay_mat
     carried = (
         jnp.einsum("mwx,mxd->mwd", query_leading, initial_state, precision=lax.Precision.HIGH)
         * growth[:, :, None]

time: 491 us -> 492 us (level)
  other arithmetic: 19.2 us -> 25.2 us
where the time goes in v12:
time: 492 us; the launch traced here: 487 us
  Pallas kernels  167 us (34%)
  blocking collectives  92.7 us (19%)
  waiting for transfers between devices  71.9 us (15%)
  matrix products  54.5 us (11%)
  local copies, waits for them, and re-layouts  43.5 us (9%)
  other arithmetic  25.2 us (5%)
  starting transfers between devices  17.3 us (4%)
  between operations  14.9 us (3%)
    pallas_call x1, Pallas kernels, chained_state(): pl.pallas_call(functools.partial(scan_kernel, count, axes, groups), out_s...  167 us
    all_to_all x1, blocking collectives, per_device(): lax.all_to_all(outgoing, ('outer', 'inner'), split_axis=1, concat_axis=1,...  92.7 us
    all_to_all x1, waiting for transfers between devices, per_device(): lax.all_to_all(served, ('outer', 'inner'), split_axis=1, concat_axis=1, t...  69.2 us
    dot_general x1, matrix products, run_experts(): jnp.einsum('esf,efd->esd', hidden, down_weight, preferred_element_type=jn...  16.8 us
    all_to_all x1, starting transfers between devices, per_device(): lax.all_to_all(served, ('outer', 'inner'), split_axis=1, concat_axis=1, t...  14.4 us
    reshape x1, local copies, waits for them, and re-layouts, per_device(): outgoing = outgoing.reshape(local_experts, n_dev * capacity, width)  13 us
    convert_element_type x1, local copies, waits for them, and re-layouts, run_experts(): return jnp.einsum('esf,efd->esd', hidden, down_weight, preferred_element_...  12.6 us
  transfers between devices with their start and end apart: 4, of which 2 were waited for; matrix products, arithmetic and copies ran while one was open for 15% of the time, Pallas kernels for 0%

profile of v12, /device:TPU:83, one launch (start us, length us, event | category | flops | bytes accessed | tf_op | source)
XLA Modules:
  0.0 486.9 jit_solution(12112579678985842693)
XLA Ops:
  7.3 1.1 copy-done
  9.2 0.9 convert_reduce_fusion
  10.4 1.2 fusion.56
  11.6 1.1 select_reduce_fusion.1
  13.5 1.3 fusion.35
  14.8 1.9 convolution_convert_fusion
  16.7 13.0 %copy.100 = bf16[2,768,2048]{2,0,1:T(2,128)(2,1)S(1)} copy(bf16[2,768,2048]{2,1,0:T(8,128)(2,1)S(1)} %bitcast.118) | data formatting | bytes 12582912 | tf_op jit(solution)/shard_map/reshape | solution.py:296
  29.8 92.7 %all_to_all.10 = bf16[2,768,2048]{2,0,1:T(2,128)(2,1)S(1)} all-to-all(bf16[2,768,2048]{2,0,1:T(2,128)(2,1)S(1)} %copy.100), channel_id=1, replica_groups=mesh['outer'=8,'inner'=16] {'outer','inner'}, dimensions={1} | all-to-all | bytes 12582912 | tf_op jit(solution)/shard_map/all_to_all | solution.py:298
  122.4 2.6 copy-done.2
  125.0 5.4 %fusion.38 = f32[2,768,512]{2,1,0:T(8,128)} fusion(bf16[2,2048,512]{2,1,0:T(8,128)(2,1)S(1)} %copy-done.14, bf16[2,768,2048]{2,0,1:T(2,128)(2,1)S(1)} %all_to_all.10), kind=kOutput, calls=%fused_computation.58 | convolution fusion | flops 3221225472 | bytes 13631488 | tf_op jit(solution)/shard_map/esd,edf->esf/dot_general | solution.py:80
  130.4 16.8 %convolution_convert_fusion.1 = bf16[2,768,2048]{2,1,0:T(8,128)(2,1)} fusion(bf16[2,512,2048]{2,1,0:T(8,128)(2,1)} %param.22, f32[2,768,512]{2,1,0:T(8,128)} %fusion.38, bf16[2,2048,512]{2,1,0:T(8,128)(2,1)} %param.21, bf16[2,768,2048]{2,0,1:T(2,128)(2,1)} %copy-done.2), kind=kOutput, calls=%fused_computation.62 | convolution fusion | flops 6450315264 | bytes 24117248 | tf_op jit(solution)/shard_map/esf,efd->esd/dot_general | solution.py:83
  147.1 12.6 %copy.103 = bf16[2,768,2048]{2,0,1:T(2,128)(2,1)} copy(bf16[2,768,2048]{2,1,0:T(8,128)(2,1)} %convolution_convert_fusion.1) | data formatting | bytes 12582912 | tf_op jit(solution)/shard_map/convert_element_type | solution.py:85
  159.8 14.4 %all-to-all-start.1 = ((bf16[2,768,2048]{2,0,1:T(2,128)(2,1)}), bf16[2,768,2048]{2,0,1:T(2,128)(2,1)}, u32[]{:S(2)}, u32[]{:S(2)}) async-start(bf16[2,768,2048]{2,0,1:T(2,128)(2,1)} %copy.103), calls=%async_computation.1 | async-start | bytes 12582912 | tf_op jit(solution)/shard_map/all_to_all | solution.py:303
  175.1 1.2 select_reduce_fusion
  176.4 69.2 %all-to-all-done.1 = bf16[2,768,2048]{2,0,1:T(2,128)(2,1)} async-done(((bf16[2,768,2048]{2,0,1:T(2,128)(2,1)}), bf16[2,768,2048]{2,0,1:T(2,128)(2,1)}, u32[]{:S(2)}, u32[]{:S(2)}) %all-to-all-start.1) | async-done | bytes 6291488 | tf_op jit(solution)/shard_map/all_to_all | solution.py:303
  245.6 5.7 %copy.104 = bf16[2,768,2048]{2,1,0:T(8,128)(2,1)S(1)} copy(bf16[2,768,2048]{2,0,1:T(2,128)(2,1)} %all-to-all-done.1) | data formatting | bytes 12582912 | tf_op jit(solution)/shard_map/all_to_all | solution.py:303
  251.3 1.0 fusion.79
  252.3 1.4 fusion.53
  254.9 4.7 fusion.76
  259.5 4.7 fusion.40
  264.2 2.3 collective-permute-start.1
  266.7 2.7 collective-permute-done.1
  269.8 1.2 divide_multiply_fusion
  271.1 1.1 slice.78
  272.7 0.9 copy.105
  274.2 1.0 copy.106
  276.5 1.7 bitcast_multiply_fusion.3
  278.6 23.7 %while.18 = (s32[]{:T(128)}, f32[16,128,128]{1,2,0:T(8,128)S(1)}, f32[16,128]{1,0:T(8,128)S(1)}, pred[128,128]{1,0:T(8,128)(4,1)S(1)}, f32[8,128,128]{2,1,0:T(8,...) while((s32[]{:T(128)}, f32[16,128,128]{1,2,0:T(8,128)S(1)}, ...), condition=%wide.region_12.13_spmd.clone.clone, body=%wide.region_11.12_spmd.clone.clone.sunk | while | flops 406208512 | bytes 10109085 | solution.py:112
  278.7 1.4 fusion.144
  280.7 1.2 fusion.146
  282.6 1.4 fusion.144
  284.7 1.2 fusion.146
  286.6 1.4 fusion.144
  288.6 1.2 fusion.146
  290.5 1.4 fusion.144
  292.6 1.2 fusion.146
  294.5 1.4 fusion.144
  296.5 1.2 fusion.146
  298.4 1.4 fusion.144
  300.4 1.2 fusion.146
  302.3 1.5 copy.112
  304.2 1.2 bitcast_multiply_fusion.1
  305.4 1.0 fusion.103
  306.4 1.3 fusion.59
  309.0 166.6 %shard_map.149 = f32[16,128,128]{2,1,0:T(8,128)S(1)} custom-call(f32[16,128,128]{2,1,0:T(8,128)S(1)} %convolution_subtract_fusion.1.map_ref, f32[16,128,128]{2,1,0:T(8,128)S(1)} %fusion.104.state_ref), custom_call_target="tpu_custom_call" | custom-call | tf_op jit(solution)/shard_map/pallas_call | solution.py:226
  476.4 1.0 fusion.52
  477.5 1.0 multiply_reduce_fusion
  478.8 1.0 copy.119
  (97 shorter events, 17.5 us)
Async XLA Ops:
  7.2 1.2 copy-start
  7.2 7.6 %copy-start.3 = (bf16[128,2048]{1,0:T(8,128)(2,1)S(1)}, bf16[128,2048]{1,0:T(8,128)(2,1)}, u32[]{:S(2)}) copy-start(bf16[128,2048]{1,0:T(8,128)(2,1)} %param.16) | copy-start | bytes 1572868
  7.2 7.6 %copy-start.10 = (f32[2048]{0:T(1024)S(1)}, f32[2048]{0:T(1024)}, u32[]{:S(2)}) copy-start(f32[2048]{0:T(1024)} %param.19) | copy-start | bytes 24580
  7.2 167.0 %all-gather.2.cloned.1.call-start = ((), (), s32[]{:S(2)}) async-start(), calls=%async_computation.2 | async-start | bytes 8912896 | tf_op jit(solution)/shard_map/all_gather | solution.py:272
  29.8 95.2 %copy-start.14 = (bf16[2,2048,512]{2,1,0:T(8,128)(2,1)S(1)}, bf16[2,2048,512]{2,1,0:T(8,128)(2,1)}, u32[]{:S(2)}) copy-start(bf16[2,2048,512]{2,1,0:T(8,128)(2,1)} %param.20) | copy-start | bytes 12582916
  122.4 2.6 copy-start.2
  159.8 15.0 %copy-start.9 = (f32[128,10]{0,1:T(8,128)S(1)}, f32[128,10]{0,1:T(8,128)}, u32[]{:S(2)}) copy-start(f32[128,10]{0,1:T(8,128)} %param.18) | copy-start | bytes 15364
  159.8 15.1 %copy-start.15 = (f32[16]{0:T(128)S(1)}, f32[16]{0:T(128)}, u32[]{:S(2)}) copy-start(f32[16]{0:T(128)} %param.27) | copy-start | bytes 196
  159.8 16.5 %copy-start.7 = (bf16[4,4096]{1,0:T(4,128)(2,1)S(1)}, bf16[4,4096]{1,0:T(4,128)(2,1)}, u32[]{:S(2)}) copy-start(bf16[4,4096]{1,0:T(4,128)(2,1)} %param.26) | copy-start | bytes 98308
  159.8 85.8 %all-to-all-start.1 = ((bf16[2,768,2048]{2,0,1:T(2,128)(2,1)}), bf16[2,768,2048]{2,0,1:T(2,128)(2,1)}, u32[]{:S(2)}, u32[]{:S(2)}) async-start(bf16[2,768,2048]{2,0,1:T(2,128)(2,1)} %copy.103), calls=%async_computation.1 | async-start | bytes 12582912 | tf_op jit(solution)/shard_map/all_to_all | solution.py:303
  174.2 85.3 %collective-permute-start = (bf16[1024,4096]{1,0:T(8,128)(2,1)}, bf16[1024,4096]{1,0:T(8,128)(2,1)}, u32[]{:S(2)}, u32[]{:S(2)}) collective-permute-start(bf16[1024,4096]{1,0:T(8,128)(2,1)} %all-gather.2.cloned.1.call-done), channel_id=1, source_target_pairs={{0,16},{16,0},{32,48},{48,32},{64,80},{80,64},{96,112},{112,96},{1... | collective-permute-start | bytes 25165832 | tf_op jit(solution)/shard_map/ppermute | solution.py:273
  252.3 1.4 copy-start.11
  252.3 1.6 copy-start.8
  252.3 1.9 copy-start.12
  253.7 5.8 %copy-start.6 = (bf16[128,2048]{1,0:T(8,128)(2,1)}, bf16[128,2048]{1,0:T(8,128)(2,1)S(1)}, u32[]{:S(2)}) copy-start(bf16[128,2048]{1,0:T(8,128)(2,1)S(1)} %get-tuple-element.341) | copy-start | bytes 1572868
  264.2 5.2 %collective-permute-start.1 = (bf16[3,4096]{1,0:T(4,128)(2,1)S(1)}, bf16[3,4096]{1,0:T(4,128)(2,1)S(1)}, u32[]{:S(2)}, u32[]{:S(2)}) collective-permute-start(bf16[3,4096]{1,0:T(4,128)(2,1)S(1)} %slice.67), channel_id=1, source_target_pairs={{0,1},{1,2},{2,3},{3,4},{4,5},{5,6},{6,7},{7,8},{8,9},{9,10},{10,1... | collective-permute-start | bytes 73736 | tf_op jit(solution)/shard_map/ppermute | solution.py:13
  308.9 167.3 %copy-start.5 = (f32[128,8,128]{2,0,1:T(8,128)S(1)}, f32[128,8,128]{2,0,1:T(8,128)}, u32[]{:S(2)}) copy-start(f32[128,8,128]{2,0,1:T(8,128)} %copy.105) | copy-start | bytes 1572868
  476.3 1.2 copy-start.4
  476.4 2.2 copy-start.13
  477.4 2.3 copy-start.1
Sparse Core Ops, SparseCore 0:
  10.7 135.7 all-gather.1

commit v13 on v11

--- a/solution.py
+++ b/solution.py
@@ -364,12 +364,13 @@
     scaled_keys = key_major * (strength * growth)[:, :, None]
     scaled_values = value_major * strength[:, :, None]
     inverse = unit_lower_inverse(system)
-    key_resolved = jnp.einsum(
-        "hts,hsd->htd", inverse, scaled_keys, precision=lax.Precision.HIGH
-    )
-    value_resolved = jnp.einsum(
-        "hts,hsd->htd", inverse, scaled_values, precision=lax.Precision.HIGH
-    )
+    resolved = jnp.einsum(
+        "hts,hsd->htd",
+        inverse,
+        jnp.concatenate([scaled_keys, scaled_values], axis=-1),
+        precision=lax.Precision.HIGH,
+    )
+    key_resolved, value_resolved = resolved[..., :head_dim], resolved[..., head_dim:]
     tail = jnp.exp(cumulative[:, -1:] - cumulative)
     trailing_keys = key_major * tail[:, :, None]
     eye_heads = jnp.broadcast_to(

time: 491 us -> 490 us (level)
  no operation moved by 1% of the time
where the time goes in v13:
time: 490 us; the launch traced here: 485 us
  Pallas kernels  167 us (34%)
  blocking collectives  92.3 us (19%)
  waiting for transfers between devices  71.9 us (15%)
  matrix products  55.4 us (11%)
  local copies, waits for them, and re-layouts  46.3 us (9%)
  other arithmetic  19.5 us (4%)
  starting transfers between devices  17.4 us (4%)
  between operations  14.9 us (3%)
    pallas_call x1, Pallas kernels, chained_state(): pl.pallas_call(functools.partial(scan_kernel, count, axes, groups), out_s...  167 us
    all_to_all x1, blocking collectives, per_device(): lax.all_to_all(outgoing, ('outer', 'inner'), split_axis=1, concat_axis=1,...  92.3 us
    all_to_all x1, waiting for transfers between devices, per_device(): lax.all_to_all(served, ('outer', 'inner'), split_axis=1, concat_axis=1, t...  69.1 us
    dot_general x1, matrix products, run_experts(): jnp.einsum('esf,efd->esd', hidden, down_weight, preferred_element_type=jn...  16.8 us
    all_to_all x1, starting transfers between devices, per_device(): lax.all_to_all(served, ('outer', 'inner'), split_axis=1, concat_axis=1, t...  14.4 us
    reshape x1, local copies, waits for them, and re-layouts, per_device(): outgoing = outgoing.reshape(local_experts, n_dev * capacity, width)  13 us
    convert_element_type x1, local copies, waits for them, and re-layouts, run_experts(): return jnp.einsum('esf,efd->esd', hidden, down_weight, preferred_element_...  12.6 us
  transfers between devices with their start and end apart: 4, of which 2 were waited for; matrix products, arithmetic and copies ran while one was open for 15% of the time, Pallas kernels for 0%

profile of v13, /device:TPU:83, one launch (start us, length us, event | category | flops | bytes accessed | tf_op | source)
XLA Modules:
  0.0 484.9 jit_solution(5183920540659803719)
XLA Ops:
  7.3 1.1 copy-done
  9.2 0.9 convert_reduce_fusion
  10.4 1.2 fusion.62
  11.6 1.1 select_reduce_fusion.1
  13.5 1.3 fusion.33
  14.8 1.9 convolution_convert_fusion
  16.7 13.0 %copy.90 = bf16[2,768,2048]{2,0,1:T(2,128)(2,1)S(1)} copy(bf16[2,768,2048]{2,1,0:T(8,128)(2,1)S(1)} %bitcast.81) | data formatting | bytes 12582912 | tf_op jit(solution)/shard_map/reshape | solution.py:296
  29.8 92.3 %all_to_all.10 = bf16[2,768,2048]{2,0,1:T(2,128)(2,1)S(1)} all-to-all(bf16[2,768,2048]{2,0,1:T(2,128)(2,1)S(1)} %copy.90), channel_id=1, replica_groups=mesh['outer'=8,'inner'=16] {'outer','inner'}, dimensions={1} | all-to-all | bytes 12582912 | tf_op jit(solution)/shard_map/all_to_all | solution.py:298
  122.1 2.6 copy-done.4
  124.6 5.4 %fusion.36 = f32[2,768,512]{2,1,0:T(8,128)} fusion(bf16[2,2048,512]{2,1,0:T(8,128)(2,1)S(1)} %copy-done.17, bf16[2,768,2048]{2,0,1:T(2,128)(2,1)S(1)} %all_to_all.10), kind=kOutput, calls=%fused_computation.56 | convolution fusion | flops 3221225472 | bytes 13631488 | tf_op jit(solution)/shard_map/esd,edf->esf/dot_general | solution.py:80
  130.0 16.8 %convolution_convert_fusion.1 = bf16[2,768,2048]{2,1,0:T(8,128)(2,1)} fusion(bf16[2,512,2048]{2,1,0:T(8,128)(2,1)} %param.22, f32[2,768,512]{2,1,0:T(8,128)} %fusion.36, bf16[2,2048,512]{2,1,0:T(8,128)(2,1)} %param.21, bf16[2,768,2048]{2,0,1:T(2,128)(2,1)} %copy-done.4), kind=kOutput, calls=%fused_computation.60 | convolution fusion | flops 6450315264 | bytes 24117248 | tf_op jit(solution)/shard_map/esf,efd->esd/dot_general | solution.py:83
  146.8 12.6 %copy.93 = bf16[2,768,2048]{2,0,1:T(2,128)(2,1)} copy(bf16[2,768,2048]{2,1,0:T(8,128)(2,1)} %convolution_convert_fusion.1) | data formatting | bytes 12582912 | tf_op jit(solution)/shard_map/convert_element_type | solution.py:85
  159.4 14.4 %all-to-all-start.1 = ((bf16[2,768,2048]{2,0,1:T(2,128)(2,1)}), bf16[2,768,2048]{2,0,1:T(2,128)(2,1)}, u32[]{:S(2)}, u32[]{:S(2)}) async-start(bf16[2,768,2048]{2,0,1:T(2,128)(2,1)} %copy.93), calls=%async_computation.1 | async-start | bytes 12582912 | tf_op jit(solution)/shard_map/all_to_all | solution.py:303
  174.8 1.2 select_reduce_fusion
  176.1 69.1 %all-to-all-done.1 = bf16[2,768,2048]{2,0,1:T(2,128)(2,1)} async-done(((bf16[2,768,2048]{2,0,1:T(2,128)(2,1)}), bf16[2,768,2048]{2,0,1:T(2,128)(2,1)}, u32[]{:S(2)}, u32[]{:S(2)}) %all-to-all-start.1) | async-done | bytes 6291488 | tf_op jit(solution)/shard_map/all_to_all | solution.py:303
  245.2 5.7 %copy.94 = bf16[2,768,2048]{2,1,0:T(8,128)(2,1)S(1)} copy(bf16[2,768,2048]{2,0,1:T(2,128)(2,1)} %all-to-all-done.1) | data formatting | bytes 12582912 | tf_op jit(solution)/shard_map/all_to_all | solution.py:303
  250.9 1.0 fusion.76
  252.0 1.4 fusion.59
  255.3 4.7 fusion.73
  259.9 4.7 fusion.38
  264.7 2.3 collective-permute-start.1
  267.2 2.7 collective-permute-done.1
  270.2 1.2 divide_multiply_fusion
  271.5 1.1 slice.86
  275.5 1.4 select_subtract_fusion
  277.3 20.4 %while.18 = (s32[]{:T(128)}, f32[16,128,128]{1,2,0:T(8,128)S(1)}, f32[16,128,128]{2,1,0:T(8,128)S(1)}, s32[]{:T(128)}, s32[]{:T(128)}) while((s32[]{:T(128)}, f32[16,128,128]{1,2,0:T(8,128)S(1)}, f32[16,128,128]{2,1,0:T(8,128)S(1)}, s32[]{:T(128)}, s32[]{:T(128)}) %tuple.75), condition=%wide.region_12.13_spmd.clone.clone, body=%wide.region_11.12_spmd.clone.clone.sunk | while | flops 404111360 | bytes 8421493 | solution.py:112
  277.8 1.4 fusion.136
  279.2 1.2 fusion.137
  281.1 1.4 fusion.136
  282.5 1.2 fusion.137
  284.5 1.4 fusion.136
  285.9 1.2 fusion.137
  287.8 1.4 fusion.136
  289.2 1.2 fusion.137
  291.1 1.4 fusion.136
  292.5 1.2 fusion.137
  294.4 1.4 fusion.136
  295.8 1.2 fusion.137
  297.7 2.6 copy.98
  300.3 1.6 copy.99
  302.8 1.0 fusion.44
  303.9 1.0 fusion.65.state_ref
  304.9 1.1 convolution_subtract_fusion.1.map_ref
  306.2 1.3 convolution_multiply_fusion
  307.4 166.5 %shard_map.149 = f32[16,128,128]{2,1,0:T(8,128)S(1)} custom-call(f32[16,128,128]{2,1,0:T(8,128)S(1)} %convolution_subtract_fusion.1.map_ref, f32[16,128,128]{2,1,0:T(8,128)S(1)} %fusion.65.state_ref), custom_call_target="tpu_custom_call" | custom-call | tf_op jit(solution)/shard_map/pallas_call | solution.py:226
  474.6 1.0 fusion.54
  475.6 1.0 multiply_reduce_fusion
  476.9 1.0 copy.105
  (97 shorter events, 14.3 us)
Async XLA Ops:
  7.2 1.2 copy-start
  7.2 7.6 %copy-start.5 = (bf16[128,2048]{1,0:T(8,128)(2,1)S(1)}, bf16[128,2048]{1,0:T(8,128)(2,1)}, u32[]{:S(2)}) copy-start(bf16[128,2048]{1,0:T(8,128)(2,1)} %param.16) | copy-start | bytes 1572868
  7.2 7.6 %copy-start.13 = (f32[2048]{0:T(1024)S(1)}, f32[2048]{0:T(1024)}, u32[]{:S(2)}) copy-start(f32[2048]{0:T(1024)} %param.19) | copy-start | bytes 24580
  7.2 166.6 %all-gather.2.cloned.1.call-start = ((), (), s32[]{:S(2)}) async-start(), calls=%async_computation.2 | async-start | bytes 8912896 | tf_op jit(solution)/shard_map/all_gather | solution.py:272
  29.8 94.9 %copy-start.17 = (bf16[2,2048,512]{2,1,0:T(8,128)(2,1)S(1)}, bf16[2,2048,512]{2,1,0:T(8,128)(2,1)}, u32[]{:S(2)}) copy-start(bf16[2,2048,512]{2,1,0:T(8,128)(2,1)} %param.20) | copy-start | bytes 12582916
  122.1 2.6 copy-start.4
  159.4 15.1 %copy-start.12 = (f32[128,10]{0,1:T(8,128)S(1)}, f32[128,10]{0,1:T(8,128)}, u32[]{:S(2)}) copy-start(f32[128,10]{0,1:T(8,128)} %param.18) | copy-start | bytes 15364
  159.4 15.2 %copy-start.18 = (f32[16]{0:T(128)S(1)}, f32[16]{0:T(128)}, u32[]{:S(2)}) copy-start(f32[16]{0:T(128)} %param.27) | copy-start | bytes 196
  159.4 16.6 %copy-start.10 = (bf16[4,4096]{1,0:T(4,128)(2,1)S(1)}, bf16[4,4096]{1,0:T(4,128)(2,1)}, u32[]{:S(2)}) copy-start(bf16[4,4096]{1,0:T(4,128)(2,1)} %param.26) | copy-start | bytes 98308
  159.4 85.8 %all-to-all-start.1 = ((bf16[2,768,2048]{2,0,1:T(2,128)(2,1)}), bf16[2,768,2048]{2,0,1:T(2,128)(2,1)}, u32[]{:S(2)}, u32[]{:S(2)}) async-start(bf16[2,768,2048]{2,0,1:T(2,128)(2,1)} %copy.93), calls=%async_computation.1 | async-start | bytes 12582912 | tf_op jit(solution)/shard_map/all_to_all | solution.py:303
  173.9 86.1 %collective-permute-start = (bf16[1024,4096]{1,0:T(8,128)(2,1)}, bf16[1024,4096]{1,0:T(8,128)(2,1)}, u32[]{:S(2)}, u32[]{:S(2)}) collective-permute-start(bf16[1024,4096]{1,0:T(8,128)(2,1)} %all-gather.2.cloned.1.call-done), channel_id=1, source_target_pairs={{0,16},{16,0},{32,48},{48,32},{64,80},{80,64},{96,112},{112,96},{1... | collective-permute-start | bytes 25165832 | tf_op jit(solution)/shard_map/ppermute | solution.py:273
  251.9 2.2 copy-start.14
  251.9 2.4 copy-start.11
  251.9 2.7 copy-start.15
  253.3 0.8 copy-start.9
  264.7 5.3 %collective-permute-start.1 = (bf16[3,4096]{1,0:T(4,128)(2,1)S(1)}, bf16[3,4096]{1,0:T(4,128)(2,1)S(1)}, u32[]{:S(2)}, u32[]{:S(2)}) collective-permute-start(bf16[3,4096]{1,0:T(4,128)(2,1)S(1)} %slice.75), channel_id=1, source_target_pairs={{0,1},{1,2},{2,3},{3,4},{4,5},{5,6},{6,7},{7,8},{8,9},{9,10},{10,1... | collective-permute-start | bytes 73736 | tf_op jit(solution)/shard_map/ppermute | solution.py:13
  274.7 0.8 copy-start.6
  274.8 2.1 copy-start.2
  297.7 4.5 copy-start.7
  303.9 2.2 copy-start.8
  304.9 1.3 copy-start.3
  474.6 2.1 copy-start.16
  474.6 3.3 copy-start.1
Sparse Core Ops, SparseCore 0:
  10.7 135.3 all-gather.1
